TPU v7x, 32 devices: a whole 2x2x4 slice. The times are simulated.
32 devices in a mesh: dp: 4 (over z), table: 8 (over y, x, core).
Axes of the slice: x: 2, y: 2, z: 4, core: 2. Of those that a mesh axis runs over, the one named last changes fastest.
Arguments:
- item_emb: bfloat16 [16384, 512], P(('dp', 'table')), may hold values from -6 to 6
- cotangent: bfloat16 [16384, 512], P(('dp', 'table')), may hold values from -6 to 6
- in_proj: bfloat16 [512, 2048], replicated, may hold values from -0.25 to 0.25
- out_proj: bfloat16 [512, 512], replicated, may hold values from -0.25 to 0.25
- history_lengths: int32 [32, 8], P(('dp', 'table')), may hold values from 1 to 256, 512 in all within a row
- item_ids: int32 [16384], P(('dp', 'table')), may hold values from 0 to 32767, as said below
Outputs:
- emb_grad: float32 [32768, 512], P(('dp', 'table'))
- in_grad: float32 [512, 2048], replicated
- out_grad: float32 [512, 512], replicated
Inputs may be any that keep to these rules, and one draw needn't show every extreme that they name: `item_ids`: among the 512 items of one device, at most 32 have ids of one device's rows (ids r with the same r // 1024), and these name at most 16 distinct ids; in every draw some device's rows get exactly 32 items with 16 distinct ids from every device. `history_lengths`: each row sums to 512.
All inputs are finite; a program needn't handle non-finite values.
Results may differ from a plain program's by a relative error of at most 0.0075.
Values sent between devices are 32-bit elements; how exact they have to be, the bound alone decides.
No kernel may reach another device: no remote copies, remote signals or barrier semaphores. Data moves between devices by JAX's collectives and lax.ppermute only.
A program may use at most 64 MiB of HBM per device.

v0:
```python
import math

import jax
import jax.numpy as jnp
from jax import lax
from jax.sharding import PartitionSpec as P

H = 4
OWN_ROWS = 1024
BLOCK = 512
LEN = 256


norm_eps = 1e-05


def silu_grad(pre_value):
    sigmoid_z = jax.nn.sigmoid(pre_value)
    return sigmoid_z * (1.0 + pre_value * (1.0 - sigmoid_z))


def block_grads(hidden, pre_act, cot_rows, lengths, out_proj):
    block_rows = hidden.shape[0]
    model_width = cot_rows.shape[1]
    head_size = model_width // H
    gating = hidden[:, :model_width].astype(jnp.float32)
    value_vecs = hidden[:, model_width : 2 * model_width].reshape(block_rows, H, head_size)
    query_vecs = hidden[:, 2 * model_width : 3 * model_width].reshape(block_rows, H, head_size)
    key_vecs = hidden[:, 3 * model_width :].reshape(block_rows, H, head_size)
    positions = jnp.arange(block_rows, dtype=jnp.int32)
    seq_ends = jnp.cumsum(lengths)
    segment = jnp.sum((positions[:, None] >= seq_ends[None, :]).astype(jnp.int32), axis=1)
    causal_mask = (
        (segment[:, None] == segment[None, :]) & (positions[None, :] <= positions[:, None])
    ).astype(jnp.float32) * (1.0 / LEN)
    score_scale = 1.0 / math.sqrt(head_size)
    scores = (
        jnp.einsum("ihd,jhd->hij", query_vecs, key_vecs, preferred_element_type=jnp.float32)
        * score_scale
    )
    weights = (jax.nn.silu(scores) * causal_mask).astype(jnp.bfloat16)
    attended = jnp.einsum(
        "hij,jhd->ihd", weights, value_vecs, preferred_element_type=jnp.float32
    ).reshape(block_rows, model_width)
    row_mean = jnp.mean(attended, axis=1, keepdims=True)
    centered = attended - row_mean
    inv_std = lax.rsqrt(jnp.mean(centered * centered, axis=1, keepdims=True) + norm_eps)
    normed = centered * inv_std
    gated_out = (normed * gating).astype(jnp.bfloat16)
    grad_out = lax.dot_general(
        cot_rows, out_proj, (((1,), (1,)), ((), ())), preferred_element_type=jnp.float32
    )
    grad_gate = grad_out * normed
    grad_norm = grad_out * gating
    grad_att = inv_std * (
        grad_norm
        - jnp.mean(grad_norm, axis=1, keepdims=True)
        - normed * jnp.mean(grad_norm * normed, axis=1, keepdims=True)
    )
    grad_att = grad_att.astype(jnp.bfloat16).reshape(block_rows, H, head_size)
    grad_weights = jnp.einsum(
        "ihd,jhd->hij", grad_att, value_vecs, preferred_element_type=jnp.float32
    )
    grad_value = jnp.einsum("hij,ihd->jhd", weights, grad_att, preferred_element_type=jnp.float32)
    grad_scores = (grad_weights * causal_mask * silu_grad(scores)).astype(jnp.bfloat16)
    grad_query = (
        jnp.einsum("hij,jhd->ihd", grad_scores, key_vecs, preferred_element_type=jnp.float32)
        * score_scale
    )
    grad_key = (
        jnp.einsum("hij,ihd->jhd", grad_scores, query_vecs, preferred_element_type=jnp.float32)
        * score_scale
    )
    grad_hidden = jnp.concatenate(
        [
            grad_gate,
            grad_value.reshape(block_rows, model_width),
            grad_query.reshape(block_rows, model_width),
            grad_key.reshape(block_rows, model_width),
        ],
        axis=1,
    )
    grad_pre = (grad_hidden * silu_grad(pre_act)).astype(jnp.bfloat16)
    return (gated_out, grad_pre)


def place_rows(row_values, owner_of, local_row, owners, capacity):
    model_width = row_values.shape[1]
    onehot = (owner_of[:, None] == jnp.arange(owners, dtype=jnp.int32)[None, :]).astype(jnp.int32)
    before = jnp.cumsum(onehot, axis=0) - onehot
    slot_rank = jnp.sum(before * onehot, axis=1)
    slot_index = jnp.where(owner_of < owners, owner_of * capacity + slot_rank, owners * capacity)
    slot_rows = (
        jnp.zeros((owners * capacity, model_width), jnp.float32)
        .at[slot_index]
        .set(row_values, mode="drop")
    )
    slot_ids = (
        jnp.full((owners * capacity,), OWN_ROWS, jnp.int32)
        .at[slot_index]
        .set(local_row, mode="drop")
    )
    return (slot_rows.reshape(owners, capacity, model_width), slot_ids.reshape(owners, capacity))


def per_device(item_emb, cotangent, in_proj, out_proj, history_lengths, item_ids):
    rows_here = item_emb.shape[0]
    model_width = item_emb.shape[1]
    block_count = rows_here // BLOCK
    dp_count = lax.axis_size("dp")
    table_count = lax.axis_size("table")
    owners = dp_count * table_count
    capacity = 2 * rows_here // owners
    pre_act = jnp.dot(item_emb, in_proj, preferred_element_type=jnp.float32)
    hidden = jax.nn.silu(pre_act).astype(jnp.bfloat16)

    def one_block(pieces):
        return block_grads(pieces[0], pieces[1], pieces[2], pieces[3], out_proj)

    gated_out, grad_pre = lax.map(
        one_block,
        (
            hidden.reshape(block_count, BLOCK, 4 * model_width),
            pre_act.reshape(block_count, BLOCK, 4 * model_width),
            cotangent.reshape(block_count, BLOCK, model_width),
            history_lengths,
        ),
    )
    gated_out = gated_out.reshape(rows_here, model_width)
    grad_pre = grad_pre.reshape(rows_here, 4 * model_width)
    out_local = lax.dot_general(
        gated_out, cotangent, (((0,), (0,)), ((), ())), preferred_element_type=jnp.float32
    )
    in_local = lax.dot_general(
        item_emb, grad_pre, (((0,), (0,)), ((), ())), preferred_element_type=jnp.float32
    )
    in_total, out_total = lax.psum((in_local, out_local), ("dp", "table"))
    item_grad = lax.dot_general(
        grad_pre, in_proj, (((1,), (1,)), ((), ())), preferred_element_type=jnp.float32
    ) + cotangent.astype(jnp.float32)
    send_rows, send_ids = place_rows(
        item_grad, item_ids // OWN_ROWS, item_ids % OWN_ROWS, owners, capacity
    )
    arrived_rows, arrived_ids = (
        lax.all_to_all(send_rows, ("dp", "table"), split_axis=0, concat_axis=0, tiled=True),
        lax.all_to_all(send_ids, ("dp", "table"), split_axis=0, concat_axis=0, tiled=True),
    )
    emb_grad = (
        jnp.zeros((OWN_ROWS, model_width), jnp.float32)
        .at[arrived_ids.reshape(-1)]
        .add(arrived_rows.reshape(-1, model_width), mode="drop")
    )
    grad_scale = 1.0 / math.sqrt(rows_here * owners)
    return (emb_grad, in_total * grad_scale, out_total * grad_scale)


def solution(mesh):
    placed = (
        P(("dp", "table"), None),
        P(("dp", "table"), None),
        P(),
        P(),
        P(("dp", "table"), None),
        P(("dp", "table")),
    )
    return jax.shard_map(
        per_device,
        mesh=mesh,
        in_specs=placed,
        out_specs=(P(("dp", "table"), None), P(), P()),
        check_vma=False,
    )
```

profile of v0, /device:TPU:0, one launch (start us, length us, event | category | flops | bytes accessed | tf_op | source)
XLA Modules:
  0.0 264.7 jit_solution(13353558803683191540)
XLA Ops:
  7.2 0.0 copy-start
  7.2 0.8 add_select_fusion
  8.0 1.2 reduce-window.18
  9.2 0.2 slice_reduce_fusion
  9.5 0.1 fusion.15
  9.6 2.4 scatter_custom_fusion
  12.0 0.7 all_to_all.9
  12.7 7.3 %all-to-all-start = ((s32[32,1,32]{2,1,0:T(1,128)}), s32[32,1,32]{2,1,0:T(1,128)S(1)}, u32[]{:S(2)}, u32[]{:S(2)}) async-start(s32[32,1,32]{2,1,0:T(1,128)} %all_to_all.9), calls=%async_computation | async-start | bytes 32768 | tf_op jit(solution)/shard_map/all_to_all | solution.py:146
  20.0 0.0 copy-done
  20.0 0.0 copy-start.13
  20.0 4.9 %multiply_convert_fusion.2 = (bf16[512,2048]{0,1:T(8,128)(2,1)S(1)}, f32[512,2048]{0,1:T(8,128)}) fusion(bf16[512,512]{1,0:T(8,128)(2,1)} %param.6, bf16[512,2048]{1,0:T(8,128)(2,1)S(1)} %copy-done), kind=kOutput, calls=%fused_computation.8 | convolution fusion | flops 1078984704 | bytes 8912896 | tf_op jit(solution)/shard_map/dot_general | solution.py:114
  24.9 1.3 copy-done.3
  26.3 0.9 fusion.20
  27.2 0.0 copy-start.6
  27.2 0.0 copy-start.8
  27.2 0.0 copy-done.13
  27.2 0.2 reduce-window.20
  27.3 0.1 convert_reduce_fusion
  27.4 0.2 fusion.10
  27.6 0.3 copy-done.6
  27.9 1.6 multiply_convert_fusion.1
  29.5 0.0 copy-done.8
  29.5 0.0 copy-start.4
  29.6 0.0 copy-start.5
  29.6 0.0 copy-start.12
  29.6 0.0 copy-done.10
  29.6 0.8 fusion.21
  30.4 0.2 fusion.4
  30.6 0.5 copy-done.4
  31.1 0.1 copy-done.5
  31.2 0.2 copy-done.12
  31.4 0.6 fusion.12
  32.0 0.3 multiply_convert_fusion.3
  32.4 0.4 fusion.22
  32.8 0.0 copy-start.9
  32.8 0.0 copy-start.7
  32.8 1.9 multiply_convert_fusion
  34.7 0.0 copy-done.9
  34.7 0.0 copy-start.2
  34.7 0.8 convolution_multiply_fusion.1
  35.5 0.0 copy-done.7
  35.6 0.4 convolution_multiply_fusion
  36.0 0.9 copy-done.2
  36.9 1.5 fusion
  38.4 0.0 copy-start.1
  38.5 1.3 copy-done.1
  39.8 2.3 convolution_add_fusion
  42.1 4.5 %scatter_custom_fusion.1 = f32[1024,512]{1,0:T(8,128)} fusion(s32[512]{0:T(512)S(1)} %compare_select_fusion.1, f32[512,512]{1,0:T(8,128)} %convolution_add_fusion, f32[]{:T(128)} %constant.80.clone.1), kind=kCustom, calls=%fused_computation.28 | custom fusion | bytes 2097664 | tf_op jit(solution)/shard_map/scatter | solution.py:96
  46.6 0.0 all-to-all-done
  46.6 6.0 %all-to-all-start.1 = ((f32[32,32,512]{2,1,0:T(8,128)}), f32[32,32,512]{2,1,0:T(8,128)}, u32[]{:S(2)}, u32[]{:S(2)}) async-start(f32[32,32,512]{2,1,0:T(8,128)} %bitcast.81), calls=%async_computation.1 | async-start | bytes 4194304 | tf_op jit(solution)/shard_map/all_to_all | solution.py:145
  52.5 0.0 all-reduce.3.cloned.1.call-start
  52.6 1.4 fusion.23
  54.0 4.9 %convolution_bitcast_fusion = f32[512,2048]{0,1:T(8,128)} fusion(bf16[512,2048]{0,1:T(8,128)(2,1)} %copy-done.1, bf16[512,512]{1,0:T(8,128)(2,1)} %param.6), kind=kOutput, calls=%fused_computation.10 | convolution fusion | flops 1073741824 | bytes 6815744 | tf_op jit(solution)/shard_map/dot_general | solution.py:134
  58.9 0.0 all-reduce.3.cloned.1.call-update
  59.0 0.5 broadcast.203
  59.5 0.7 reduce.8
  60.1 0.1 reshape.200
  60.2 177.8 %all-reduce.3.cloned.1.call-done = (f32[512,2048]{0,1:T(8,128)}, f32[512,512]{1,0:T(8,128)}) async-done(((f32[512,2048]{0,1:T(8,128)}, f32[512,512]{1,0:T(8,128)}), (f32[512,2048]{0,1:T(8,128)}, f32[512,512]{1,0:T(8,128)})) %all-reduce.3.cloned.1.call-update) | async-done | bytes 5242896 | tf_op jit(solution)/shard_map/psum | solution.py:137
  238.1 4.7 %broadcast_multiply_fusion = f32[512,2048]{0,1:T(8,128)} fusion(f32[512,2048]{0,1:T(8,128)} %get-tuple-element.38), kind=kLoop, calls=%fused_computation.11 | loop fusion | flops 1048576 | bytes 8388608 | tf_op jit(solution)/shard_map/mul | solution.py:154
  242.7 5.4 %copy.34 = f32[512,2048]{1,0:T(8,128)} copy(f32[512,2048]{0,1:T(8,128)} %broadcast_multiply_fusion) | data formatting | bytes 8388608
  248.2 0.0 copy-done.11
  248.2 1.1 broadcast_multiply_fusion.1
  249.2 0.0 all-to-all-done.1
  249.2 8.7 %scatter_custom_fusion.2 = f32[1024,512]{1,0:T(8,128)} fusion(s32[1024]{0:T(1024)S(1)} %bitcast.94, f32[1024,512]{1,0:T(8,128)} %bitcast.18, f32[]{:T(128)} %constant.80.clone.1), kind=kCustom, calls=%fused_computation.26 | custom fusion | flops 524288 | bytes 2097664 | tf_op jit(solution)/shard_map/scatter-add | solution.py:151
  (11 shorter events, 0.1 us)
Async XLA Ops:
  7.2 12.9 %copy-start = (bf16[512,2048]{1,0:T(8,128)(2,1)S(1)}, bf16[512,2048]{1,0:T(8,128)(2,1)}, u32[]{:S(2)}) copy-start(bf16[512,2048]{1,0:T(8,128)(2,1)} %param.8) | copy-start | bytes 6291460
  12.7 33.8 %all-to-all-start = ((s32[32,1,32]{2,1,0:T(1,128)}), s32[32,1,32]{2,1,0:T(1,128)S(1)}, u32[]{:S(2)}, u32[]{:S(2)}) async-start(s32[32,1,32]{2,1,0:T(1,128)} %all_to_all.9), calls=%async_computation | async-start | bytes 32768 | tf_op jit(solution)/shard_map/all_to_all | solution.py:146
  20.0 7.1 %copy-start.13 = (s32[1,8]{1,0:T(1,128)S(1)}, s32[1,8]{1,0:T(1,128)}, u32[]{:S(2)}) copy-start(s32[1,8]{1,0:T(1,128)} %param.10) | copy-start | bytes 100
  24.9 1.3 copy-start.3
  27.2 0.8 copy-start.6
  27.2 2.4 copy-start.8
  27.9 1.6 copy-start.10
  29.5 1.6 copy-start.4
  29.6 1.7 copy-start.5
  29.6 1.8 copy-start.12
  32.8 1.9 copy-start.9
  32.8 2.7 %copy-start.7 = (bf16[512,512]{0,1:T(8,128)(2,1)S(1)}, bf16[512,512]{0,1:T(8,128)(2,1)}, u32[]{:S(2)}) copy-start(bf16[512,512]{0,1:T(8,128)(2,1)} %copy-done.6) | copy-start | bytes 1572868
  34.7 2.2 copy-start.2
  38.4 1.4 copy-start.1
  46.6 202.7 %all-to-all-start.1 = ((f32[32,32,512]{2,1,0:T(8,128)}), f32[32,32,512]{2,1,0:T(8,128)}, u32[]{:S(2)}, u32[]{:S(2)}) async-start(f32[32,32,512]{2,1,0:T(8,128)} %bitcast.81), calls=%async_computation.1 | async-start | bytes 4194304 | tf_op jit(solution)/shard_map/all_to_all | solution.py:145
  52.5 185.5 %all-reduce.3.cloned.1.call-start = ((), (), s32[]{:S(2)}) async-start(), calls=%async_computation.2 | async-start | bytes 10485760 | tf_op jit(solution)/shard_map/psum | solution.py:137
  242.7 5.4 %copy-start.11 = (f32[512,512]{1,0:T(8,128)S(1)}, f32[512,512]{1,0:T(8,128)}, u32[]{:S(2)}) copy-start(f32[512,512]{1,0:T(8,128)} %get-tuple-element.39) | copy-start | bytes 3145732
Sparse Core Ops, SparseCore 0:
  59.5 178.5 all-reduce.2
where the time goes:
time: 265 us
  waiting for transfers between devices  178 us (67%)
  matrix products  20.1 us (8%)
  other arithmetic  19.7 us (7%)
  local copies, waits for them, and re-layouts  19.5 us (7%)
  between operations  14.3 us (5%)
  starting transfers between devices  13.3 us (5%)
    psum x1, waiting for transfers between devices, per_device(): in_total, out_total = lax.psum((in_local, out_local), ('dp', 'table'))  178 us
    unnamed x29, local copies, waits for them, and re-layouts  10.1 us
    scatter-add x1, other arithmetic, per_device(): emb_grad = jnp.zeros((OWN_ROWS, model_width), jnp.float32).at[arrived_ids...  8.65 us
    all_to_all x1, starting transfers between devices, per_device(): lax.all_to_all(send_ids, ('dp', 'table'), split_axis=0, concat_axis=0, ti...  7.3 us
    all_to_all x1, starting transfers between devices, per_device(): lax.all_to_all(send_rows, ('dp', 'table'), split_axis=0, concat_axis=0, t...  5.96 us
    mul x2, other arithmetic, per_device(): return (emb_grad, in_total * grad_scale, out_total * grad_scale)  5.72 us
  transfers between devices with their start and end apart: 3, of which 1 were waited for; matrix products, arithmetic and copies ran while one was open for 15% of the time, Pallas kernels for 0%

commit v1 on v0

v1 whole, which is shorter than its diff:
```python
import functools
import math

import jax
import jax.numpy as jnp
from jax import lax
from jax.experimental import pallas as pl
from jax.experimental.pallas import tpu as pltpu
from jax.sharding import PartitionSpec as P

H = 4
OWN_ROWS = 1024
BLOCK = 512
LEN = 256
TILE = 256

norm_eps = 1e-05
VMEM = pltpu.MemorySpace.VMEM
SMEM = pltpu.MemorySpace.SMEM


def dot_nn(a, b):
    return lax.dot_general(a, b, (((1,), (0,)), ((), ())), preferred_element_type=jnp.float32)


def dot_nt(a, b):
    return lax.dot_general(a, b, (((1,), (1,)), ((), ())), preferred_element_type=jnp.float32)


def dot_tn(a, b):
    return lax.dot_general(a, b, (((0,), (0,)), ((), ())), preferred_element_type=jnp.float32)


def sigmoid(z):
    return 0.5 * jnp.tanh(0.5 * z) + 0.5


def block_kernel(lengths, emb, cot, in_proj, out_proj, gated_out, grad_pre, hid, dpre, mask, wts, dsc, att):
    rows, width = emb.shape
    head = width // H
    scale = 1.0 / math.sqrt(head)
    along_lane = lax.broadcasted_iota(jnp.int32, (1, rows), 1)
    along_row = lax.broadcasted_iota(jnp.int32, (rows, 1), 0)
    end = jnp.int32(0)
    seg_lane, seg_row = jnp.zeros_like(along_lane), jnp.zeros_like(along_row)
    for s in range(lengths.shape[1]):
        end = end + lengths[0, s]
        seg_lane = seg_lane + (along_lane >= end).astype(jnp.int32)
        seg_row = seg_row + (along_row >= end).astype(jnp.int32)
    for i in range(rows // TILE):
        r, n = pl.ds(i * TILE, TILE), (i + 1) * TILE
        own = seg_row[i * TILE : n] == seg_lane[:, :n]
        past = along_lane[:, :n] <= along_row[i * TILE : n]
        mask[r, :n] = jnp.where(own & past, 1.0 / LEN, 0.0)
    for c in range(4):
        cols = pl.ds(c * width, width)
        z = dot_nn(emb[...], in_proj[:, cols])
        sig = sigmoid(z)
        act = z * sig
        hid[:, cols] = act.astype(jnp.bfloat16)
        dpre[:, cols] = sig + act * (1.0 - sig)
    for h in range(H):
        v, q, k = (pl.ds((c * H + h) * head, head) for c in (1, 2, 3))
        for i in range(rows // TILE):
            r, n = pl.ds(i * TILE, TILE), (i + 1) * TILE
            m = mask[r, :n]
            s = dot_nt(hid[r, q], hid[:n, k]) * scale
            sig = sigmoid(s)
            act = s * sig
            w = (act * m).astype(jnp.bfloat16)
            wts[h, r, :n] = w
            dsc[h, r, :n] = (sig + act * (1.0 - sig)) * m
            att[r, pl.ds(h * head, head)] = dot_nn(w, hid[:n, v])
    grad_att = []
    for i in range(rows // TILE):
        r = pl.ds(i * TILE, TILE)
        a = att[r, :]
        centered = a - jnp.mean(a, axis=1, keepdims=True)
        inv_std = lax.rsqrt(jnp.mean(centered * centered, axis=1, keepdims=True) + norm_eps)
        normed = centered * inv_std
        gating = hid[r, :width].astype(jnp.float32)
        gated_out[r, :] = (normed * gating).astype(jnp.bfloat16)
        grad_out = dot_nt(cot[r, :], out_proj[...])
        grad_pre[r, :width] = (grad_out * normed * dpre[r, :width]).astype(jnp.bfloat16)
        grad_norm = grad_out * gating
        g = inv_std * (
            grad_norm
            - jnp.mean(grad_norm, axis=1, keepdims=True)
            - normed * jnp.mean(grad_norm * normed, axis=1, keepdims=True)
        )
        grad_att.append(g.astype(jnp.bfloat16))
    for h in range(H):
        v, q, k = (pl.ds((c * H + h) * head, head) for c in (1, 2, 3))
        grad_v, grad_k = [None] * (rows // TILE), [None] * (rows // TILE)
        for i in range(rows // TILE):
            r, n = pl.ds(i * TILE, TILE), (i + 1) * TILE
            g = grad_att[i][:, h * head : (h + 1) * head]
            gs = (dot_nt(g, hid[:n, v]) * dsc[h, r, :n]).astype(jnp.bfloat16)
            gq = dot_nn(gs, hid[:n, k]) * scale
            grad_pre[r, q] = (gq * dpre[r, q]).astype(jnp.bfloat16)
            for j in range(i + 1):
                cut = slice(j * TILE, (j + 1) * TILE)
                gv = dot_tn(wts[h, r, cut], g)
                gk = dot_tn(gs[:, cut], hid[r, q])
                grad_v[j] = gv if grad_v[j] is None else grad_v[j] + gv
                grad_k[j] = gk if grad_k[j] is None else grad_k[j] + gk
        for j in range(rows // TILE):
            r = pl.ds(j * TILE, TILE)
            grad_pre[r, v] = (grad_v[j] * dpre[r, v]).astype(jnp.bfloat16)
            grad_pre[r, k] = (grad_k[j] * scale * dpre[r, k]).astype(jnp.bfloat16)


def block_call(lengths, emb, cot, in_proj, out_proj):
    rows, width = emb.shape
    vmem = pl.BlockSpec(memory_space=VMEM)
    return pl.pallas_call(
        block_kernel,
        name="block",
        out_shape=(
            jax.ShapeDtypeStruct((rows, width), jnp.bfloat16),
            jax.ShapeDtypeStruct((rows, 4 * width), jnp.bfloat16),
        ),
        in_specs=[pl.BlockSpec(memory_space=SMEM)] + [vmem] * 4,
        out_specs=(vmem, vmem),
        scratch_shapes=[
            pltpu.VMEM((rows, 4 * width), jnp.bfloat16),
            pltpu.VMEM((rows, 4 * width), jnp.float32),
            pltpu.VMEM((rows, rows), jnp.float32),
            pltpu.VMEM((H, rows, rows), jnp.bfloat16),
            pltpu.VMEM((H, rows, rows), jnp.float32),
            pltpu.VMEM((rows, width), jnp.float32),
        ],
        compiler_params=pltpu.CompilerParams(vmem_limit_bytes=40 << 20),
    )(lengths, emb, cot, in_proj, out_proj)


def weight_kernel(chunk, place, emb, cot, gated_out, grad_pre, a_keep, b_keep, a_send, b_send, rel_a, rel_b, rel_g):
    width = emb.shape[1]
    half, rest = a_keep.shape
    emb_t, gated_t = emb[...].T, gated_out[...].T
    count = width // chunk
    for c in range(count):
        src = slice(c * chunk, (c + 1) * chunk)
        to_a = pl.ds(pl.multiple_of((c ^ place[0]) * chunk, chunk), chunk)
        to_b = pl.ds(pl.multiple_of((c ^ place[1]) * chunk, chunk), chunk)
        rel_a[to_a, :] = emb_t[src]
        rel_b[to_b, :] = emb_t[src]
        rel_g[to_b, :] = gated_t[src]
    in_b = 4 * width - rest
    for out_a, out_b, r in ((a_send, b_send, pl.ds(half, half)), (a_keep, b_keep, pl.ds(0, half))):
        out_a[...] = dot_nn(rel_a[r, :], grad_pre[:, :rest])
        out_b[:, :in_b] = dot_nn(rel_b[r, :], grad_pre[:, rest:])
        out_b[:, in_b:] = dot_nn(rel_g[r, :], cot[...])


def weight_call(chunk, place, emb, cot, gated_out, grad_pre):
    width = emb.shape[1]
    vmem = pl.BlockSpec(memory_space=VMEM)
    part = jax.ShapeDtypeStruct((width // 2, 5 * width // 2), jnp.float32)
    return pl.pallas_call(
        functools.partial(weight_kernel, chunk),
        name="weights",
        out_shape=(part,) * 4,
        in_specs=[pl.BlockSpec(memory_space=SMEM)] + [vmem] * 4,
        out_specs=(vmem,) * 4,
        scratch_shapes=[pltpu.VMEM((width, width), jnp.bfloat16)] * 3,
        compiler_params=pltpu.CompilerParams(vmem_limit_bytes=40 << 20),
    )(place, emb, cot, gated_out, grad_pre)


def split_bf16(x):
    high = x.astype(jnp.bfloat16)
    return high, (x - high.astype(jnp.float32)).astype(jnp.bfloat16)


def item_kernel(owners, slots, ids, cot, grad_pre, in_proj, sent):
    rows, width = cot.shape
    item_grad = dot_nt(grad_pre[...], in_proj[...]) + cot[...].astype(jnp.float32)
    high, low = split_bf16(item_grad)
    id_lane = ids[...]
    sub = lax.broadcasted_iota(jnp.int32, (rows, rows), 0)
    lane = lax.broadcasted_iota(jnp.int32, (rows, rows), 1)
    id_row = jnp.sum(jnp.where(sub == lane, id_lane, 0), axis=1, keepdims=True)
    repeat = jnp.max(jnp.where((id_row == id_lane) & (lane < sub), 1, 0), axis=1, keepdims=True)
    key = jnp.where(repeat == 0, id_row, jnp.int32(2**30))
    owner = id_lane // OWN_ROWS
    below = (key >= owner * OWN_ROWS) & (key < id_lane)
    rank = jnp.sum(jnp.where(below, 1, 0), axis=0, keepdims=True)
    slot = owner * slots + rank
    total = owners * slots
    pick = lax.broadcasted_iota(jnp.int32, (total, rows), 0) == slot
    onehot = jnp.where(pick, 1.0, 0.0).astype(jnp.bfloat16)
    summed = dot_nn(onehot, high) + dot_nn(onehot, low)
    for c in range(width // 128):
        sent[:, c * slots : (c + 1) * slots, :] = summed[:, c * 128 : (c + 1) * 128].reshape(owners, slots, 128)
    number = jnp.max(jnp.where(pick, id_lane - owner * OWN_ROWS, -1), axis=1, keepdims=True)
    number = jnp.broadcast_to(number.astype(jnp.float32), (total, 128)).reshape(owners, slots, 128)
    groups = slots // 8
    at = lax.broadcasted_iota(jnp.int32, (owners, 8, 128), 2) // (128 // groups)
    tail = number[:, :8]
    for g in range(1, groups):
        tail = jnp.where(at == g, number[:, g * 8 : (g + 1) * 8], tail)
    sent[:, (width // 128) * slots :, :] = tail


def item_call(owners, slots, ids, cot, grad_pre, in_proj):
    width = cot.shape[1]
    vmem = pl.BlockSpec(memory_space=VMEM)
    return pl.pallas_call(
        functools.partial(item_kernel, owners, slots),
        name="items",
        out_shape=jax.ShapeDtypeStruct((owners, (width // 128) * slots + 8, 128), jnp.float32),
        in_specs=[vmem] * 4,
        out_specs=vmem,
        compiler_params=pltpu.CompilerParams(vmem_limit_bytes=40 << 20),
    )(ids, cot, grad_pre, in_proj)


def table_kernel(owners, slots, got, emb_grad):
    width = emb_grad.shape[1]
    groups = slots // 8
    tail = got[:, (width // 128) * slots :, :]
    number = [tail[:, :, g * (128 // groups) : g * (128 // groups) + 1] for g in range(groups)]
    number = jnp.concatenate(number, axis=1).reshape(owners * slots, 1).astype(jnp.int32)
    pick = number == lax.broadcasted_iota(jnp.int32, (owners * slots, OWN_ROWS), 1)
    onehot = jnp.where(pick, 1.0, 0.0).astype(jnp.bfloat16).T
    for c in range(0, width // 128, 2):
        rows = [got[:, d * slots : (d + 1) * slots, :].reshape(owners * slots, 128) for d in (c, c + 1)]
        high, low = split_bf16(jnp.concatenate(rows, axis=1))
        emb_grad[:, c * 128 : (c + 2) * 128] = dot_nn(onehot, high) + dot_nn(onehot, low)


def table_call(owners, slots, got, width):
    vmem = pl.BlockSpec(memory_space=VMEM)
    return pl.pallas_call(
        functools.partial(table_kernel, owners, slots),
        name="table",
        out_shape=jax.ShapeDtypeStruct((OWN_ROWS, width), jnp.float32),
        in_specs=[vmem],
        out_specs=vmem,
        compiler_params=pltpu.CompilerParams(vmem_limit_bytes=40 << 20),
    )(got)


def place_kernel(count, chunk, place, *refs):
    pieces, (in_grad, out_grad), sems = refs[:-3], refs[-3:-1], refs[-1]
    width = in_grad.shape[0]
    rest = pieces[0].shape[1]
    in_b = 4 * width - rest
    copies = []
    for side in range(2):
        position = 0
        for piece in pieces[side * len(pieces) // 2 : (side + 1) * len(pieces) // 2]:
            for c in range(piece.shape[0] // chunk):
                row = pl.ds(pl.multiple_of((position ^ place[side]) * chunk, chunk), chunk)
                src = piece.at[pl.ds(c * chunk, chunk)]
                if side == 0:
                    copies.append((src, in_grad.at[row, pl.ds(0, rest)]))
                else:
                    copies.append((src.at[:, pl.ds(0, in_b)], in_grad.at[row, pl.ds(rest, in_b)]))
                    copies.append((src.at[:, pl.ds(in_b, width)], out_grad.at[row, :]))
                position += 1
    copies = [pltpu.make_async_copy(s, d, sems.at[i]) for i, (s, d) in enumerate(copies)]
    for c in copies:
        c.start()
    for c in copies:
        c.wait()


def place_call(chunk, place, pieces, width):
    count = width // chunk
    return pl.pallas_call(
        functools.partial(place_kernel, count, chunk),
        name="place",
        out_shape=(
            jax.ShapeDtypeStruct((width, 4 * width), jnp.float32),
            jax.ShapeDtypeStruct((width, width), jnp.float32),
        ),
        in_specs=[pl.BlockSpec(memory_space=SMEM)] + [pl.BlockSpec(memory_space=VMEM)] * len(pieces),
        out_specs=(pl.BlockSpec(memory_space=pl.ANY),) * 2,
        scratch_shapes=[pltpu.SemaphoreType.DMA((3 * count,))],
        compiler_params=pltpu.CompilerParams(vmem_limit_bytes=40 << 20),
    )(place, *pieces)


def swap(x, axis, distance):
    size = lax.axis_size(axis)
    return lax.ppermute(x, axis, [(i, i ^ distance) for i in range(size)])


def orders(table_count):
    bits = [1 << b for b in range(table_count.bit_length() - 1)]
    first, rest = bits[:1], bits[1:]
    cut = len(rest) // 2
    return first + rest, first + rest[cut:] + rest[:cut]


def position(order, index):
    at = jnp.int32(0)
    for bit in order:
        at = 2 * at + (index // bit) % 2
    return at


def halve(x):
    n = x.shape[0] // 2
    return x[:n], x[n:]


def per_device(item_emb, cotangent, in_proj, out_proj, history_lengths, item_ids):
    rows_here, width = item_emb.shape
    dp_count = lax.axis_size("dp")
    table_count = lax.axis_size("table")
    owners = dp_count * table_count
    slots = max(8, rows_here // owners)
    order_a, order_b = orders(table_count)
    table_index, dp_index = lax.axis_index("table"), lax.axis_index("dp")
    place = jnp.stack([position(order_a, table_index), position(order_b, table_index)])
    chunk = width // table_count

    gated_out, grad_pre = block_call(history_lengths, item_emb, cotangent, in_proj, out_proj)
    a_keep, b_keep, a_send, b_send = weight_call(chunk, place, item_emb, cotangent, gated_out, grad_pre)
    sent = item_call(owners, slots, item_ids.reshape(1, rows_here), cotangent, grad_pre, in_proj)

    for step, (bit_a, bit_b) in enumerate(zip(order_a, order_b)):
        a_got, b_got = swap(a_send, "table", bit_a), swap(b_send, "table", bit_b)
        a_sum, b_sum = a_keep + a_got, b_keep + b_got
        if step + 1 < len(order_a):
            (a_keep, a_send), (b_keep, b_send) = halve(a_sum), halve(b_sum)
    got = lax.all_to_all(sent, ("dp", "table"), split_axis=0, concat_axis=0, tiled=True)

    cut = 2 * a_sum.shape[1] // dp_count
    pieces = [x[:, i * cut : (i + 1) * cut] for x in (a_sum, b_sum) for i in range(dp_count // 2)]
    pieces = jnp.stack(pieces)
    mine = lambda d: lax.dynamic_index_in_dim(pieces, dp_index ^ d, 0, keepdims=False)
    total = mine(0)
    for d in range(1, dp_count):
        total = total + swap(mine(d), "dp", d)
    total = total * (1.0 / math.sqrt(rows_here * owners))
    whole = [total] + [swap(total, "dp", d) for d in range(1, dp_count)]
    whole = jnp.stack(whole)
    whole = [lax.dynamic_index_in_dim(whole, dp_index ^ d, 0, keepdims=False) for d in range(dp_count)]
    a = [jnp.concatenate(whole[: dp_count // 2], axis=1)]
    b = [jnp.concatenate(whole[dp_count // 2 :], axis=1)]

    for bit_a, bit_b in zip(order_a[::-1], order_b[::-1]):
        join = lambda x: x[0] if len(x) == 1 else jnp.concatenate(x, axis=0)
        a, b = [join(a)], [join(b)]
        a.append(swap(a[0], "table", bit_a))
        b.append(swap(b[0], "table", bit_b))
    in_grad, out_grad = place_call(chunk, place, a + b, width)
    emb_grad = table_call(owners, slots, got, width)
    return (emb_grad, in_grad, out_grad)


def solution(mesh):
    placed = (
        P(("dp", "table"), None),
        P(("dp", "table"), None),
        P(),
        P(),
        P(("dp", "table"), None),
        P(("dp", "table")),
    )
    return jax.shard_map(
        per_device,
        mesh=mesh,
        in_specs=placed,
        out_specs=(P(("dp", "table"), None), P(), P()),
        check_vma=False,
    )
```

time: 265 us -> 143 us (0.54)
  waiting for transfers between devices: 178 us -> 75.1 us
  Pallas kernels: 0 us -> 20.5 us
  matrix products: 20.1 us -> 0 us
  starting transfers between devices: 13.3 us -> 28 us
  between operations: 14.3 us -> 0.91 us
  local copies, waits for them, and re-layouts: 19.5 us -> 8.4 us
  other arithmetic: 19.7 us -> 9.01 us
    psum x1 -> x0, waiting for transfers between devices: 178 us -> none  [per_device(): in_total, out_total = lax.psum((in_local, out_local), ('dp', 'table'))]
    ppermute x0 -> x18, waiting for transfers between devices: none -> 75.1 us  [swap(): return lax.ppermute(x, axis, [(i, i ^ distance) for i in range(size)])]
    ppermute x0 -> x18, starting transfers between devices: none -> 24.1 us  [swap(): return lax.ppermute(x, axis, [(i, i ^ distance) for i in range(size)])]
    pallas_call x0 -> x5, Pallas kernels: none -> 20.5 us  [the longest x1 6.61 us: block_call(): pl.pallas_call(block_kernel, name='block', out_shape=(jax.ShapeDtypeStruc...]
    dot_general x11 -> x0, matrix products: 20.1 us -> none  [the longest x1 4.94 us: per_device(): lax.dot_general(item_emb, grad_pre, (((0,), (0,)), ((), ())), preferred_e...]
    all_to_all x2 -> x1, starting transfers between devices: 13.3 us -> 3.91 us  [per_device(): lax.all_to_all(sent, ('dp', 'table'), split_axis=0, concat_axis=0, tiled=...]
    scatter-add x1 -> x0, other arithmetic: 8.65 us -> none  [per_device(): emb_grad = jnp.zeros((OWN_ROWS, model_width), jnp.float32).at[arrived_ids...]
    scatter x2 -> x0, local copies, waits for them, and re-layouts: 6.94 us -> none  [the longest x1 4.5 us: place_rows(): slot_rows = jnp.zeros((owners * capacity, model_width), jnp.float32).at[s...]
  transfers between devices with their start and end apart: 3 -> 19, of which waited for: 1 -> 12; matrix products, arithmetic and copies ran while one was open for 15% -> 6% of each run, Pallas kernels for 0% -> 5%
where the time goes in v1:
time: 143 us; the launch traced here: 142 us
  waiting for transfers between devices  75.1 us (53%)
  starting transfers between devices  28 us (20%)
  Pallas kernels  20.5 us (14%)
  other arithmetic  9.01 us (6%)
  local copies, waits for them, and re-layouts  8.4 us (6%)
    ppermute x18, waiting for transfers between devices, swap(): return lax.ppermute(x, axis, [(i, i ^ distance) for i in range(size)])  75.1 us
    ppermute x18, starting transfers between devices, swap(): return lax.ppermute(x, axis, [(i, i ^ distance) for i in range(size)])  24.1 us
    pallas_call x1, Pallas kernels, block_call(): pl.pallas_call(block_kernel, name='block', out_shape=(jax.ShapeDtypeStruc...  6.61 us
    unnamed x26, local copies, waits for them, and re-layouts  6.47 us
    pallas_call x1, Pallas kernels, place_call(): pl.pallas_call(functools.partial(place_kernel, count, chunk), name='place...  4.24 us
    concatenate x4, other arithmetic, per_device(): join = lambda x: x[0] if len(x) == 1 else jnp.concatenate(x, axis=0)  4.13 us
    pallas_call x1, Pallas kernels, table_call(): pl.pallas_call(functools.partial(table_kernel, owners, slots), name='tabl...  4.05 us
    all_to_all x1, starting transfers between devices, per_device(): lax.all_to_all(sent, ('dp', 'table'), split_axis=0, concat_axis=0, tiled=...  3.91 us
  transfers between devices with their start and end apart: 19, of which 12 were waited for; matrix products, arithmetic and copies ran while one was open for 6% of the time, Pallas kernels for 5%

profile of v1, /device:TPU:0, one launch (start us, length us, event | category | flops | bytes accessed | tf_op | source)
XLA Modules:
  0.0 142.0 jit_solution(10091062457701280046)
XLA Ops:
  0.7 0.1 pad_add_fusion.place
  0.8 1.6 %copy-done = bf16[512,2048]{1,0:T(8,128)(2,1)S(1)} copy-done((bf16[512,2048]{1,0:T(8,128)(2,1)S(1)}, bf16[512,2048]{1,0:T(8,128)(2,1)}, u32[]{:S(2)}) %copy-start) | copy-done | bytes 2097176
  2.4 1.0 copy-done.2
  3.4 1.0 copy-done.4
  4.4 1.0 copy-done.5
  5.5 0.7 copy-done.7
  6.1 6.6 %block.1 = (bf16[512,512]{1,0:T(8,128)(2,1)S(1)}, bf16[512,2048]{1,0:T(8,128)(2,1)S(1)}) custom-call(s32[1,8]{1,0:T(1,128)S(1)} %copy-done.7, bf16[512,512]{1,0:T(8,128)(2,1)S(1)} %copy-done.4, bf16[512,512]{1,0:T(8,128)(2,1)S(1)} %copy-done.2, bf16[512,2048]{1,0:T(8,128)(2,1)S(1)} %copy-done, bf16[512,512]{1,0:T(8,128)(2,1)S(1)} %copy-done.5), custom_call_target="tpu_custom_call" | custom-call | tf_op jit(solution)/shard_map/block/pallas_call | solution.py:116
  12.8 2.3 %weights.1 = (f32[256,1280]{1,0:T(8,128)S(1)}, f32[256,1280]{1,0:T(8,128)S(1)}, f32[256,1280]{1,0:T(8,128)S(1)}, f32[256,1280]{1,0:T(8,128)S(1)}) custom-call(s32[2]{0:T(128)S(1)} %pad_add_fusion.place, bf16[512,512]{1,0:T(8,128)(2,1)S(1)} %copy-done.4, bf16[512,512]{1,0:T(8,128)(2,1)S(1)} %copy-done.3, bf16[512,512]{1,0:T(8,128)(2,1)S(1)} %get-tuple-element.12.gated_out, ...), custom_call_target="tpu_custom_call" | custom-call | tf_op jit(solution)/shard_map/weights/pallas_call | solution.py:160
  15.1 0.5 collective-permute-start
  15.6 0.1 collective-permute-start.3
  15.7 2.6 %collective-permute-done = f32[256,1280]{1,0:T(8,128)S(1)} collective-permute-done((f32[256,1280]{1,0:T(8,128)S(1)}, f32[256,1280]{1,0:T(8,128)S(1)}, u32[]{:S(2)}, u32[]{:S(2)}) %collective-permute-start) | collective-permute-done | bytes 1310752 | tf_op jit(solution)/shard_map/ppermute | solution.py:288
  18.2 0.1 add.79
  18.4 0.0 copy-start.8
  18.4 2.9 %collective-permute-start.1 = (f32[128,1280]{1,0:T(8,128)S(1)}, f32[128,1280]{1,0:T(8,128)}, u32[]{:S(2)}, u32[]{:S(2)}) collective-permute-start(f32[128,1280]{1,0:T(8,128)S(1)} %slice.49), channel_id=1, source_target_pairs={{0,2},{1,3},{2,0},{3,1},{4,6},{5,7},{6,4},{7,5},{8,10},{9,11},{10,... | collective-permute-start | bytes 1966088 | tf_op jit(solution)/shard_map/ppermute | solution.py:288
  21.4 0.1 add.82
  21.5 0.0 copy-start.9
  21.5 0.9 slice.55
  22.5 0.3 copy-done.9
  22.8 1.6 %collective-permute-start.4 = (f32[128,1280]{1,0:T(8,128)}, f32[128,1280]{1,0:T(8,128)}, u32[]{:S(2)}, u32[]{:S(2)}) collective-permute-start(f32[128,1280]{1,0:T(8,128)} %slice.55), channel_id=1, source_target_pairs={{0,4},{1,5},{2,6},{3,7},{4,0},{5,1},{6,2},{7,3},{8,12},{9,13},{10,... | collective-permute-start | bytes 1966088 | tf_op jit(solution)/shard_map/ppermute | solution.py:288
  24.4 12.1 %collective-permute-done.1 = f32[128,1280]{1,0:T(8,128)} collective-permute-done((f32[128,1280]{1,0:T(8,128)S(1)}, f32[128,1280]{1,0:T(8,128)}, u32[]{:S(2)}, u32[]{:S(2)}) %collective-permute-start.1) | collective-permute-done | bytes 655392 | tf_op jit(solution)/shard_map/ppermute | solution.py:288
  36.5 1.4 slice_add_fusion.1
  37.9 1.8 %collective-permute-start.2 = (f32[64,1280]{1,0:T(8,128)S(1)}, f32[64,1280]{1,0:T(8,128)S(1)}, u32[]{:S(2)}, u32[]{:S(2)}) collective-permute-start(f32[64,1280]{1,0:T(8,128)S(1)} %slice.51), channel_id=1, source_target_pairs={{0,4},{1,5},{2,6},{3,7},{4,0},{5,1},{6,2},{7,3},{8,12},{9,13},{10,... | collective-permute-start | bytes 983048 | tf_op jit(solution)/shard_map/ppermute | solution.py:288
  39.7 0.0 collective-permute-done.4
  39.8 1.2 slice_add_fusion
  41.0 1.8 %collective-permute-start.5 = (f32[64,1280]{1,0:T(8,128)S(1)}, f32[64,1280]{1,0:T(8,128)S(1)}, u32[]{:S(2)}, u32[]{:S(2)}) collective-permute-start(f32[64,1280]{1,0:T(8,128)S(1)} %slice.57), channel_id=1, source_target_pairs={{0,2},{1,3},{2,0},{3,1},{4,6},{5,7},{6,4},{7,5},{8,10},{9,11},{10,... | collective-permute-start | bytes 983048 | tf_op jit(solution)/shard_map/ppermute | solution.py:288
  42.8 4.4 %collective-permute-done.2 = f32[64,1280]{1,0:T(8,128)S(1)} collective-permute-done((f32[64,1280]{1,0:T(8,128)S(1)}, f32[64,1280]{1,0:T(8,128)S(1)}, u32[]{:S(2)}, u32[]{:S(2)}) %collective-permute-start.2) | collective-permute-done | bytes 327712 | tf_op jit(solution)/shard_map/ppermute | solution.py:288
  47.3 2.7 %collective-permute-done.5 = f32[64,1280]{1,0:T(8,128)S(1)} collective-permute-done((f32[64,1280]{1,0:T(8,128)S(1)}, f32[64,1280]{1,0:T(8,128)S(1)}, u32[]{:S(2)}, u32[]{:S(2)}) %collective-permute-start.5) | collective-permute-done | bytes 327712 | tf_op jit(solution)/shard_map/ppermute | solution.py:288
  50.1 0.8 dynamic-slice_bitcast_fusion.6
  50.9 1.8 %collective-permute-start.6 = (f32[64,640]{1,0:T(8,128)}, f32[64,640]{1,0:T(8,128)S(1)}, u32[]{:S(2)}, u32[]{:S(2)}) collective-permute-start(f32[64,640]{1,0:T(8,128)} %get-tuple-element.23), channel_id=1, source_target_pairs={{0,8},{8,0},{16,24},{24,16},{1,9},{9,1},{17,25},{25,17},{2,10},{10... | collective-permute-start | bytes 491528 | tf_op jit(solution)/shard_map/ppermute | solution.py:288
  52.7 2.5 %collective-permute-start.8 = (f32[64,640]{1,0:T(8,128)}, f32[64,640]{1,0:T(8,128)}, u32[]{:S(2)}, u32[]{:S(2)}) collective-permute-start(f32[64,640]{1,0:T(8,128)} %get-tuple-element.24), channel_id=1, source_target_pairs={{0,24},{8,16},{16,8},{24,0},{1,25},{9,17},{17,9},{25,1},{2,26},{10... | collective-permute-start | bytes 491528 | tf_op jit(solution)/shard_map/ppermute | solution.py:288
  55.2 0.1 collective-permute-start.7
  55.3 2.8 %collective-permute-done.6 = f32[64,640]{1,0:T(8,128)S(1)} collective-permute-done((f32[64,640]{1,0:T(8,128)}, f32[64,640]{1,0:T(8,128)S(1)}, u32[]{:S(2)}, u32[]{:S(2)}) %collective-permute-start.6) | collective-permute-done | bytes 163872 | tf_op jit(solution)/shard_map/ppermute | solution.py:288
  58.1 5.1 %collective-permute-done.8 = f32[64,640]{1,0:T(8,128)} collective-permute-done((f32[64,640]{1,0:T(8,128)}, f32[64,640]{1,0:T(8,128)}, u32[]{:S(2)}, u32[]{:S(2)}) %collective-permute-start.8) | collective-permute-done | bytes 163872 | tf_op jit(solution)/shard_map/ppermute | solution.py:288
  63.2 5.4 %collective-permute-done.7 = f32[64,640]{1,0:T(8,128)} collective-permute-done((f32[64,640]{1,0:T(8,128)}, f32[64,640]{1,0:T(8,128)}, u32[]{:S(2)}, u32[]{:S(2)}) %collective-permute-start.7) | collective-permute-done | bytes 163872 | tf_op jit(solution)/shard_map/ppermute | solution.py:288
  68.6 1.0 fusion.2
  69.7 2.7 %collective-permute-start.11 = (f32[64,640]{1,0:T(8,128)S(1)}, f32[64,640]{1,0:T(8,128)S(1)}, u32[]{:S(2)}, u32[]{:S(2)}) collective-permute-start(f32[64,640]{1,0:T(8,128)S(1)} %fusion.2), channel_id=1, source_target_pairs={{0,24},{8,16},{16,8},{24,0},{1,25},{9,17},{17,9},{25,1},{2,26},{10... | collective-permute-start | bytes 491528 | tf_op jit(solution)/shard_map/ppermute | solution.py:288
  72.4 0.0 collective-permute-start.10
  72.4 1.7 %collective-permute-start.9 = (f32[64,640]{1,0:T(8,128)S(1)}, f32[64,640]{1,0:T(8,128)S(1)}, u32[]{:S(2)}, u32[]{:S(2)}) collective-permute-start(f32[64,640]{1,0:T(8,128)S(1)} %fusion.2), channel_id=1, source_target_pairs={{0,8},{8,0},{16,24},{24,16},{1,9},{9,1},{17,25},{25,17},{2,10},{10... | collective-permute-start | bytes 491528 | tf_op jit(solution)/shard_map/ppermute | solution.py:288
  74.1 4.5 %collective-permute-done.11 = f32[64,640]{1,0:T(8,128)S(1)} collective-permute-done((f32[64,640]{1,0:T(8,128)S(1)}, f32[64,640]{1,0:T(8,128)S(1)}, u32[]{:S(2)}, u32[]{:S(2)}) %collective-permute-start.11) | collective-permute-done | bytes 163872 | tf_op jit(solution)/shard_map/ppermute | solution.py:288
  78.7 5.8 %collective-permute-done.10 = f32[64,640]{1,0:T(8,128)S(1)} collective-permute-done((f32[64,640]{1,0:T(8,128)S(1)}, f32[64,640]{1,0:T(8,128)S(1)}, u32[]{:S(2)}, u32[]{:S(2)}) %collective-permute-start.10) | collective-permute-done | bytes 163872 | tf_op jit(solution)/shard_map/ppermute | solution.py:288
  84.4 0.0 collective-permute-done.9
  84.5 0.1 dynamic-slice_bitcast_fusion.1
  84.6 0.0 copy-start.1
  84.6 0.0 copy-start.6
  84.6 1.6 %collective-permute-start.15 = (f32[64,1280]{1,0:T(8,128)S(1)}, f32[64,1280]{1,0:T(8,128)S(1)}, u32[]{:S(2)}, u32[]{:S(2)}) collective-permute-start(f32[64,1280]{1,0:T(8,128)S(1)} %pad_maximum_fusion.7), channel_id=1, source_target_pairs={{0,2},{1,3},{2,0},{3,1},{4,6},{5,7},{6,4},{7,5},{8,10},{9,11},{10,... | collective-permute-start | bytes 983048 | tf_op jit(solution)/shard_map/ppermute | solution.py:288
  86.2 0.7 pad_maximum_fusion.6
  86.9 1.5 %collective-permute-start.12 = (f32[64,1280]{1,0:T(8,128)}, f32[64,1280]{1,0:T(8,128)}, u32[]{:S(2)}, u32[]{:S(2)}) collective-permute-start(f32[64,1280]{1,0:T(8,128)} %pad_maximum_fusion.6), channel_id=1, source_target_pairs={{0,4},{1,5},{2,6},{3,7},{4,0},{5,1},{6,2},{7,3},{8,12},{9,13},{10,... | collective-permute-start | bytes 983048 | tf_op jit(solution)/shard_map/ppermute | solution.py:288
  88.4 4.3 %collective-permute-done.15 = f32[64,1280]{1,0:T(8,128)S(1)} collective-permute-done((f32[64,1280]{1,0:T(8,128)S(1)}, f32[64,1280]{1,0:T(8,128)S(1)}, u32[]{:S(2)}, u32[]{:S(2)}) %collective-permute-start.15) | collective-permute-done | bytes 327712 | tf_op jit(solution)/shard_map/ppermute | solution.py:288
  92.7 0.7 copy-done.11
  93.5 0.9 pad_maximum_fusion.5
  94.4 1.5 %collective-permute-start.16 = (f32[128,1280]{1,0:T(8,128)}, f32[128,1280]{1,0:T(8,128)}, u32[]{:S(2)}, u32[]{:S(2)}) collective-permute-start(f32[128,1280]{1,0:T(8,128)} %pad_maximum_fusion.5), channel_id=1, source_target_pairs={{0,4},{1,5},{2,6},{3,7},{4,0},{5,1},{6,2},{7,3},{8,12},{9,13},{10,... | collective-permute-start | bytes 1966088 | tf_op jit(solution)/shard_map/ppermute | solution.py:288
  95.9 3.3 %items.1 = f32[32,72,128]{2,1,0:T(8,128)} custom-call(s32[1,512]{1,0:T(1,128)S(1)} %bitcast.37, bf16[512,512]{1,0:T(8,128)(2,1)S(1)} %copy-done.3, bf16[512,2048]{1,0:T(8,128)(2,1)S(1)} %get-tuple-element.11.grad_pre, bf16[512,2048]{1,0:T(8,128)(2,1)S(1)} %copy-done.1), custom_call_target="tpu_custom_call" | custom-call | tf_op jit(solution)/shard_map/items/pallas_call | solution.py:209
  99.2 3.9 %all-to-all-start = ((f32[32,72,128]{2,1,0:T(8,128)}), f32[32,72,128]{2,1,0:T(8,128)}, u32[]{:S(2)}, u32[]{:S(2)}) async-start(f32[32,72,128]{2,1,0:T(8,128)} %items.1), calls=%async_computation | async-start | bytes 2359296 | tf_op jit(solution)/shard_map/all_to_all | solution.py:330
  103.1 0.0 collective-permute-done.12
  103.1 1.0 pad_maximum_fusion.4
  104.1 1.8 %collective-permute-start.13 = (f32[128,1280]{1,0:T(8,128)S(1)}, f32[128,1280]{1,0:T(8,128)S(1)}, u32[]{:S(2)}, u32[]{:S(2)}) collective-permute-start(f32[128,1280]{1,0:T(8,128)S(1)} %pad_maximum_fusion.4), channel_id=1, source_target_pairs={{0,2},{1,3},{2,0},{3,1},{4,6},{5,7},{6,4},{7,5},{8,10},{9,11},{10,... | collective-permute-start | bytes 1966088 | tf_op jit(solution)/shard_map/ppermute | solution.py:288
  105.9 10.4 %collective-permute-done.16 = f32[128,1280]{1,0:T(8,128)} collective-permute-done((f32[128,1280]{1,0:T(8,128)}, f32[128,1280]{1,0:T(8,128)}, u32[]{:S(2)}, u32[]{:S(2)}) %collective-permute-start.16) | collective-permute-done | bytes 655392 | tf_op jit(solution)/shard_map/ppermute | solution.py:288
  116.4 1.2 pad_maximum_fusion.1.refs_2_
  117.5 0.1 collective-permute-start.17
  117.6 14.9 %collective-permute-done.13 = f32[128,1280]{1,0:T(8,128)S(1)} collective-permute-done((f32[128,1280]{1,0:T(8,128)S(1)}, f32[128,1280]{1,0:T(8,128)S(1)}, u32[]{:S(2)}, u32[]{:S(2)}) %collective-permute-start.13) | collective-permute-done | bytes 655392 | tf_op jit(solution)/shard_map/ppermute | solution.py:288
  132.5 1.1 pad_maximum_fusion.refs_0_
  133.6 0.1 collective-permute-start.14
  133.7 4.1 %table.1 = f32[1024,512]{1,0:T(8,128)} custom-call(f32[32,72,128]{2,1,0:T(8,128)} %all-to-all-done.got), custom_call_target="tpu_custom_call" | custom-call | tf_op jit(solution)/shard_map/table/pallas_call | solution.py:235
  137.8 4.2 %place.1 = (f32[512,2048]{1,0:T(8,128)}, f32[512,512]{1,0:T(8,128)}) custom-call(s32[2]{0:T(128)S(1)} %pad_add_fusion.place, f32[256,1280]{1,0:T(8,128)S(1)} %pad_maximum_fusion.refs_0_, f32[256,1280]{1,0:T(8,128)} %collective-permute-done.14.refs_1_, f32[256,1280]{1,0:T(8,128)S(1)} %pad_maximum_fusion.1.refs_2_, f32[256,1280]{1,0:T(8,128)} %collective-permute-done.17.refs_3_), custom_call_target="tpu_custom_call" | custom-call | tf_op jit(solution)/shard_map/place/pallas_call | solution.py:272
  (29 shorter events, 0.4 us)
Async XLA Ops:
  0.8 1.6 %copy-start = (bf16[512,2048]{1,0:T(8,128)(2,1)S(1)}, bf16[512,2048]{1,0:T(8,128)(2,1)}, u32[]{:S(2)}) copy-start(bf16[512,2048]{1,0:T(8,128)(2,1)} %in_proj.3) | copy-start | bytes 6291460
  2.4 1.0 copy-start.2
  3.4 1.0 copy-start.4
  4.4 1.0 copy-start.5
  5.5 0.7 copy-start.7
  6.1 6.6 %copy-start.3 = (bf16[512,512]{1,0:T(8,128)(2,1)S(1)}, bf16[512,512]{1,0:T(8,128)(2,1)}, u32[]{:S(2)}) copy-start(bf16[512,512]{1,0:T(8,128)(2,1)} %cot.5) | copy-start | bytes 1572868
  15.1 3.2 %collective-permute-start = (f32[256,1280]{1,0:T(8,128)S(1)}, f32[256,1280]{1,0:T(8,128)S(1)}, u32[]{:S(2)}, u32[]{:S(2)}) collective-permute-start(f32[256,1280]{1,0:T(8,128)S(1)} %get-tuple-element.14), channel_id=1, source_target_pairs={{0,1},{1,0},{2,3},{3,2},{4,5},{5,4},{6,7},{7,6},{8,9},{9,8},{10,11... | collective-permute-start | bytes 3932168 | tf_op jit(solution)/shard_map/ppermute | solution.py:288
  15.6 5.8 %collective-permute-start.3 = (f32[256,1280]{1,0:T(8,128)S(1)}, f32[256,1280]{1,0:T(8,128)S(1)}, u32[]{:S(2)}, u32[]{:S(2)}) collective-permute-start(f32[256,1280]{1,0:T(8,128)S(1)} %get-tuple-element.16), channel_id=1, source_target_pairs={{0,1},{1,0},{2,3},{3,2},{4,5},{5,4},{6,7},{7,6},{8,9},{9,8},{10,11... | collective-permute-start | bytes 3932168 | tf_op jit(solution)/shard_map/ppermute | solution.py:288
  18.4 3.1 %copy-start.8 = (f32[256,1280]{1,0:T(8,128)}, f32[256,1280]{1,0:T(8,128)S(1)}, u32[]{:S(2)}) copy-start(f32[256,1280]{1,0:T(8,128)S(1)} %add.79) | copy-start | bytes 3932164
  18.4 18.1 %collective-permute-start.1 = (f32[128,1280]{1,0:T(8,128)S(1)}, f32[128,1280]{1,0:T(8,128)}, u32[]{:S(2)}, u32[]{:S(2)}) collective-permute-start(f32[128,1280]{1,0:T(8,128)S(1)} %slice.49), channel_id=1, source_target_pairs={{0,2},{1,3},{2,0},{3,1},{4,6},{5,7},{6,4},{7,5},{8,10},{9,11},{10,... | collective-permute-start | bytes 1966088 | tf_op jit(solution)/shard_map/ppermute | solution.py:288
  21.5 1.3 copy-start.9
  22.8 17.0 %collective-permute-start.4 = (f32[128,1280]{1,0:T(8,128)}, f32[128,1280]{1,0:T(8,128)}, u32[]{:S(2)}, u32[]{:S(2)}) collective-permute-start(f32[128,1280]{1,0:T(8,128)} %slice.55), channel_id=1, source_target_pairs={{0,4},{1,5},{2,6},{3,7},{4,0},{5,1},{6,2},{7,3},{8,12},{9,13},{10,... | collective-permute-start | bytes 1966088 | tf_op jit(solution)/shard_map/ppermute | solution.py:288
  24.4 15.3 %copy-start.10 = (f32[256,1280]{1,0:T(8,128)S(1)}, f32[256,1280]{1,0:T(8,128)}, u32[]{:S(2)}) copy-start(f32[256,1280]{1,0:T(8,128)} %copy-done.9) | copy-start | bytes 3932164
  37.9 9.3 %collective-permute-start.2 = (f32[64,1280]{1,0:T(8,128)S(1)}, f32[64,1280]{1,0:T(8,128)S(1)}, u32[]{:S(2)}, u32[]{:S(2)}) collective-permute-start(f32[64,1280]{1,0:T(8,128)S(1)} %slice.51), channel_id=1, source_target_pairs={{0,4},{1,5},{2,6},{3,7},{4,0},{5,1},{6,2},{7,3},{8,12},{9,13},{10,... | collective-permute-start | bytes 983048 | tf_op jit(solution)/shard_map/ppermute | solution.py:288
  41.0 9.0 %collective-permute-start.5 = (f32[64,1280]{1,0:T(8,128)S(1)}, f32[64,1280]{1,0:T(8,128)S(1)}, u32[]{:S(2)}, u32[]{:S(2)}) collective-permute-start(f32[64,1280]{1,0:T(8,128)S(1)} %slice.57), channel_id=1, source_target_pairs={{0,2},{1,3},{2,0},{3,1},{4,6},{5,7},{6,4},{7,5},{8,10},{9,11},{10,... | collective-permute-start | bytes 983048 | tf_op jit(solution)/shard_map/ppermute | solution.py:288
  50.9 7.2 %collective-permute-start.6 = (f32[64,640]{1,0:T(8,128)}, f32[64,640]{1,0:T(8,128)S(1)}, u32[]{:S(2)}, u32[]{:S(2)}) collective-permute-start(f32[64,640]{1,0:T(8,128)} %get-tuple-element.23), channel_id=1, source_target_pairs={{0,8},{8,0},{16,24},{24,16},{1,9},{9,1},{17,25},{25,17},{2,10},{10... | collective-permute-start | bytes 491528 | tf_op jit(solution)/shard_map/ppermute | solution.py:288
  52.7 10.5 %collective-permute-start.8 = (f32[64,640]{1,0:T(8,128)}, f32[64,640]{1,0:T(8,128)}, u32[]{:S(2)}, u32[]{:S(2)}) collective-permute-start(f32[64,640]{1,0:T(8,128)} %get-tuple-element.24), channel_id=1, source_target_pairs={{0,24},{8,16},{16,8},{24,0},{1,25},{9,17},{17,9},{25,1},{2,26},{10... | collective-permute-start | bytes 491528 | tf_op jit(solution)/shard_map/ppermute | solution.py:288
  55.2 13.4 %collective-permute-start.7 = (f32[64,640]{1,0:T(8,128)}, f32[64,640]{1,0:T(8,128)}, u32[]{:S(2)}, u32[]{:S(2)}) collective-permute-start(f32[64,640]{1,0:T(8,128)} %get-tuple-element.25), channel_id=1, source_target_pairs={{0,16},{8,24},{16,0},{24,8},{1,17},{9,25},{17,1},{25,9},{2,18},{10... | collective-permute-start | bytes 491528 | tf_op jit(solution)/shard_map/ppermute | solution.py:288
  69.7 9.0 %collective-permute-start.11 = (f32[64,640]{1,0:T(8,128)S(1)}, f32[64,640]{1,0:T(8,128)S(1)}, u32[]{:S(2)}, u32[]{:S(2)}) collective-permute-start(f32[64,640]{1,0:T(8,128)S(1)} %fusion.2), channel_id=1, source_target_pairs={{0,24},{8,16},{16,8},{24,0},{1,25},{9,17},{17,9},{25,1},{2,26},{10... | collective-permute-start | bytes 491528 | tf_op jit(solution)/shard_map/ppermute | solution.py:288
  72.4 12.1 %collective-permute-start.10 = (f32[64,640]{1,0:T(8,128)S(1)}, f32[64,640]{1,0:T(8,128)S(1)}, u32[]{:S(2)}, u32[]{:S(2)}) collective-permute-start(f32[64,640]{1,0:T(8,128)S(1)} %fusion.2), channel_id=1, source_target_pairs={{0,16},{8,24},{16,0},{24,8},{1,17},{9,25},{17,1},{25,9},{2,18},{10... | collective-permute-start | bytes 491528 | tf_op jit(solution)/shard_map/ppermute | solution.py:288
  72.4 12.1 %collective-permute-start.9 = (f32[64,640]{1,0:T(8,128)S(1)}, f32[64,640]{1,0:T(8,128)S(1)}, u32[]{:S(2)}, u32[]{:S(2)}) collective-permute-start(f32[64,640]{1,0:T(8,128)S(1)} %fusion.2), channel_id=1, source_target_pairs={{0,8},{8,0},{16,24},{24,16},{1,9},{9,1},{17,25},{25,17},{2,10},{10... | collective-permute-start | bytes 491528 | tf_op jit(solution)/shard_map/ppermute | solution.py:288
  84.6 11.3 %copy-start.1 = (bf16[512,2048]{1,0:T(8,128)(2,1)S(1)}, bf16[512,2048]{1,0:T(8,128)(2,1)}, u32[]{:S(2)}) copy-start(bf16[512,2048]{1,0:T(8,128)(2,1)} %in_proj.3) | copy-start | bytes 6291460
  84.6 11.3 %copy-start.6 = (s32[512]{0:T(512)S(1)}, s32[512]{0:T(512)}, u32[]{:S(2)}) copy-start(s32[512]{0:T(512)} %param.11) | copy-start | bytes 6148
  84.6 8.1 %collective-permute-start.15 = (f32[64,1280]{1,0:T(8,128)S(1)}, f32[64,1280]{1,0:T(8,128)S(1)}, u32[]{:S(2)}, u32[]{:S(2)}) collective-permute-start(f32[64,1280]{1,0:T(8,128)S(1)} %pad_maximum_fusion.7), channel_id=1, source_target_pairs={{0,2},{1,3},{2,0},{3,1},{4,6},{5,7},{6,4},{7,5},{8,10},{9,11},{10,... | collective-permute-start | bytes 983048 | tf_op jit(solution)/shard_map/ppermute | solution.py:288
  86.9 16.2 %collective-permute-start.12 = (f32[64,1280]{1,0:T(8,128)}, f32[64,1280]{1,0:T(8,128)}, u32[]{:S(2)}, u32[]{:S(2)}) collective-permute-start(f32[64,1280]{1,0:T(8,128)} %pad_maximum_fusion.6), channel_id=1, source_target_pairs={{0,4},{1,5},{2,6},{3,7},{4,0},{5,1},{6,2},{7,3},{8,12},{9,13},{10,... | collective-permute-start | bytes 983048 | tf_op jit(solution)/shard_map/ppermute | solution.py:288
  92.7 0.7 copy-start.11
  94.4 22.0 %collective-permute-start.16 = (f32[128,1280]{1,0:T(8,128)}, f32[128,1280]{1,0:T(8,128)}, u32[]{:S(2)}, u32[]{:S(2)}) collective-permute-start(f32[128,1280]{1,0:T(8,128)} %pad_maximum_fusion.5), channel_id=1, source_target_pairs={{0,4},{1,5},{2,6},{3,7},{4,0},{5,1},{6,2},{7,3},{8,12},{9,13},{10,... | collective-permute-start | bytes 1966088 | tf_op jit(solution)/shard_map/ppermute | solution.py:288
  99.2 17.2 %copy-start.12 = (f32[64,1280]{1,0:T(8,128)S(1)}, f32[64,1280]{1,0:T(8,128)}, u32[]{:S(2)}) copy-start(f32[64,1280]{1,0:T(8,128)} %copy-done.11) | copy-start | bytes 983044
  99.2 34.5 %all-to-all-start = ((f32[32,72,128]{2,1,0:T(8,128)}), f32[32,72,128]{2,1,0:T(8,128)}, u32[]{:S(2)}, u32[]{:S(2)}) async-start(f32[32,72,128]{2,1,0:T(8,128)} %items.1), calls=%async_computation | async-start | bytes 2359296 | tf_op jit(solution)/shard_map/all_to_all | solution.py:330
  104.1 28.4 %collective-permute-start.13 = (f32[128,1280]{1,0:T(8,128)S(1)}, f32[128,1280]{1,0:T(8,128)S(1)}, u32[]{:S(2)}, u32[]{:S(2)}) collective-permute-start(f32[128,1280]{1,0:T(8,128)S(1)} %pad_maximum_fusion.4), channel_id=1, source_target_pairs={{0,2},{1,3},{2,0},{3,1},{4,6},{5,7},{6,4},{7,5},{8,10},{9,11},{10,... | collective-permute-start | bytes 1966088 | tf_op jit(solution)/shard_map/ppermute | solution.py:288
  117.5 20.2 %collective-permute-start.17 = (f32[256,1280]{1,0:T(8,128)S(1)}, f32[256,1280]{1,0:T(8,128)}, u32[]{:S(2)}, u32[]{:S(2)}) collective-permute-start(f32[256,1280]{1,0:T(8,128)S(1)} %pad_maximum_fusion.1.refs_2_), channel_id=1, source_target_pairs={{0,1},{1,0},{2,3},{3,2},{4,5},{5,4},{6,7},{7,6},{8,9},{9,8},{10,11... | collective-permute-start | bytes 3932168 | tf_op jit(solution)/shard_map/ppermute | solution.py:288
  133.6 4.2 %collective-permute-start.14 = (f32[256,1280]{1,0:T(8,128)S(1)}, f32[256,1280]{1,0:T(8,128)}, u32[]{:S(2)}, u32[]{:S(2)}) collective-permute-start(f32[256,1280]{1,0:T(8,128)S(1)} %pad_maximum_fusion.refs_0_), channel_id=1, source_target_pairs={{0,1},{1,0},{2,3},{3,2},{4,5},{5,4},{6,7},{7,6},{8,9},{9,8},{10,11... | collective-permute-start | bytes 3932168 | tf_op jit(solution)/shard_map/ppermute | solution.py:288

commit v2 on v1

--- a/solution.py
+++ b/solution.py
@@ -17,6 +17,7 @@
 norm_eps = 1e-05
 VMEM = pltpu.MemorySpace.VMEM
 SMEM = pltpu.MemorySpace.SMEM
+HBM = pltpu.MemorySpace.HBM
 
 
 def dot_nn(a, b):
@@ -35,10 +36,22 @@
     return 0.5 * jnp.tanh(0.5 * z) + 0.5
 
 
-def block_kernel(lengths, emb, cot, in_proj, out_proj, gated_out, grad_pre, hid, dpre, mask, wts, dsc, att):
+def block_kernel(
+    chunk, place, lengths, emb_hbm, cot_hbm, in_hbm, out_hbm,
+    keep, send, grad_pre, rel_a, rel_b, rel_g,
+    emb, cot, in_proj, out_proj, hid, dpre, mask, wts, dsc, att, gated_out, sems,
+):
     rows, width = emb.shape
     head = width // H
     scale = 1.0 / math.sqrt(head)
+    copies = [pltpu.make_async_copy(emb_hbm, emb, sems.at[0])]
+    for c in range(4):
+        cols = pl.ds(c * width, width)
+        copies.append(pltpu.make_async_copy(in_hbm.at[:, cols], in_proj.at[:, cols], sems.at[1 + c]))
+    copies.append(pltpu.make_async_copy(cot_hbm, cot, sems.at[5]))
+    copies.append(pltpu.make_async_copy(out_hbm, out_proj, sems.at[6]))
+    for c in copies:
+        c.start()
     along_lane = lax.broadcasted_iota(jnp.int32, (1, rows), 1)
     along_row = lax.broadcasted_iota(jnp.int32, (rows, 1), 0)
     end = jnp.int32(0)
@@ -52,13 +65,23 @@
         own = seg_row[i * TILE : n] == seg_lane[:, :n]
         past = along_lane[:, :n] <= along_row[i * TILE : n]
         mask[r, :n] = jnp.where(own & past, 1.0 / LEN, 0.0)
+    copies[0].wait()
     for c in range(4):
         cols = pl.ds(c * width, width)
+        copies[1 + c].wait()
         z = dot_nn(emb[...], in_proj[:, cols])
         sig = sigmoid(z)
         act = z * sig
         hid[:, cols] = act.astype(jnp.bfloat16)
         dpre[:, cols] = sig + act * (1.0 - sig)
+    emb_t = emb[...].T
+    count = width // chunk
+    for c in range(count):
+        src = slice(c * chunk, (c + 1) * chunk)
+        to_a = pl.ds(pl.multiple_of((c ^ place[0]) * chunk, chunk), chunk)
+        to_b = pl.ds(pl.multiple_of((c ^ place[1]) * chunk, chunk), chunk)
+        rel_a[to_a, :] = emb_t[src]
+        rel_b[to_b, :] = emb_t[src]
     for h in range(H):
         v, q, k = (pl.ds((c * H + h) * head, head) for c in (1, 2, 3))
         for i in range(rows // TILE):
@@ -71,6 +94,8 @@
             wts[h, r, :n] = w
             dsc[h, r, :n] = (sig + act * (1.0 - sig)) * m
             att[r, pl.ds(h * head, head)] = dot_nn(w, hid[:n, v])
+    copies[5].wait()
+    copies[6].wait()
     grad_att = []
     for i in range(rows // TILE):
         r = pl.ds(i * TILE, TILE)
@@ -89,6 +114,10 @@
             - normed * jnp.mean(grad_norm * normed, axis=1, keepdims=True)
         )
         grad_att.append(g.astype(jnp.bfloat16))
+    gated_t = gated_out[...].T
+    for c in range(count):
+        to_b = pl.ds(pl.multiple_of((c ^ place[1]) * chunk, chunk), chunk)
+        rel_g[to_b, :] = gated_t[c * chunk : (c + 1) * chunk]
     for h in range(H):
         v, q, k = (pl.ds((c * H + h) * head, head) for c in (1, 2, 3))
         grad_v, grad_k = [None] * (rows // TILE), [None] * (rows // TILE)
@@ -108,64 +137,63 @@
             r = pl.ds(j * TILE, TILE)
             grad_pre[r, v] = (grad_v[j] * dpre[r, v]).astype(jnp.bfloat16)
             grad_pre[r, k] = (grad_k[j] * scale * dpre[r, k]).astype(jnp.bfloat16)
-
-
-def block_call(lengths, emb, cot, in_proj, out_proj):
+    half, cut = width // 2, keep.shape[1]
+    for out, r in ((send, pl.ds(half, half)), (keep, pl.ds(0, half))):
+        out[:half, :] = dot_nn(rel_a[r, :], grad_pre[:, :cut])
+        out[half:, :] = dot_nn(rel_b[r, :], grad_pre[:, cut : 2 * cut])
+
+
+def block_call(chunk, place, lengths, emb, cot, in_proj, out_proj):
     rows, width = emb.shape
     vmem = pl.BlockSpec(memory_space=VMEM)
+    part = jax.ShapeDtypeStruct((width, 5 * width // 4), jnp.float32)
+    square = jax.ShapeDtypeStruct((width, rows), jnp.bfloat16)
     return pl.pallas_call(
-        block_kernel,
+        functools.partial(block_kernel, chunk),
         name="block",
-        out_shape=(
-            jax.ShapeDtypeStruct((rows, width), jnp.bfloat16),
-            jax.ShapeDtypeStruct((rows, 4 * width), jnp.bfloat16),
-        ),
-        in_specs=[pl.BlockSpec(memory_space=SMEM)] + [vmem] * 4,
-        out_specs=(vmem, vmem),
+        out_shape=(part, part, jax.ShapeDtypeStruct((rows, 4 * width), jnp.bfloat16), square, square, square),
+        in_specs=[pl.BlockSpec(memory_space=SMEM)] * 2 + [pl.BlockSpec(memory_space=HBM)] * 4,
+        out_specs=(vmem,) * 6,
         scratch_shapes=[
+            pltpu.VMEM((rows, width), jnp.bfloat16),
+            pltpu.VMEM((rows, width), jnp.bfloat16),
+            pltpu.VMEM((width, 4 * width), jnp.bfloat16),
+            pltpu.VMEM((width, width), jnp.bfloat16),
             pltpu.VMEM((rows, 4 * width), jnp.bfloat16),
             pltpu.VMEM((rows, 4 * width), jnp.float32),
             pltpu.VMEM((rows, rows), jnp.float32),
             pltpu.VMEM((H, rows, rows), jnp.bfloat16),
             pltpu.VMEM((H, rows, rows), jnp.float32),
             pltpu.VMEM((rows, width), jnp.float32),
+            pltpu.VMEM((rows, width), jnp.bfloat16),
+            pltpu.SemaphoreType.DMA((7,)),
         ],
         compiler_params=pltpu.CompilerParams(vmem_limit_bytes=40 << 20),
-    )(lengths, emb, cot, in_proj, out_proj)
-
-
-def weight_kernel(chunk, place, emb, cot, gated_out, grad_pre, a_keep, b_keep, a_send, b_send, rel_a, rel_b, rel_g):
-    width = emb.shape[1]
-    half, rest = a_keep.shape
-    emb_t, gated_t = emb[...].T, gated_out[...].T
-    count = width // chunk
-    for c in range(count):
-        src = slice(c * chunk, (c + 1) * chunk)
-        to_a = pl.ds(pl.multiple_of((c ^ place[0]) * chunk, chunk), chunk)
-        to_b = pl.ds(pl.multiple_of((c ^ place[1]) * chunk, chunk), chunk)
-        rel_a[to_a, :] = emb_t[src]
-        rel_b[to_b, :] = emb_t[src]
-        rel_g[to_b, :] = gated_t[src]
-    in_b = 4 * width - rest
-    for out_a, out_b, r in ((a_send, b_send, pl.ds(half, half)), (a_keep, b_keep, pl.ds(0, half))):
-        out_a[...] = dot_nn(rel_a[r, :], grad_pre[:, :rest])
-        out_b[:, :in_b] = dot_nn(rel_b[r, :], grad_pre[:, rest:])
-        out_b[:, in_b:] = dot_nn(rel_g[r, :], cot[...])
-
-
-def weight_call(chunk, place, emb, cot, gated_out, grad_pre):
-    width = emb.shape[1]
+    )(place, lengths, emb, cot, in_proj, out_proj)
+
+
+def second_kernel(rel_a, rel_b, rel_g, cot, grad_pre, keep, send):
+    width = cot.shape[1]
+    half, cut = width // 2, keep.shape[1]
+    inner = 4 * width - 3 * cut
+    for out, r in ((send, pl.ds(half, half)), (keep, pl.ds(0, half))):
+        out[:half, :] = dot_nn(rel_a[r, :], grad_pre[:, 2 * cut : 3 * cut])
+        out[half:, :inner] = dot_nn(rel_b[r, :], grad_pre[:, 3 * cut :])
+        out[half:, inner:] = dot_nn(rel_g[r, :], cot[...])
+
+
+def second_call(rel_a, rel_b, rel_g, cot, grad_pre):
+    width = cot.shape[1]
     vmem = pl.BlockSpec(memory_space=VMEM)
-    part = jax.ShapeDtypeStruct((width // 2, 5 * width // 2), jnp.float32)
+    part = jax.ShapeDtypeStruct((width, 5 * width // 4), jnp.float32)
     return pl.pallas_call(
-        functools.partial(weight_kernel, chunk),
-        name="weights",
-        out_shape=(part,) * 4,
-        in_specs=[pl.BlockSpec(memory_space=SMEM)] + [vmem] * 4,
-        out_specs=(vmem,) * 4,
-        scratch_shapes=[pltpu.VMEM((width, width), jnp.bfloat16)] * 3,
-        compiler_params=pltpu.CompilerParams(vmem_limit_bytes=40 << 20),
-    )(place, emb, cot, gated_out, grad_pre)
+        second_kernel,
+        name="second",
+        out_shape=(part, part),
+        in_specs=[vmem] * 5,
+        out_specs=(vmem,) * 2,
+        compiler_params=pltpu.CompilerParams(vmem_limit_bytes=16 << 20),
+    )(rel_a, rel_b, rel_g, cot, grad_pre)
 
 
 def split_bf16(x):
@@ -242,23 +270,22 @@
     )(got)
 
 
-def place_kernel(count, chunk, place, *refs):
-    pieces, (in_grad, out_grad), sems = refs[:-3], refs[-3:-1], refs[-1]
-    width = in_grad.shape[0]
-    rest = pieces[0].shape[1]
-    in_b = 4 * width - rest
+def place_kernel(chunk, column, place, *refs):
+    pieces, outs, sems = refs[:8], refs[-3:-1], refs[-1]
+    in_grad, out_grad = outs
+    cut = pieces[0].shape[1]
     copies = []
     for side in range(2):
+        first = column + side * cut
+        inner = min(cut, in_grad.shape[1] - first)
         position = 0
-        for piece in pieces[side * len(pieces) // 2 : (side + 1) * len(pieces) // 2]:
+        for piece in pieces[side * 4 : side * 4 + 4]:
             for c in range(piece.shape[0] // chunk):
                 row = pl.ds(pl.multiple_of((position ^ place[side]) * chunk, chunk), chunk)
                 src = piece.at[pl.ds(c * chunk, chunk)]
-                if side == 0:
-                    copies.append((src, in_grad.at[row, pl.ds(0, rest)]))
-                else:
-                    copies.append((src.at[:, pl.ds(0, in_b)], in_grad.at[row, pl.ds(rest, in_b)]))
-                    copies.append((src.at[:, pl.ds(in_b, width)], out_grad.at[row, :]))
+                copies.append((src.at[:, pl.ds(0, inner)], in_grad.at[row, pl.ds(first, inner)]))
+                if inner < cut:
+                    copies.append((src.at[:, pl.ds(inner, cut - inner)], out_grad.at[row, :]))
                 position += 1
     copies = [pltpu.make_async_copy(s, d, sems.at[i]) for i, (s, d) in enumerate(copies)]
     for c in copies:
@@ -267,20 +294,22 @@
         c.wait()
 
 
-def place_call(chunk, place, pieces, width):
+def place_call(chunk, column, place, pieces, width, grads):
     count = width // chunk
+    anywhere = pl.BlockSpec(memory_space=HBM)
     return pl.pallas_call(
-        functools.partial(place_kernel, count, chunk),
+        functools.partial(place_kernel, chunk, column),
         name="place",
         out_shape=(
             jax.ShapeDtypeStruct((width, 4 * width), jnp.float32),
             jax.ShapeDtypeStruct((width, width), jnp.float32),
         ),
-        in_specs=[pl.BlockSpec(memory_space=SMEM)] + [pl.BlockSpec(memory_space=VMEM)] * len(pieces),
-        out_specs=(pl.BlockSpec(memory_space=pl.ANY),) * 2,
+        in_specs=[pl.BlockSpec(memory_space=SMEM)] + [pl.BlockSpec(memory_space=VMEM)] * 8 + [anywhere] * len(grads),
+        out_specs=(anywhere,) * 2,
         scratch_shapes=[pltpu.SemaphoreType.DMA((3 * count,))],
-        compiler_params=pltpu.CompilerParams(vmem_limit_bytes=40 << 20),
-    )(place, *pieces)
+        input_output_aliases={9 + i: i for i in range(len(grads))},
+        compiler_params=pltpu.CompilerParams(vmem_limit_bytes=16 << 20),
+    )(place, *pieces, *grads)
 
 
 def swap(x, axis, distance):
@@ -307,48 +336,53 @@
     return x[:n], x[n:]
 
 
+def reduce_all(keep, send, order_a, order_b, scale):
+    dp_count = lax.axis_size("dp")
+    odd = lax.axis_index("dp") % 2 == 1
+    a, b = halve(keep + swap(send, "table", order_a[0]))
+    for bit_a, bit_b in zip(order_a[1:], order_b[1:]):
+        (a_keep, a_send), (b_keep, b_send) = halve(a), halve(b)
+        a = a_keep + swap(a_send, "table", bit_a)
+        b = b_keep + swap(b_send, "table", bit_b)
+    x = jnp.where(odd, b, a) + swap(jnp.where(odd, a, b), "dp", 1)
+    distance = 2
+    while distance < dp_count:
+        x = x + swap(x, "dp", distance)
+        distance *= 2
+    x = x * scale
+    other = swap(x, "dp", 1)
+    a, b = jnp.where(odd, other, x), jnp.where(odd, x, other)
+    for bit_a, bit_b in zip(order_a[:1:-1], order_b[:1:-1]):
+        a = jnp.concatenate([a, swap(a, "table", bit_a)], axis=0)
+        b = jnp.concatenate([b, swap(b, "table", bit_b)], axis=0)
+    pieces = []
+    for x, bit in ((a, order_a[1]), (b, order_b[1])):
+        far = swap(x, "table", bit)
+        pieces += [x, far, swap(x, "table", order_a[0]), swap(far, "table", order_a[0])]
+    return pieces
+
+
 def per_device(item_emb, cotangent, in_proj, out_proj, history_lengths, item_ids):
     rows_here, width = item_emb.shape
-    dp_count = lax.axis_size("dp")
     table_count = lax.axis_size("table")
-    owners = dp_count * table_count
+    owners = lax.axis_size("dp") * table_count
     slots = max(8, rows_here // owners)
     order_a, order_b = orders(table_count)
-    table_index, dp_index = lax.axis_index("table"), lax.axis_index("dp")
+    table_index = lax.axis_index("table")
     place = jnp.stack([position(order_a, table_index), position(order_b, table_index)])
     chunk = width // table_count
-
-    gated_out, grad_pre = block_call(history_lengths, item_emb, cotangent, in_proj, out_proj)
-    a_keep, b_keep, a_send, b_send = weight_call(chunk, place, item_emb, cotangent, gated_out, grad_pre)
+    scale = 1.0 / math.sqrt(rows_here * owners)
+
+    keep_e, send_e, grad_pre, *rel = block_call(
+        chunk, place, history_lengths, item_emb, cotangent, in_proj, out_proj
+    )
+    keep_f, send_f = second_call(*rel, cotangent, grad_pre)
     sent = item_call(owners, slots, item_ids.reshape(1, rows_here), cotangent, grad_pre, in_proj)
-
-    for step, (bit_a, bit_b) in enumerate(zip(order_a, order_b)):
-        a_got, b_got = swap(a_send, "table", bit_a), swap(b_send, "table", bit_b)
-        a_sum, b_sum = a_keep + a_got, b_keep + b_got
-        if step + 1 < len(order_a):
-            (a_keep, a_send), (b_keep, b_send) = halve(a_sum), halve(b_sum)
     got = lax.all_to_all(sent, ("dp", "table"), split_axis=0, concat_axis=0, tiled=True)
-
-    cut = 2 * a_sum.shape[1] // dp_count
-    pieces = [x[:, i * cut : (i + 1) * cut] for x in (a_sum, b_sum) for i in range(dp_count // 2)]
-    pieces = jnp.stack(pieces)
-    mine = lambda d: lax.dynamic_index_in_dim(pieces, dp_index ^ d, 0, keepdims=False)
-    total = mine(0)
-    for d in range(1, dp_count):
-        total = total + swap(mine(d), "dp", d)
-    total = total * (1.0 / math.sqrt(rows_here * owners))
-    whole = [total] + [swap(total, "dp", d) for d in range(1, dp_count)]
-    whole = jnp.stack(whole)
-    whole = [lax.dynamic_index_in_dim(whole, dp_index ^ d, 0, keepdims=False) for d in range(dp_count)]
-    a = [jnp.concatenate(whole[: dp_count // 2], axis=1)]
-    b = [jnp.concatenate(whole[dp_count // 2 :], axis=1)]
-
-    for bit_a, bit_b in zip(order_a[::-1], order_b[::-1]):
-        join = lambda x: x[0] if len(x) == 1 else jnp.concatenate(x, axis=0)
-        a, b = [join(a)], [join(b)]
-        a.append(swap(a[0], "table", bit_a))
-        b.append(swap(b[0], "table", bit_b))
-    in_grad, out_grad = place_call(chunk, place, a + b, width)
+    pieces_e = reduce_all(keep_e, send_e, order_a, order_b, scale)
+    pieces_f = reduce_all(keep_f, send_f, order_a, order_b, scale)
+    grads = place_call(chunk, 0, place, pieces_e, width, ())
+    in_grad, out_grad = place_call(chunk, 2 * keep_e.shape[1], place, pieces_f, width, grads)
     emb_grad = table_call(owners, slots, got, width)
     return (emb_grad, in_grad, out_grad)
 

time: 143 us -> 142 us (level)
  starting transfers between devices: 28 us -> 37.1 us
  waiting for transfers between devices: 75.1 us -> 69.2 us
  other arithmetic: 9.01 us -> 3.66 us
  Pallas kernels: 20.5 us -> 22.3 us
    ppermute x18 -> x32, starting transfers between devices: 24.1 us -> 32.2 us  [swap(): return lax.ppermute(x, axis, [(i, i ^ distance) for i in range(size)])]
    ppermute x18 -> x32, waiting for transfers between devices: 75.1 us -> 69.2 us  [swap(): return lax.ppermute(x, axis, [(i, i ^ distance) for i in range(size)])]
    concatenate x6 -> x4, other arithmetic: 4.9 us -> 0.09 us  [the longest x2 0.04 us: reduce_all(): a = jnp.concatenate([a, swap(a, 'table', bit_a)], axis=0)]
    pallas_call x3 -> x4, Pallas kernels: 13.1 us -> 16.2 us  [the longest x1 9.58 us: block_call(): pl.pallas_call(functools.partial(block_kernel, chunk), name='block', out_...]
    unnamed x26 -> x34, local copies, waits for them, and re-layouts: 6.47 us -> 8.31 us
    add x6 -> x8, other arithmetic: 2.9 us -> 3.32 us  [the longest x2 2.12 us: reduce_all(): b = b_keep + swap(b_send, 'table', bit_b)]
  transfers between devices with their start and end apart: 19 -> 33, of which waited for: 12 -> 17; matrix products, arithmetic and copies ran while one was open for 6% -> 3% of each run, Pallas kernels for 5% -> 6%
where the time goes in v2:
time: 142 us
  waiting for transfers between devices  69.2 us (49%)
  starting transfers between devices  37.1 us (26%)
  Pallas kernels  22.3 us (16%)
  local copies, waits for them, and re-layouts  8.41 us (6%)
  other arithmetic  3.66 us (3%)
    ppermute x32, waiting for transfers between devices, swap(): return lax.ppermute(x, axis, [(i, i ^ distance) for i in range(size)])  69.2 us
    ppermute x32, starting transfers between devices, swap(): return lax.ppermute(x, axis, [(i, i ^ distance) for i in range(size)])  32.2 us
    pallas_call x1, Pallas kernels, block_call(): pl.pallas_call(functools.partial(block_kernel, chunk), name='block', out_...  9.58 us
    unnamed x34, local copies, waits for them, and re-layouts  8.31 us
    pallas_call x2, Pallas kernels, place_call(): pl.pallas_call(functools.partial(place_kernel, chunk, column), name='plac...  5.65 us
    all_to_all x1, starting transfers between devices, per_device(): lax.all_to_all(sent, ('dp', 'table'), split_axis=0, concat_axis=0, tiled=...  4.89 us
    pallas_call x1, Pallas kernels, item_call(): pl.pallas_call(functools.partial(item_kernel, owners, slots), name='items...  3.32 us
  transfers between devices with their start and end apart: 33, of which 17 were waited for; matrix products, arithmetic and copies ran while one was open for 3% of the time, Pallas kernels for 6%

profile of v2, /device:TPU:0, one launch (start us, length us, event | category | flops | bytes accessed | tf_op | source)
XLA Modules:
  0.0 141.8 jit_solution(10263051030962443459)
XLA Ops:
  0.7 0.1 pad_add_fusion.place
  0.8 1.6 %copy-done = bf16[512,2048]{1,0:T(8,128)(2,1)S(1)} copy-done((bf16[512,2048]{1,0:T(8,128)(2,1)S(1)}, bf16[512,2048]{1,0:T(8,128)(2,1)}, u32[]{:S(2)}) %copy-start) | copy-done | bytes 2097176
  2.4 1.0 copy-done.2
  3.4 1.0 copy-done.4
  4.4 1.0 copy-done.5
  5.5 0.7 copy-done.15
  6.1 9.6 %block.1 = (f32[512,640]{1,0:T(8,128)S(1)}, f32[512,640]{1,0:T(8,128)S(1)}, bf16[512,2048]{1,0:T(8,128)(2,1)S(1)}, bf16[512,512]{1,0:T(8,128)(2,1)S(1)}, bf16[51...) custom-call(s32[2]{0:T(128)S(1)} %pad_add_fusion.place, s32[1,8]{1,0:T(1,128)S(1)} %copy-done.15, ...), custom_call_target="tpu_custom_call" | custom-call | tf_op jit(solution)/shard_map/block/pallas_call | solution.py:151
  15.7 1.0 second.1
  16.7 0.5 collective-permute-start
  17.2 0.1 collective-permute-start.16
  17.3 2.6 %collective-permute-done = f32[512,640]{1,0:T(8,128)S(1)} collective-permute-done((f32[512,640]{1,0:T(8,128)S(1)}, f32[512,640]{1,0:T(8,128)S(1)}, u32[]{:S(2)}, u32[]{:S(2)}) %collective-permute-start) | collective-permute-done | bytes 1310752 | tf_op jit(solution)/shard_map/ppermute | solution.py:317
  19.9 0.1 add.82
  20.1 2.9 %collective-permute-start.3 = (f32[128,640]{1,0:T(8,128)S(1)}, f32[128,640]{1,0:T(8,128)S(1)}, u32[]{:S(2)}, u32[]{:S(2)}) collective-permute-start(f32[128,640]{1,0:T(8,128)S(1)} %slice.81), channel_id=1, source_target_pairs={{0,2},{1,3},{2,0},{3,1},{4,6},{5,7},{6,4},{7,5},{8,10},{9,11},{10,... | collective-permute-start | bytes 983048 | tf_op jit(solution)/shard_map/ppermute | solution.py:317
  23.0 0.1 add.89
  23.2 1.7 %collective-permute-start.19 = (f32[128,640]{1,0:T(8,128)S(1)}, f32[128,640]{1,0:T(8,128)S(1)}, u32[]{:S(2)}, u32[]{:S(2)}) collective-permute-start(f32[128,640]{1,0:T(8,128)S(1)} %slice.89), channel_id=1, source_target_pairs={{0,2},{1,3},{2,0},{3,1},{4,6},{5,7},{6,4},{7,5},{8,10},{9,11},{10,... | collective-permute-start | bytes 983048 | tf_op jit(solution)/shard_map/ppermute | solution.py:317
  24.9 6.6 %collective-permute-done.3 = f32[128,640]{1,0:T(8,128)S(1)} collective-permute-done((f32[128,640]{1,0:T(8,128)S(1)}, f32[128,640]{1,0:T(8,128)S(1)}, u32[]{:S(2)}, u32[]{:S(2)}) %collective-permute-start.3) | collective-permute-done | bytes 327712 | tf_op jit(solution)/shard_map/ppermute | solution.py:317
  31.5 0.8 slice_add_fusion.2
  32.3 2.1 %collective-permute-start.1 = (f32[128,640]{1,0:T(8,128)}, f32[128,640]{1,0:T(8,128)}, u32[]{:S(2)}, u32[]{:S(2)}) collective-permute-start(f32[128,640]{1,0:T(8,128)} %get-tuple-element.30), channel_id=1, source_target_pairs={{0,4},{1,5},{2,6},{3,7},{4,0},{5,1},{6,2},{7,3},{8,12},{9,13},{10,... | collective-permute-start | bytes 983048 | tf_op jit(solution)/shard_map/ppermute | solution.py:317
  34.3 3.7 %collective-permute-done.19 = f32[128,640]{1,0:T(8,128)S(1)} collective-permute-done((f32[128,640]{1,0:T(8,128)S(1)}, f32[128,640]{1,0:T(8,128)S(1)}, u32[]{:S(2)}, u32[]{:S(2)}) %collective-permute-start.19) | collective-permute-done | bytes 327712 | tf_op jit(solution)/shard_map/ppermute | solution.py:317
  38.1 1.8 %collective-permute-start.17 = (f32[128,640]{1,0:T(8,128)S(1)}, f32[128,640]{1,0:T(8,128)}, u32[]{:S(2)}, u32[]{:S(2)}) collective-permute-start(f32[128,640]{1,0:T(8,128)S(1)} %get-tuple-element.28), channel_id=1, source_target_pairs={{0,4},{1,5},{2,6},{3,7},{4,0},{5,1},{6,2},{7,3},{8,12},{9,13},{10,... | collective-permute-start | bytes 983048 | tf_op jit(solution)/shard_map/ppermute | solution.py:317
  39.9 3.3 %items.1 = f32[32,72,128]{2,1,0:T(8,128)} custom-call(s32[1,512]{1,0:T(1,128)S(1)} %bitcast.3, bf16[512,512]{1,0:T(8,128)(2,1)S(1)} %copy-done.3, bf16[512,2048]{1,0:T(8,128)(2,1)S(1)} %get-tuple-element.15.grad_pre, bf16[512,2048]{1,0:T(8,128)(2,1)S(1)} %copy-done.1), custom_call_target="tpu_custom_call" | custom-call | tf_op jit(solution)/shard_map/items/pallas_call | solution.py:237
  43.2 4.9 %all-to-all-start = ((f32[32,72,128]{2,1,0:T(8,128)}), f32[32,72,128]{2,1,0:T(8,128)S(1)}, u32[]{:S(2)}, u32[]{:S(2)}) async-start(f32[32,72,128]{2,1,0:T(8,128)} %items.1), calls=%async_computation | async-start | bytes 2359296 | tf_op jit(solution)/shard_map/all_to_all | solution.py:381
  48.2 1.8 %collective-permute-start.4 = (f32[64,640]{1,0:T(8,128)S(1)}, f32[64,640]{1,0:T(8,128)S(1)}, u32[]{:S(2)}, u32[]{:S(2)}) collective-permute-start(f32[64,640]{1,0:T(8,128)S(1)} %slice.83), channel_id=1, source_target_pairs={{0,4},{1,5},{2,6},{3,7},{4,0},{5,1},{6,2},{7,3},{8,12},{9,13},{10,... | collective-permute-start | bytes 491528 | tf_op jit(solution)/shard_map/ppermute | solution.py:317
  50.0 0.3 collective-permute-start.20
  50.4 1.0 slice_add_fusion.3
  51.4 1.8 %collective-permute-start.2 = (f32[64,640]{1,0:T(8,128)S(1)}, f32[64,640]{1,0:T(8,128)S(1)}, u32[]{:S(2)}, u32[]{:S(2)}) collective-permute-start(f32[64,640]{1,0:T(8,128)S(1)} %slice.79), channel_id=1, source_target_pairs={{0,2},{1,3},{2,0},{3,1},{4,6},{5,7},{6,4},{7,5},{8,10},{9,11},{10,... | collective-permute-start | bytes 491528 | tf_op jit(solution)/shard_map/ppermute | solution.py:317
  53.2 1.1 slice_add_fusion.1
  54.3 0.3 collective-permute-start.18
  54.7 9.2 %collective-permute-done.4 = f32[64,640]{1,0:T(8,128)S(1)} collective-permute-done((f32[64,640]{1,0:T(8,128)S(1)}, f32[64,640]{1,0:T(8,128)S(1)}, u32[]{:S(2)}, u32[]{:S(2)}) %collective-permute-start.4) | collective-permute-done | bytes 163872 | tf_op jit(solution)/shard_map/ppermute | solution.py:317
  63.8 1.0 collective-permute-done.2
  65.0 3.6 %collective-permute-done.20 = f32[64,640]{1,0:T(8,128)S(1)} collective-permute-done((f32[64,640]{1,0:T(8,128)S(1)}, f32[64,640]{1,0:T(8,128)S(1)}, u32[]{:S(2)}, u32[]{:S(2)}) %collective-permute-start.20) | collective-permute-done | bytes 163872 | tf_op jit(solution)/shard_map/ppermute | solution.py:317
  68.6 0.5 collective-permute-done.18
  69.1 1.5 %collective-permute-start.21 = (f32[64,640]{1,0:T(8,128)S(1)}, f32[64,640]{1,0:T(8,128)S(1)}, u32[]{:S(2)}, u32[]{:S(2)}) collective-permute-start(f32[64,640]{1,0:T(8,128)S(1)} %broadcast_select_fusion.2), channel_id=1, source_target_pairs={{0,8},{8,0},{16,24},{24,16},{1,9},{9,1},{17,25},{25,17},{2,10},{10... | collective-permute-start | bytes 491528 | tf_op jit(solution)/shard_map/ppermute | solution.py:317
  70.7 2.2 %collective-permute-done.5 = f32[64,640]{1,0:T(8,128)S(1)} collective-permute-done((f32[64,640]{1,0:T(8,128)S(1)}, f32[64,640]{1,0:T(8,128)S(1)}, u32[]{:S(2)}, u32[]{:S(2)}) %collective-permute-start.5) | collective-permute-done | bytes 163872 | tf_op jit(solution)/shard_map/ppermute | solution.py:317
  72.9 3.6 %collective-permute-start.6 = (f32[64,640]{1,0:T(8,128)S(1)}, f32[64,640]{1,0:T(8,128)S(1)}, u32[]{:S(2)}, u32[]{:S(2)}) collective-permute-start(f32[64,640]{1,0:T(8,128)S(1)} %select_add_fusion.1), channel_id=1, source_target_pairs={{0,16},{8,24},{16,0},{24,8},{1,17},{9,25},{17,1},{25,9},{2,18},{10... | collective-permute-start | bytes 491528 | tf_op jit(solution)/shard_map/ppermute | solution.py:317
  76.5 3.7 %collective-permute-done.21 = f32[64,640]{1,0:T(8,128)S(1)} collective-permute-done((f32[64,640]{1,0:T(8,128)S(1)}, f32[64,640]{1,0:T(8,128)S(1)}, u32[]{:S(2)}, u32[]{:S(2)}) %collective-permute-start.21) | collective-permute-done | bytes 163872 | tf_op jit(solution)/shard_map/ppermute | solution.py:317
  80.3 0.4 collective-permute-start.22
  80.6 8.0 %collective-permute-done.6 = f32[64,640]{1,0:T(8,128)S(1)} collective-permute-done((f32[64,640]{1,0:T(8,128)S(1)}, f32[64,640]{1,0:T(8,128)S(1)}, u32[]{:S(2)}, u32[]{:S(2)}) %collective-permute-start.6) | collective-permute-done | bytes 163872 | tf_op jit(solution)/shard_map/ppermute | solution.py:317
  88.7 2.7 %collective-permute-done.22 = f32[64,640]{1,0:T(8,128)S(1)} collective-permute-done((f32[64,640]{1,0:T(8,128)S(1)}, f32[64,640]{1,0:T(8,128)S(1)}, u32[]{:S(2)}, u32[]{:S(2)}) %collective-permute-start.22) | collective-permute-done | bytes 163872 | tf_op jit(solution)/shard_map/ppermute | solution.py:317
  91.5 4.3 %collective-permute-done.7 = f32[64,640]{1,0:T(8,128)S(1)} collective-permute-done((f32[64,640]{1,0:T(8,128)S(1)}, f32[64,640]{1,0:T(8,128)S(1)}, u32[]{:S(2)}, u32[]{:S(2)}) %collective-permute-start.7) | collective-permute-done | bytes 163872 | tf_op jit(solution)/shard_map/ppermute | solution.py:317
  95.9 1.6 %collective-permute-start.8 = (f32[64,640]{1,0:T(8,128)S(1)}, f32[64,640]{1,0:T(8,128)S(1)}, u32[]{:S(2)}, u32[]{:S(2)}) collective-permute-start(f32[64,640]{1,0:T(8,128)S(1)} %get-tuple-element.34), channel_id=1, source_target_pairs={{0,4},{1,5},{2,6},{3,7},{4,0},{5,1},{6,2},{7,3},{8,12},{9,13},{10,... | collective-permute-start | bytes 491528 | tf_op jit(solution)/shard_map/ppermute | solution.py:317
  97.4 0.9 collective-permute-done.23
  98.4 1.5 %collective-permute-start.24 = (f32[64,640]{1,0:T(8,128)S(1)}, f32[64,640]{1,0:T(8,128)S(1)}, u32[]{:S(2)}, u32[]{:S(2)}) collective-permute-start(f32[64,640]{1,0:T(8,128)S(1)} %get-tuple-element.32), channel_id=1, source_target_pairs={{0,4},{1,5},{2,6},{3,7},{4,0},{5,1},{6,2},{7,3},{8,12},{9,13},{10,... | collective-permute-start | bytes 491528 | tf_op jit(solution)/shard_map/ppermute | solution.py:317
  99.9 1.5 %collective-permute-start.12 = (f32[64,640]{1,0:T(8,128)S(1)}, f32[64,640]{1,0:T(8,128)S(1)}, u32[]{:S(2)}, u32[]{:S(2)}) collective-permute-start(f32[64,640]{1,0:T(8,128)S(1)} %get-tuple-element.33), channel_id=1, source_target_pairs={{0,2},{1,3},{2,0},{3,1},{4,6},{5,7},{6,4},{7,5},{8,10},{9,11},{10,... | collective-permute-start | bytes 491528 | tf_op jit(solution)/shard_map/ppermute | solution.py:317
  101.3 1.1 collective-permute-done.8
  102.5 2.2 %collective-permute-start.9 = (f32[128,640]{1,0:T(8,128)S(1)}, f32[128,640]{1,0:T(8,128)S(1)}, u32[]{:S(2)}, u32[]{:S(2)}) collective-permute-start(f32[128,640]{1,0:T(8,128)S(1)} %pad_maximum_fusion.refs_0_), channel_id=1, source_target_pairs={{0,2},{1,3},{2,0},{3,1},{4,6},{5,7},{6,4},{7,5},{8,10},{9,11},{10,... | collective-permute-start | bytes 983048 | tf_op jit(solution)/shard_map/ppermute | solution.py:317
  104.8 1.8 %collective-permute-start.25 = (f32[128,640]{1,0:T(8,128)S(1)}, f32[128,640]{1,0:T(8,128)S(1)}, u32[]{:S(2)}, u32[]{:S(2)}) collective-permute-start(f32[128,640]{1,0:T(8,128)S(1)} %pad_maximum_fusion.2.refs_0_), channel_id=1, source_target_pairs={{0,2},{1,3},{2,0},{3,1},{4,6},{5,7},{6,4},{7,5},{8,10},{9,11},{10,... | collective-permute-start | bytes 983048 | tf_op jit(solution)/shard_map/ppermute | solution.py:317
  106.6 0.3 collective-permute-start.28
  106.9 0.1 collective-permute-done.12
  107.0 1.4 %collective-permute-start.13 = (f32[128,640]{1,0:T(8,128)S(1)}, f32[128,640]{1,0:T(8,128)S(1)}, u32[]{:S(2)}, u32[]{:S(2)}) collective-permute-start(f32[128,640]{1,0:T(8,128)S(1)} %pad_maximum_fusion.1.refs_4_), channel_id=1, source_target_pairs={{0,4},{1,5},{2,6},{3,7},{4,0},{5,1},{6,2},{7,3},{8,12},{9,13},{10,... | collective-permute-start | bytes 983048 | tf_op jit(solution)/shard_map/ppermute | solution.py:317
  108.5 13.8 %collective-permute-done.28 = f32[64,640]{1,0:T(8,128)S(1)} collective-permute-done((f32[64,640]{1,0:T(8,128)S(1)}, f32[64,640]{1,0:T(8,128)S(1)}, u32[]{:S(2)}, u32[]{:S(2)}) %collective-permute-start.28) | collective-permute-done | bytes 163872 | tf_op jit(solution)/shard_map/ppermute | solution.py:317
  122.3 0.7 collective-permute-start.29
  123.0 0.5 collective-permute-start.30
  123.6 0.7 copy-done.6
  124.3 0.4 collective-permute-start.10
  124.8 5.2 %collective-permute-done.29.refs_5_ = f32[128,640]{1,0:T(8,128)} collective-permute-done((f32[128,640]{1,0:T(8,128)S(1)}, f32[128,640]{1,0:T(8,128)}, u32[]{:S(2)}, u32[]{:S(2)}) %collective-permute-start.29) | collective-permute-done | bytes 327712 | tf_op jit(solution)/shard_map/ppermute | solution.py:317
  129.9 0.7 copy-done.8
  130.7 0.5 collective-permute-start.14
  131.2 0.7 copy-done.10
  131.9 0.7 copy-done.12
  132.6 0.5 collective-permute-start.15
  133.2 2.8 %table.1 = f32[1024,512]{1,0:T(8,128)} custom-call(f32[32,72,128]{2,1,0:T(8,128)S(1)} %all-to-all-done.got), custom_call_target="tpu_custom_call" | custom-call | tf_op jit(solution)/shard_map/table/pallas_call | solution.py:263
  136.0 2.8 %place.2 = (f32[512,2048]{1,0:T(8,128)}, f32[512,512]{1,0:T(8,128)}) custom-call(s32[2]{0:T(128)S(1)} %pad_add_fusion.place, f32[128,640]{1,0:T(8,128)S(1)} %pad_maximum_fusion.2.refs_0_, f32[128,640]{1,0:T(8,128)S(1)} %copy-done.7, f32[128,640]{1,0:T(8,128)S(1)} %copy-done.9, f32[128,640]{1,0:T(8,128)S(1)} %copy-done.13, ...), custom_call_target="tpu_custom_call" | custom-call | tf_op jit(solution)/shard_map/place/pallas_call | solution.py:300
  138.8 2.9 %place.3 = (f32[512,2048]{1,0:T(8,128)}, f32[512,512]{1,0:T(8,128)}) custom-call(s32[2]{0:T(128)S(1)} %pad_add_fusion.place, f32[128,640]{1,0:T(8,128)S(1)} %pad_maximum_fusion.refs_0_, f32[128,640]{1,0:T(8,128)S(1)} %collective-permute-done.9.refs_1_, ...), custom_call_target="tpu_custom_call", output_to_operand_aliasing={{0}: (9, {}), {1}: (10, {})} | custom-call | tf_op jit(solution)/shard_map/place/pallas_call | solution.py:300
  (67 shorter events, 0.9 us)
Async XLA Ops:
  0.8 1.6 %copy-start = (bf16[512,2048]{1,0:T(8,128)(2,1)S(1)}, bf16[512,2048]{1,0:T(8,128)(2,1)}, u32[]{:S(2)}) copy-start(bf16[512,2048]{1,0:T(8,128)(2,1)} %in_proj.1) | copy-start | bytes 6291460
  2.4 1.0 copy-start.2
  3.4 1.0 copy-start.4
  4.4 1.0 copy-start.5
  5.5 0.7 copy-start.15
  16.7 3.2 %collective-permute-start = (f32[512,640]{1,0:T(8,128)S(1)}, f32[512,640]{1,0:T(8,128)S(1)}, u32[]{:S(2)}, u32[]{:S(2)}) collective-permute-start(f32[512,640]{1,0:T(8,128)S(1)} %get-tuple-element.20), channel_id=1, source_target_pairs={{0,1},{1,0},{2,3},{3,2},{4,5},{5,4},{6,7},{7,6},{8,9},{9,8},{10,11... | collective-permute-start | bytes 3932168 | tf_op jit(solution)/shard_map/ppermute | solution.py:317
  17.2 5.8 %collective-permute-start.16 = (f32[512,640]{1,0:T(8,128)S(1)}, f32[512,640]{1,0:T(8,128)S(1)}, u32[]{:S(2)}, u32[]{:S(2)}) collective-permute-start(f32[512,640]{1,0:T(8,128)S(1)} %get-tuple-element.22), channel_id=1, source_target_pairs={{0,1},{1,0},{2,3},{3,2},{4,5},{5,4},{6,7},{7,6},{8,9},{9,8},{10,11... | collective-permute-start | bytes 3932168 | tf_op jit(solution)/shard_map/ppermute | solution.py:317
  20.1 11.4 %collective-permute-start.3 = (f32[128,640]{1,0:T(8,128)S(1)}, f32[128,640]{1,0:T(8,128)S(1)}, u32[]{:S(2)}, u32[]{:S(2)}) collective-permute-start(f32[128,640]{1,0:T(8,128)S(1)} %slice.81), channel_id=1, source_target_pairs={{0,2},{1,3},{2,0},{3,1},{4,6},{5,7},{6,4},{7,5},{8,10},{9,11},{10,... | collective-permute-start | bytes 983048 | tf_op jit(solution)/shard_map/ppermute | solution.py:317
  23.1 15.0 %copy-start.16 = (f32[512,640]{1,0:T(8,128)}, f32[512,640]{1,0:T(8,128)S(1)}, u32[]{:S(2)}) copy-start(f32[512,640]{1,0:T(8,128)S(1)} %add.89) | copy-start | bytes 3932164
  23.2 16.8 %copy-start.1 = (bf16[512,2048]{1,0:T(8,128)(2,1)S(1)}, bf16[512,2048]{1,0:T(8,128)(2,1)}, u32[]{:S(2)}) copy-start(bf16[512,2048]{1,0:T(8,128)(2,1)} %in_proj.1) | copy-start | bytes 6291460
  23.2 16.7 %copy-start.3 = (bf16[512,512]{1,0:T(8,128)(2,1)S(1)}, bf16[512,512]{1,0:T(8,128)(2,1)}, u32[]{:S(2)}) copy-start(bf16[512,512]{1,0:T(8,128)(2,1)} %cot.3) | copy-start | bytes 1572868
  23.2 16.7 %copy-start.14 = (s32[512]{0:T(512)S(1)}, s32[512]{0:T(512)}, u32[]{:S(2)}) copy-start(s32[512]{0:T(512)} %param.11) | copy-start | bytes 6148
  23.2 14.8 %collective-permute-start.19 = (f32[128,640]{1,0:T(8,128)S(1)}, f32[128,640]{1,0:T(8,128)S(1)}, u32[]{:S(2)}, u32[]{:S(2)}) collective-permute-start(f32[128,640]{1,0:T(8,128)S(1)} %slice.89), channel_id=1, source_target_pairs={{0,2},{1,3},{2,0},{3,1},{4,6},{5,7},{6,4},{7,5},{8,10},{9,11},{10,... | collective-permute-start | bytes 983048 | tf_op jit(solution)/shard_map/ppermute | solution.py:317
  32.3 18.1 %collective-permute-start.1 = (f32[128,640]{1,0:T(8,128)}, f32[128,640]{1,0:T(8,128)}, u32[]{:S(2)}, u32[]{:S(2)}) collective-permute-start(f32[128,640]{1,0:T(8,128)} %get-tuple-element.30), channel_id=1, source_target_pairs={{0,4},{1,5},{2,6},{3,7},{4,0},{5,1},{6,2},{7,3},{8,12},{9,13},{10,... | collective-permute-start | bytes 983048 | tf_op jit(solution)/shard_map/ppermute | solution.py:317
  38.1 15.1 %collective-permute-start.17 = (f32[128,640]{1,0:T(8,128)S(1)}, f32[128,640]{1,0:T(8,128)}, u32[]{:S(2)}, u32[]{:S(2)}) collective-permute-start(f32[128,640]{1,0:T(8,128)S(1)} %get-tuple-element.28), channel_id=1, source_target_pairs={{0,4},{1,5},{2,6},{3,7},{4,0},{5,1},{6,2},{7,3},{8,12},{9,13},{10,... | collective-permute-start | bytes 983048 | tf_op jit(solution)/shard_map/ppermute | solution.py:317
  43.2 89.9 %all-to-all-start = ((f32[32,72,128]{2,1,0:T(8,128)}), f32[32,72,128]{2,1,0:T(8,128)S(1)}, u32[]{:S(2)}, u32[]{:S(2)}) async-start(f32[32,72,128]{2,1,0:T(8,128)} %items.1), calls=%async_computation | async-start | bytes 2359296 | tf_op jit(solution)/shard_map/all_to_all | solution.py:381
  48.2 15.7 %collective-permute-start.4 = (f32[64,640]{1,0:T(8,128)S(1)}, f32[64,640]{1,0:T(8,128)S(1)}, u32[]{:S(2)}, u32[]{:S(2)}) collective-permute-start(f32[64,640]{1,0:T(8,128)S(1)} %slice.83), channel_id=1, source_target_pairs={{0,4},{1,5},{2,6},{3,7},{4,0},{5,1},{6,2},{7,3},{8,12},{9,13},{10,... | collective-permute-start | bytes 491528 | tf_op jit(solution)/shard_map/ppermute | solution.py:317
  50.0 18.6 %collective-permute-start.20 = (f32[64,640]{1,0:T(8,128)S(1)}, f32[64,640]{1,0:T(8,128)S(1)}, u32[]{:S(2)}, u32[]{:S(2)}) collective-permute-start(f32[64,640]{1,0:T(8,128)S(1)} %slice.91), channel_id=1, source_target_pairs={{0,4},{1,5},{2,6},{3,7},{4,0},{5,1},{6,2},{7,3},{8,12},{9,13},{10,... | collective-permute-start | bytes 491528 | tf_op jit(solution)/shard_map/ppermute | solution.py:317
  51.4 13.5 %collective-permute-start.2 = (f32[64,640]{1,0:T(8,128)S(1)}, f32[64,640]{1,0:T(8,128)S(1)}, u32[]{:S(2)}, u32[]{:S(2)}) collective-permute-start(f32[64,640]{1,0:T(8,128)S(1)} %slice.79), channel_id=1, source_target_pairs={{0,2},{1,3},{2,0},{3,1},{4,6},{5,7},{6,4},{7,5},{8,10},{9,11},{10,... | collective-permute-start | bytes 491528 | tf_op jit(solution)/shard_map/ppermute | solution.py:317
  54.3 14.7 %collective-permute-start.18 = (f32[64,640]{1,0:T(8,128)S(1)}, f32[64,640]{1,0:T(8,128)S(1)}, u32[]{:S(2)}, u32[]{:S(2)}) collective-permute-start(f32[64,640]{1,0:T(8,128)S(1)} %slice.87), channel_id=1, source_target_pairs={{0,2},{1,3},{2,0},{3,1},{4,6},{5,7},{6,4},{7,5},{8,10},{9,11},{10,... | collective-permute-start | bytes 491528 | tf_op jit(solution)/shard_map/ppermute | solution.py:317
  64.9 7.9 %collective-permute-start.5 = (f32[64,640]{1,0:T(8,128)S(1)}, f32[64,640]{1,0:T(8,128)S(1)}, u32[]{:S(2)}, u32[]{:S(2)}) collective-permute-start(f32[64,640]{1,0:T(8,128)S(1)} %broadcast_select_fusion.5), channel_id=1, source_target_pairs={{0,8},{8,0},{16,24},{24,16},{1,9},{9,1},{17,25},{25,17},{2,10},{10... | collective-permute-start | bytes 491528 | tf_op jit(solution)/shard_map/ppermute | solution.py:317
  69.1 11.1 %collective-permute-start.21 = (f32[64,640]{1,0:T(8,128)S(1)}, f32[64,640]{1,0:T(8,128)S(1)}, u32[]{:S(2)}, u32[]{:S(2)}) collective-permute-start(f32[64,640]{1,0:T(8,128)S(1)} %broadcast_select_fusion.2), channel_id=1, source_target_pairs={{0,8},{8,0},{16,24},{24,16},{1,9},{9,1},{17,25},{25,17},{2,10},{10... | collective-permute-start | bytes 491528 | tf_op jit(solution)/shard_map/ppermute | solution.py:317
  72.9 15.7 %collective-permute-start.6 = (f32[64,640]{1,0:T(8,128)S(1)}, f32[64,640]{1,0:T(8,128)S(1)}, u32[]{:S(2)}, u32[]{:S(2)}) collective-permute-start(f32[64,640]{1,0:T(8,128)S(1)} %select_add_fusion.1), channel_id=1, source_target_pairs={{0,16},{8,24},{16,0},{24,8},{1,17},{9,25},{17,1},{25,9},{2,18},{10... | collective-permute-start | bytes 491528 | tf_op jit(solution)/shard_map/ppermute | solution.py:317
  80.3 11.1 %collective-permute-start.22 = (f32[64,640]{1,0:T(8,128)S(1)}, f32[64,640]{1,0:T(8,128)S(1)}, u32[]{:S(2)}, u32[]{:S(2)}) collective-permute-start(f32[64,640]{1,0:T(8,128)S(1)} %select_add_fusion), channel_id=1, source_target_pairs={{0,16},{8,24},{16,0},{24,8},{1,17},{9,25},{17,1},{25,9},{2,18},{10... | collective-permute-start | bytes 491528 | tf_op jit(solution)/shard_map/ppermute | solution.py:317
  88.6 7.2 %collective-permute-start.7 = (f32[64,640]{1,0:T(8,128)S(1)}, f32[64,640]{1,0:T(8,128)S(1)}, u32[]{:S(2)}, u32[]{:S(2)}) collective-permute-start(f32[64,640]{1,0:T(8,128)S(1)} %add_multiply_fusion.1), channel_id=1, source_target_pairs={{0,8},{8,0},{16,24},{24,16},{1,9},{9,1},{17,25},{25,17},{2,10},{10... | collective-permute-start | bytes 491528 | tf_op jit(solution)/shard_map/ppermute | solution.py:317
  91.4 6.9 %collective-permute-start.23 = (f32[64,640]{1,0:T(8,128)S(1)}, f32[64,640]{1,0:T(8,128)S(1)}, u32[]{:S(2)}, u32[]{:S(2)}) collective-permute-start(f32[64,640]{1,0:T(8,128)S(1)} %add_multiply_fusion), channel_id=1, source_target_pairs={{0,8},{8,0},{16,24},{24,16},{1,9},{9,1},{17,25},{25,17},{2,10},{10... | collective-permute-start | bytes 491528 | tf_op jit(solution)/shard_map/ppermute | solution.py:317
  95.9 6.6 %collective-permute-start.8 = (f32[64,640]{1,0:T(8,128)S(1)}, f32[64,640]{1,0:T(8,128)S(1)}, u32[]{:S(2)}, u32[]{:S(2)}) collective-permute-start(f32[64,640]{1,0:T(8,128)S(1)} %get-tuple-element.34), channel_id=1, source_target_pairs={{0,4},{1,5},{2,6},{3,7},{4,0},{5,1},{6,2},{7,3},{8,12},{9,13},{10,... | collective-permute-start | bytes 491528 | tf_op jit(solution)/shard_map/ppermute | solution.py:317
  98.4 6.4 %collective-permute-start.24 = (f32[64,640]{1,0:T(8,128)S(1)}, f32[64,640]{1,0:T(8,128)S(1)}, u32[]{:S(2)}, u32[]{:S(2)}) collective-permute-start(f32[64,640]{1,0:T(8,128)S(1)} %get-tuple-element.32), channel_id=1, source_target_pairs={{0,4},{1,5},{2,6},{3,7},{4,0},{5,1},{6,2},{7,3},{8,12},{9,13},{10,... | collective-permute-start | bytes 491528 | tf_op jit(solution)/shard_map/ppermute | solution.py:317
  99.9 7.1 %collective-permute-start.12 = (f32[64,640]{1,0:T(8,128)S(1)}, f32[64,640]{1,0:T(8,128)S(1)}, u32[]{:S(2)}, u32[]{:S(2)}) collective-permute-start(f32[64,640]{1,0:T(8,128)S(1)} %get-tuple-element.33), channel_id=1, source_target_pairs={{0,2},{1,3},{2,0},{3,1},{4,6},{5,7},{6,4},{7,5},{8,10},{9,11},{10,... | collective-permute-start | bytes 491528 | tf_op jit(solution)/shard_map/ppermute | solution.py:317
  102.5 20.5 %collective-permute-start.9 = (f32[128,640]{1,0:T(8,128)S(1)}, f32[128,640]{1,0:T(8,128)S(1)}, u32[]{:S(2)}, u32[]{:S(2)}) collective-permute-start(f32[128,640]{1,0:T(8,128)S(1)} %pad_maximum_fusion.refs_0_), channel_id=1, source_target_pairs={{0,2},{1,3},{2,0},{3,1},{4,6},{5,7},{6,4},{7,5},{8,10},{9,11},{10,... | collective-permute-start | bytes 983048 | tf_op jit(solution)/shard_map/ppermute | solution.py:317
  104.8 18.7 %collective-permute-start.25 = (f32[128,640]{1,0:T(8,128)S(1)}, f32[128,640]{1,0:T(8,128)S(1)}, u32[]{:S(2)}, u32[]{:S(2)}) collective-permute-start(f32[128,640]{1,0:T(8,128)S(1)} %pad_maximum_fusion.2.refs_0_), channel_id=1, source_target_pairs={{0,2},{1,3},{2,0},{3,1},{4,6},{5,7},{6,4},{7,5},{8,10},{9,11},{10,... | collective-permute-start | bytes 983048 | tf_op jit(solution)/shard_map/ppermute | solution.py:317
  106.6 15.7 %collective-permute-start.28 = (f32[64,640]{1,0:T(8,128)S(1)}, f32[64,640]{1,0:T(8,128)S(1)}, u32[]{:S(2)}, u32[]{:S(2)}) collective-permute-start(f32[64,640]{1,0:T(8,128)S(1)} %get-tuple-element.31), channel_id=1, source_target_pairs={{0,2},{1,3},{2,0},{3,1},{4,6},{5,7},{6,4},{7,5},{8,10},{9,11},{10,... | collective-permute-start | bytes 491528 | tf_op jit(solution)/shard_map/ppermute | solution.py:317
  107.0 17.3 %collective-permute-start.13 = (f32[128,640]{1,0:T(8,128)S(1)}, f32[128,640]{1,0:T(8,128)S(1)}, u32[]{:S(2)}, u32[]{:S(2)}) collective-permute-start(f32[128,640]{1,0:T(8,128)S(1)} %pad_maximum_fusion.1.refs_4_), channel_id=1, source_target_pairs={{0,4},{1,5},{2,6},{3,7},{4,0},{5,1},{6,2},{7,3},{8,12},{9,13},{10,... | collective-permute-start | bytes 983048 | tf_op jit(solution)/shard_map/ppermute | solution.py:317
  122.3 7.6 %collective-permute-start.29 = (f32[128,640]{1,0:T(8,128)S(1)}, f32[128,640]{1,0:T(8,128)}, u32[]{:S(2)}, u32[]{:S(2)}) collective-permute-start(f32[128,640]{1,0:T(8,128)S(1)} %pad_maximum_fusion.3.refs_4_), channel_id=1, source_target_pairs={{0,4},{1,5},{2,6},{3,7},{4,0},{5,1},{6,2},{7,3},{8,12},{9,13},{10,... | collective-permute-start | bytes 983048 | tf_op jit(solution)/shard_map/ppermute | solution.py:317
  123.0 6.9 %collective-permute-start.26 = (f32[128,640]{1,0:T(8,128)S(1)}, f32[128,640]{1,0:T(8,128)S(1)}, u32[]{:S(2)}, u32[]{:S(2)}) collective-permute-start(f32[128,640]{1,0:T(8,128)S(1)} %pad_maximum_fusion.2.refs_0_), channel_id=1, source_target_pairs={{0,1},{1,0},{2,3},{3,2},{4,5},{5,4},{6,7},{7,6},{8,9},{9,8},{10,11... | collective-permute-start | bytes 983048 | tf_op jit(solution)/shard_map/ppermute | solution.py:317
  123.0 8.1 %collective-permute-start.30 = (f32[128,640]{1,0:T(8,128)S(1)}, f32[128,640]{1,0:T(8,128)S(1)}, u32[]{:S(2)}, u32[]{:S(2)}) collective-permute-start(f32[128,640]{1,0:T(8,128)S(1)} %pad_maximum_fusion.3.refs_4_), channel_id=1, source_target_pairs={{0,1},{1,0},{2,3},{3,2},{4,5},{5,4},{6,7},{7,6},{8,9},{9,8},{10,11... | collective-permute-start | bytes 983048 | tf_op jit(solution)/shard_map/ppermute | solution.py:317
  123.5 8.4 %collective-permute-start.27 = (f32[128,640]{1,0:T(8,128)S(1)}, f32[128,640]{1,0:T(8,128)S(1)}, u32[]{:S(2)}, u32[]{:S(2)}) collective-permute-start(f32[128,640]{1,0:T(8,128)S(1)} %collective-permute-done.25.refs_1_), channel_id=1, source_target_pairs={{0,1},{1,0},{2,3},{3,2},{4,5},{5,4},{6,7},{7,6},{8,9},{9,8},{10,11... | collective-permute-start | bytes 983048 | tf_op jit(solution)/shard_map/ppermute | solution.py:317
  123.6 0.7 copy-start.6
  124.3 14.4 %collective-permute-start.10 = (f32[128,640]{1,0:T(8,128)S(1)}, f32[128,640]{1,0:T(8,128)S(1)}, u32[]{:S(2)}, u32[]{:S(2)}) collective-permute-start(f32[128,640]{1,0:T(8,128)S(1)} %pad_maximum_fusion.refs_0_), channel_id=1, source_target_pairs={{0,1},{1,0},{2,3},{3,2},{4,5},{5,4},{6,7},{7,6},{8,9},{9,8},{10,11... | collective-permute-start | bytes 983048 | tf_op jit(solution)/shard_map/ppermute | solution.py:317
  129.9 6.0 %collective-permute-start.31 = (f32[128,640]{1,0:T(8,128)}, f32[128,640]{1,0:T(8,128)}, u32[]{:S(2)}, u32[]{:S(2)}) collective-permute-start(f32[128,640]{1,0:T(8,128)} %collective-permute-done.29.refs_5_), channel_id=1, source_target_pairs={{0,1},{1,0},{2,3},{3,2},{4,5},{5,4},{6,7},{7,6},{8,9},{9,8},{10,11... | collective-permute-start | bytes 983048 | tf_op jit(solution)/shard_map/ppermute | solution.py:317
  129.9 0.7 copy-start.8
  130.7 8.1 %collective-permute-start.14 = (f32[128,640]{1,0:T(8,128)S(1)}, f32[128,640]{1,0:T(8,128)}, u32[]{:S(2)}, u32[]{:S(2)}) collective-permute-start(f32[128,640]{1,0:T(8,128)S(1)} %pad_maximum_fusion.1.refs_4_), channel_id=1, source_target_pairs={{0,1},{1,0},{2,3},{3,2},{4,5},{5,4},{6,7},{7,6},{8,9},{9,8},{10,11... | collective-permute-start | bytes 983048 | tf_op jit(solution)/shard_map/ppermute | solution.py:317
  131.2 0.7 copy-start.10
  131.9 6.9 %collective-permute-start.11 = (f32[128,640]{1,0:T(8,128)S(1)}, f32[128,640]{1,0:T(8,128)}, u32[]{:S(2)}, u32[]{:S(2)}) collective-permute-start(f32[128,640]{1,0:T(8,128)S(1)} %collective-permute-done.9.refs_1_), channel_id=1, source_target_pairs={{0,1},{1,0},{2,3},{3,2},{4,5},{5,4},{6,7},{7,6},{8,9},{9,8},{10,11... | collective-permute-start | bytes 983048 | tf_op jit(solution)/shard_map/ppermute | solution.py:317
  131.9 0.7 copy-start.12
  132.6 6.1 %collective-permute-start.15 = (f32[128,640]{1,0:T(8,128)S(1)}, f32[128,640]{1,0:T(8,128)}, u32[]{:S(2)}, u32[]{:S(2)}) collective-permute-start(f32[128,640]{1,0:T(8,128)S(1)} %collective-permute-done.13.refs_5_), channel_id=1, source_target_pairs={{0,1},{1,0},{2,3},{3,2},{4,5},{5,4},{6,7},{7,6},{8,9},{9,8},{10,11... | collective-permute-start | bytes 983048 | tf_op jit(solution)/shard_map/ppermute | solution.py:317
  133.1 2.8 %copy-start.7 = (f32[128,640]{1,0:T(8,128)S(1)}, f32[128,640]{1,0:T(8,128)}, u32[]{:S(2)}) copy-start(f32[128,640]{1,0:T(8,128)} %copy-done.6) | copy-start | bytes 983044
  133.1 2.8 %copy-start.9 = (f32[128,640]{1,0:T(8,128)S(1)}, f32[128,640]{1,0:T(8,128)}, u32[]{:S(2)}) copy-start(f32[128,640]{1,0:T(8,128)} %copy-done.8) | copy-start | bytes 983044
  133.1 2.8 %copy-start.11 = (f32[128,640]{1,0:T(8,128)S(1)}, f32[128,640]{1,0:T(8,128)}, u32[]{:S(2)}) copy-start(f32[128,640]{1,0:T(8,128)} %copy-done.10) | copy-start | bytes 983044
  133.1 2.8 %copy-start.13 = (f32[128,640]{1,0:T(8,128)S(1)}, f32[128,640]{1,0:T(8,128)}, u32[]{:S(2)}) copy-start(f32[128,640]{1,0:T(8,128)} %copy-done.12) | copy-start | bytes 983044

commit v3 on v2

--- a/solution.py
+++ b/solution.py
@@ -169,7 +169,7 @@
             pltpu.SemaphoreType.DMA((7,)),
         ],
         compiler_params=pltpu.CompilerParams(vmem_limit_bytes=40 << 20),
-    )(place, lengths, emb, cot, in_proj, out_proj)
+    )(place, lengths, *(pltpu.with_memory_space_constraint(x, HBM) for x in (emb, cot, in_proj, out_proj)))
 
 
 def second_kernel(rel_a, rel_b, rel_g, cot, grad_pre, keep, send):
@@ -240,7 +240,7 @@
         out_shape=jax.ShapeDtypeStruct((owners, (width // 128) * slots + 8, 128), jnp.float32),
         in_specs=[vmem] * 4,
         out_specs=vmem,
-        compiler_params=pltpu.CompilerParams(vmem_limit_bytes=40 << 20),
+        compiler_params=pltpu.CompilerParams(vmem_limit_bytes=16 << 20),
     )(ids, cot, grad_pre, in_proj)
 
 
@@ -266,7 +266,7 @@
         out_shape=jax.ShapeDtypeStruct((OWN_ROWS, width), jnp.float32),
         in_specs=[vmem],
         out_specs=vmem,
-        compiler_params=pltpu.CompilerParams(vmem_limit_bytes=40 << 20),
+        compiler_params=pltpu.CompilerParams(vmem_limit_bytes=16 << 20),
     )(got)
 
 
@@ -336,14 +336,31 @@
     return x[:n], x[n:]
 
 
-def reduce_all(keep, send, order_a, order_b, scale):
+def after(x, *others):
+    return lax.optimization_barrier((x, *others))[0]
+
+
+def apart(*xs):
+    return lax.optimization_barrier(xs)
+
+
+def reduce_all(keep, send, order_a, order_b, scale, first=()):
     dp_count = lax.axis_size("dp")
     odd = lax.axis_index("dp") % 2 == 1
-    a, b = halve(keep + swap(send, "table", order_a[0]))
-    for bit_a, bit_b in zip(order_a[1:], order_b[1:]):
-        (a_keep, a_send), (b_keep, b_send) = halve(a), halve(b)
-        a = a_keep + swap(a_send, "table", bit_a)
-        b = b_keep + swap(b_send, "table", bit_b)
+    total = keep + swap(send, "table", order_a[0])
+    n = total.shape[0] // 4
+    a_keep, a_send, b_keep, b_send = apart(*(total[i * n : (i + 1) * n] for i in range(4)))
+    arrived = ()
+    for step, (bit_a, bit_b) in enumerate(zip(order_a[1:], order_b[1:])):
+        if step:
+            (a_keep, a_send), (b_keep, b_send) = halve(a), halve(b)
+            a_keep, a_send = apart(a_keep, a_send)
+            b_keep, b_send = apart(b_keep, b_send)
+        elif first:
+            a_send, b_send = after(a_send, first[0]), after(b_send, first[1])
+        a_got, b_got = swap(a_send, "table", bit_a), swap(b_send, "table", bit_b)
+        arrived = arrived or (a_got, b_got)
+        a, b = a_keep + a_got, b_keep + b_got
     x = jnp.where(odd, b, a) + swap(jnp.where(odd, a, b), "dp", 1)
     distance = 2
     while distance < dp_count:
@@ -353,12 +370,17 @@
     other = swap(x, "dp", 1)
     a, b = jnp.where(odd, other, x), jnp.where(odd, x, other)
     for bit_a, bit_b in zip(order_a[:1:-1], order_b[:1:-1]):
+        a, b = apart(a)[0], apart(b)[0]
         a = jnp.concatenate([a, swap(a, "table", bit_a)], axis=0)
         b = jnp.concatenate([b, swap(b, "table", bit_b)], axis=0)
+    a, b = apart(a)[0], apart(b)[0]
+    return arrived, (a, b), (swap(a, "table", order_a[1]), swap(b, "table", order_b[1]))
+
+
+def both_cores(near, far, bit):
     pieces = []
-    for x, bit in ((a, order_a[1]), (b, order_b[1])):
-        far = swap(x, "table", bit)
-        pieces += [x, far, swap(x, "table", order_a[0]), swap(far, "table", order_a[0])]
+    for a, b in zip(near, far):
+        pieces += [a, b, swap(a, "table", bit), swap(b, "table", bit)]
     return pieces
 
 
@@ -379,11 +401,14 @@
     keep_f, send_f = second_call(*rel, cotangent, grad_pre)
     sent = item_call(owners, slots, item_ids.reshape(1, rows_here), cotangent, grad_pre, in_proj)
     got = lax.all_to_all(sent, ("dp", "table"), split_axis=0, concat_axis=0, tiled=True)
-    pieces_e = reduce_all(keep_e, send_e, order_a, order_b, scale)
-    pieces_f = reduce_all(keep_f, send_f, order_a, order_b, scale)
+    arrived, near_e, far_e = reduce_all(keep_e, send_e, order_a, order_b, scale)
+    _, near_f, far_f = reduce_all(keep_f, send_f, order_a, order_b, scale, arrived)
+    pieces_e = both_cores(near_e, far_e, order_a[0])
     grads = place_call(chunk, 0, place, pieces_e, width, ())
+    emb_grad = table_call(owners, slots, got, width)
+    far_f, grads, emb_grad = lax.optimization_barrier((far_f, grads, emb_grad))
+    pieces_f = both_cores(near_f, far_f, order_a[0])
     in_grad, out_grad = place_call(chunk, 2 * keep_e.shape[1], place, pieces_f, width, grads)
-    emb_grad = table_call(owners, slots, got, width)
     return (emb_grad, in_grad, out_grad)
 
 

time: 142 us -> 120 us (0.85)
  waiting for transfers between devices: 69.2 us -> 54.6 us
  local copies, waits for them, and re-layouts: 8.41 us -> 1.67 us
  other arithmetic: 3.66 us -> 1.89 us
    ppermute x32, waiting for transfers between devices: 69.2 us -> 54.5 us  [swap(): return lax.ppermute(x, axis, [(i, i ^ distance) for i in range(size)])]
    unnamed x34 -> x12, local copies, waits for them, and re-layouts: 8.31 us -> 1.4 us
    add x6, other arithmetic: 3.22 us -> 1.48 us  [the longest x4 1.12 us: reduce_all(): a, b = (a_keep + a_got, b_keep + b_got)]
  transfers between devices with their start and end apart: 33 -> 33, of which waited for: 17 -> 17; matrix products, arithmetic and copies ran while one was open for 3% -> 2% of each run, Pallas kernels for 6% -> 8%
where the time goes in v3:
time: 120 us; the launch traced here: 119 us
  waiting for transfers between devices  54.6 us (46%)
  starting transfers between devices  38 us (32%)
  Pallas kernels  22.1 us (18%)
  other arithmetic  1.89 us (2%)
  local copies, waits for them, and re-layouts  1.67 us (1%)
    ppermute x32, waiting for transfers between devices, swap(): return lax.ppermute(x, axis, [(i, i ^ distance) for i in range(size)])  54.5 us
    ppermute x32, starting transfers between devices, swap(): return lax.ppermute(x, axis, [(i, i ^ distance) for i in range(size)])  33.1 us
    pallas_call x1, Pallas kernels, block_call(): pl.pallas_call(functools.partial(block_kernel, chunk), name='block', out_...  9.87 us
    pallas_call x2, Pallas kernels, place_call(): pl.pallas_call(functools.partial(place_kernel, chunk, column), name='plac...  5.19 us
    all_to_all x1, starting transfers between devices, per_device(): lax.all_to_all(sent, ('dp', 'table'), split_axis=0, concat_axis=0, tiled=...  4.91 us
    pallas_call x1, Pallas kernels, item_call(): pl.pallas_call(functools.partial(item_kernel, owners, slots), name='items...  3.31 us
    pallas_call x1, Pallas kernels, table_call(): pl.pallas_call(functools.partial(table_kernel, owners, slots), name='tabl...  2.77 us
  transfers between devices with their start and end apart: 33, of which 17 were waited for; matrix products, arithmetic and copies ran while one was open for 2% of the time, Pallas kernels for 8%

profile of v3, /device:TPU:0, one launch (start us, length us, event | category | flops | bytes accessed | tf_op | source)
XLA Modules:
  0.0 119.3 jit_solution(2173135379657623666)
XLA Ops:
  0.7 0.1 pad_add_fusion.place
  0.8 0.7 copy-done.5
  1.4 9.9 %block.1 = (f32[512,640]{1,0:T(8,128)S(1)}, f32[512,640]{1,0:T(8,128)S(1)}, bf16[512,2048]{1,0:T(8,128)(2,1)S(1)}, bf16[512,512]{1,0:T(8,128)(2,1)S(1)}, bf16[51...) custom-call(s32[2]{0:T(128)S(1)} %pad_add_fusion.place, s32[1,8]{1,0:T(1,128)S(1)} %copy-done.5, ...), custom_call_target="tpu_custom_call" | custom-call | tf_op jit(solution)/shard_map/block/pallas_call | solution.py:151
  11.3 0.5 collective-permute-start.1
  11.8 1.0 second.1
  12.8 0.1 collective-permute-start
  12.9 1.5 %collective-permute-done.1 = f32[512,640]{1,0:T(8,128)S(1)} collective-permute-done((f32[512,640]{1,0:T(8,128)S(1)}, f32[512,640]{1,0:T(8,128)S(1)}, u32[]{:S(2)}, u32[]{:S(2)}) %collective-permute-start.1) | collective-permute-done | bytes 1310752 | tf_op jit(solution)/shard_map/ppermute | solution.py:317
  14.5 0.2 add.83
  14.7 0.1 fusion
  14.8 3.0 %collective-permute-start.2 = (f32[128,640]{1,0:T(8,128)S(1)}, f32[128,640]{1,0:T(8,128)S(1)}, u32[]{:S(2)}, u32[]{:S(2)}) collective-permute-start(f32[128,640]{1,0:T(8,128)S(1)} %get-tuple-element.48), channel_id=1, source_target_pairs={{0,4},{1,5},{2,6},{3,7},{4,0},{5,1},{6,2},{7,3},{8,12},{9,13},{10,... | collective-permute-start | bytes 983048 | tf_op jit(solution)/shard_map/ppermute | solution.py:317
  17.7 1.5 %collective-permute-start.5 = (f32[128,640]{1,0:T(8,128)S(1)}, f32[128,640]{1,0:T(8,128)S(1)}, u32[]{:S(2)}, u32[]{:S(2)}) collective-permute-start(f32[128,640]{1,0:T(8,128)S(1)} %get-tuple-element.54), channel_id=1, source_target_pairs={{0,2},{1,3},{2,0},{3,1},{4,6},{5,7},{6,4},{7,5},{8,10},{9,11},{10,... | collective-permute-start | bytes 983048 | tf_op jit(solution)/shard_map/ppermute | solution.py:317
  19.2 0.2 add.82
  19.4 6.3 %collective-permute-done.2 = f32[128,640]{1,0:T(8,128)S(1)} collective-permute-done((f32[128,640]{1,0:T(8,128)S(1)}, f32[128,640]{1,0:T(8,128)S(1)}, u32[]{:S(2)}, u32[]{:S(2)}) %collective-permute-start.2) | collective-permute-done | bytes 327712 | tf_op jit(solution)/shard_map/ppermute | solution.py:317
  25.8 1.8 %collective-permute-start.15 = (f32[64,640]{1,0:T(8,128)S(1)}, f32[64,640]{1,0:T(8,128)S(1)}, u32[]{:S(2)}, u32[]{:S(2)}) collective-permute-start(f32[64,640]{1,0:T(8,128)S(1)} %get-tuple-element.60), channel_id=1, source_target_pairs={{0,2},{1,3},{2,0},{3,1},{4,6},{5,7},{6,4},{7,5},{8,10},{9,11},{10,... | collective-permute-start | bytes 491528 | tf_op jit(solution)/shard_map/ppermute | solution.py:317
  27.7 0.0 copy-start
  27.7 0.0 copy-start.4
  27.7 1.6 %collective-permute-start.16 = (f32[64,640]{1,0:T(8,128)S(1)}, f32[64,640]{1,0:T(8,128)S(1)}, u32[]{:S(2)}, u32[]{:S(2)}) collective-permute-start(f32[64,640]{1,0:T(8,128)S(1)} %get-tuple-element.63), channel_id=1, source_target_pairs={{0,4},{1,5},{2,6},{3,7},{4,0},{5,1},{6,2},{7,3},{8,12},{9,13},{10,... | collective-permute-start | bytes 491528 | tf_op jit(solution)/shard_map/ppermute | solution.py:317
  29.3 0.1 fusion.1
  29.4 0.6 collective-permute-start.3
  29.9 3.3 %items.1 = f32[32,72,128]{2,1,0:T(8,128)} custom-call(s32[1,512]{1,0:T(1,128)S(1)} %bitcast.3, bf16[512,512]{1,0:T(8,128)(2,1)S(1)} %copy-done.1, bf16[512,2048]{1,0:T(8,128)(2,1)S(1)} %get-tuple-element.41.grad_pre, bf16[512,2048]{1,0:T(8,128)(2,1)S(1)} %copy-done), custom_call_target="tpu_custom_call" | custom-call | tf_op jit(solution)/shard_map/items/pallas_call | solution.py:237
  33.2 4.9 %all-to-all-start = ((f32[32,72,128]{2,1,0:T(8,128)}), f32[32,72,128]{2,1,0:T(8,128)S(1)}, u32[]{:S(2)}, u32[]{:S(2)}) async-start(f32[32,72,128]{2,1,0:T(8,128)} %items.1), calls=%async_computation | async-start | bytes 2359296 | tf_op jit(solution)/shard_map/all_to_all | solution.py:403
  38.2 1.8 %collective-permute-start.6 = (f32[128,640]{1,0:T(8,128)S(1)}, f32[128,640]{1,0:T(8,128)S(1)}, u32[]{:S(2)}, u32[]{:S(2)}) collective-permute-start(f32[128,640]{1,0:T(8,128)S(1)} %get-tuple-element.55), channel_id=1, source_target_pairs={{0,2},{1,3},{2,0},{3,1},{4,6},{5,7},{6,4},{7,5},{8,10},{9,11},{10,... | collective-permute-start | bytes 983048 | tf_op jit(solution)/shard_map/ppermute | solution.py:317
  40.1 1.5 %collective-permute-start.17 = (f32[64,640]{1,0:T(8,128)S(1)}, f32[64,640]{1,0:T(8,128)S(1)}, u32[]{:S(2)}, u32[]{:S(2)}) collective-permute-start(f32[64,640]{1,0:T(8,128)S(1)} %broadcast_select_fusion.2), channel_id=1, source_target_pairs={{0,8},{8,0},{16,24},{24,16},{1,9},{9,1},{17,25},{25,17},{2,10},{10... | collective-permute-start | bytes 491528 | tf_op jit(solution)/shard_map/ppermute | solution.py:317
  41.6 0.0 collective-permute-done.3
  41.6 1.0 add.84
  42.6 0.6 collective-permute-start.4
  43.3 16.3 %collective-permute-done.6 = f32[128,640]{1,0:T(8,128)S(1)} collective-permute-done((f32[128,640]{1,0:T(8,128)S(1)}, f32[128,640]{1,0:T(8,128)S(1)}, u32[]{:S(2)}, u32[]{:S(2)}) %collective-permute-start.6) | collective-permute-done | bytes 327712 | tf_op jit(solution)/shard_map/ppermute | solution.py:317
  59.7 1.1 collective-permute-start.7
  60.8 0.7 collective-permute-done.17
  61.5 4.5 %collective-permute-start.18 = (f32[64,640]{1,0:T(8,128)S(1)}, f32[64,640]{1,0:T(8,128)S(1)}, u32[]{:S(2)}, u32[]{:S(2)}) collective-permute-start(f32[64,640]{1,0:T(8,128)S(1)} %select_add_fusion), channel_id=1, source_target_pairs={{0,16},{8,24},{16,0},{24,8},{1,17},{9,25},{17,1},{25,9},{2,18},{10... | collective-permute-start | bytes 491528 | tf_op jit(solution)/shard_map/ppermute | solution.py:317
  66.0 0.6 collective-permute-done.7
  66.7 0.5 collective-permute-start.8
  67.2 7.2 %collective-permute-done.18 = f32[64,640]{1,0:T(8,128)S(1)} collective-permute-done((f32[64,640]{1,0:T(8,128)S(1)}, f32[64,640]{1,0:T(8,128)S(1)}, u32[]{:S(2)}, u32[]{:S(2)}) %collective-permute-start.18) | collective-permute-done | bytes 163872 | tf_op jit(solution)/shard_map/ppermute | solution.py:317
  74.4 0.1 collective-permute-start.19
  74.5 1.1 collective-permute-done.8
  75.7 0.8 collective-permute-start.9
  76.5 5.1 %collective-permute-done.19 = f32[64,640]{1,0:T(8,128)S(1)} collective-permute-done((f32[64,640]{1,0:T(8,128)S(1)}, f32[64,640]{1,0:T(8,128)S(1)}, u32[]{:S(2)}, u32[]{:S(2)}) %collective-permute-start.19) | collective-permute-done | bytes 163872 | tf_op jit(solution)/shard_map/ppermute | solution.py:317
  81.7 1.6 %collective-permute-start.24 = (f32[64,640]{1,0:T(8,128)S(1)}, f32[64,640]{1,0:T(8,128)S(1)}, u32[]{:S(2)}, u32[]{:S(2)}) collective-permute-start(f32[64,640]{1,0:T(8,128)S(1)} %get-tuple-element.81), channel_id=1, source_target_pairs={{0,2},{1,3},{2,0},{3,1},{4,6},{5,7},{6,4},{7,5},{8,10},{9,11},{10,... | collective-permute-start | bytes 491528 | tf_op jit(solution)/shard_map/ppermute | solution.py:317
  83.3 1.4 %collective-permute-done.9 = f32[64,640]{1,0:T(8,128)S(1)} collective-permute-done((f32[64,640]{1,0:T(8,128)S(1)}, f32[64,640]{1,0:T(8,128)S(1)}, u32[]{:S(2)}, u32[]{:S(2)}) %collective-permute-start.9) | collective-permute-done | bytes 163872 | tf_op jit(solution)/shard_map/ppermute | solution.py:317
  84.8 0.1 collective-permute-start.10
  84.8 1.5 %collective-permute-start.20 = (f32[64,640]{1,0:T(8,128)S(1)}, f32[64,640]{1,0:T(8,128)S(1)}, u32[]{:S(2)}, u32[]{:S(2)}) collective-permute-start(f32[64,640]{1,0:T(8,128)S(1)} %get-tuple-element.82), channel_id=1, source_target_pairs={{0,4},{1,5},{2,6},{3,7},{4,0},{5,1},{6,2},{7,3},{8,12},{9,13},{10,... | collective-permute-start | bytes 491528 | tf_op jit(solution)/shard_map/ppermute | solution.py:317
  86.4 0.7 collective-permute-done.24
  87.1 1.8 %collective-permute-start.25 = (f32[128,640]{1,0:T(8,128)S(1)}, f32[128,640]{1,0:T(8,128)S(1)}, u32[]{:S(2)}, u32[]{:S(2)}) collective-permute-start(f32[128,640]{1,0:T(8,128)S(1)} %pad_maximum_fusion.3.refs_4_), channel_id=1, source_target_pairs={{0,4},{1,5},{2,6},{3,7},{4,0},{5,1},{6,2},{7,3},{8,12},{9,13},{10,... | collective-permute-start | bytes 983048 | tf_op jit(solution)/shard_map/ppermute | solution.py:317
  88.9 1.3 %collective-permute-done.10 = f32[64,640]{1,0:T(8,128)S(1)} collective-permute-done((f32[64,640]{1,0:T(8,128)S(1)}, f32[64,640]{1,0:T(8,128)S(1)}, u32[]{:S(2)}, u32[]{:S(2)}) %collective-permute-start.10) | collective-permute-done | bytes 163872 | tf_op jit(solution)/shard_map/ppermute | solution.py:317
  90.2 1.5 %collective-permute-start.11 = (f32[64,640]{1,0:T(8,128)S(1)}, f32[64,640]{1,0:T(8,128)S(1)}, u32[]{:S(2)}, u32[]{:S(2)}) collective-permute-start(f32[64,640]{1,0:T(8,128)S(1)} %get-tuple-element.88), channel_id=1, source_target_pairs={{0,4},{1,5},{2,6},{3,7},{4,0},{5,1},{6,2},{7,3},{8,12},{9,13},{10,... | collective-permute-start | bytes 491528 | tf_op jit(solution)/shard_map/ppermute | solution.py:317
  91.7 0.4 collective-permute-done.20
  92.1 1.5 %collective-permute-start.21 = (f32[128,640]{1,0:T(8,128)S(1)}, f32[128,640]{1,0:T(8,128)}, u32[]{:S(2)}, u32[]{:S(2)}) collective-permute-start(f32[128,640]{1,0:T(8,128)S(1)} %pad_maximum_fusion.2.refs_0_), channel_id=1, source_target_pairs={{0,2},{1,3},{2,0},{3,1},{4,6},{5,7},{6,4},{7,5},{8,10},{9,11},{10,... | collective-permute-start | bytes 983048 | tf_op jit(solution)/shard_map/ppermute | solution.py:317
  93.6 0.5 collective-permute-start.13
  94.2 5.9 %collective-permute-done.11 = f32[64,640]{1,0:T(8,128)S(1)} collective-permute-done((f32[64,640]{1,0:T(8,128)S(1)}, f32[64,640]{1,0:T(8,128)S(1)}, u32[]{:S(2)}, u32[]{:S(2)}) %collective-permute-start.11) | collective-permute-done | bytes 163872 | tf_op jit(solution)/shard_map/ppermute | solution.py:317
  100.1 2.6 %collective-permute-done.13 = f32[64,640]{1,0:T(8,128)S(1)} collective-permute-done((f32[64,640]{1,0:T(8,128)S(1)}, f32[64,640]{1,0:T(8,128)S(1)}, u32[]{:S(2)}, u32[]{:S(2)}) %collective-permute-start.13) | collective-permute-done | bytes 163872 | tf_op jit(solution)/shard_map/ppermute | solution.py:317
  102.8 0.0 collective-permute-done.25.refs_5_
  102.8 0.1 collective-permute-start.27
  102.9 0.5 collective-permute-start.23
  103.3 1.3 %collective-permute-start.14 = (f32[128,640]{1,0:T(8,128)S(1)}, f32[128,640]{1,0:T(8,128)S(1)}, u32[]{:S(2)}, u32[]{:S(2)}) collective-permute-start(f32[128,640]{1,0:T(8,128)S(1)} %pad_maximum_fusion.1.refs_4_), channel_id=1, source_target_pairs={{0,4},{1,5},{2,6},{3,7},{4,0},{5,1},{6,2},{7,3},{8,12},{9,13},{10,... | collective-permute-start | bytes 983048 | tf_op jit(solution)/shard_map/ppermute | solution.py:317
  104.7 0.7 copy-done.2
  105.4 1.5 %collective-permute-start.12 = (f32[128,640]{1,0:T(8,128)S(1)}, f32[128,640]{1,0:T(8,128)S(1)}, u32[]{:S(2)}, u32[]{:S(2)}) collective-permute-start(f32[128,640]{1,0:T(8,128)S(1)} %pad_maximum_fusion.refs_0_), channel_id=1, source_target_pairs={{0,2},{1,3},{2,0},{3,1},{4,6},{5,7},{6,4},{7,5},{8,10},{9,11},{10,... | collective-permute-start | bytes 983048 | tf_op jit(solution)/shard_map/ppermute | solution.py:317
  106.9 2.8 %table.1 = f32[1024,512]{1,0:T(8,128)} custom-call(f32[32,72,128]{2,1,0:T(8,128)S(1)} %all-to-all-done.got), custom_call_target="tpu_custom_call" | custom-call | tf_op jit(solution)/shard_map/table/pallas_call | solution.py:263
  109.7 0.5 collective-permute-start.28
  110.2 3.0 %place.2 = (f32[512,2048]{1,0:T(8,128)}, f32[512,512]{1,0:T(8,128)}) custom-call(s32[2]{0:T(128)S(1)} %pad_add_fusion.place, f32[128,640]{1,0:T(8,128)S(1)} %pad_maximum_fusion.2.refs_0_, f32[128,640]{1,0:T(8,128)} %collective-permute-done.21.refs_1_, f32[128,640]{1,0:T(8,128)} %collective-permute-done.22.refs_2_, ...), custom_call_target="tpu_custom_call" | custom-call | tf_op jit(solution)/shard_map/place/pallas_call | solution.py:300
  113.2 1.6 %collective-permute-done.12.refs_1_ = f32[128,640]{1,0:T(8,128)S(1)} collective-permute-done((f32[128,640]{1,0:T(8,128)S(1)}, f32[128,640]{1,0:T(8,128)S(1)}, u32[]{:S(2)}, u32[]{:S(2)}) %collective-permute-start.12) | collective-permute-done | bytes 327712 | tf_op jit(solution)/shard_map/ppermute | solution.py:317
  114.8 0.5 collective-permute-start.31
  115.3 1.1 collective-permute-done.29.refs_3_
  116.5 0.5 collective-permute-done.31.refs_7_
  116.9 2.2 %place.3 = (f32[512,2048]{1,0:T(8,128)}, f32[512,512]{1,0:T(8,128)}) custom-call(s32[2]{0:T(128)S(1)} %pad_add_fusion.place, f32[128,640]{1,0:T(8,128)S(1)} %pad_maximum_fusion.refs_0_, f32[128,640]{1,0:T(8,128)S(1)} %collective-permute-done.12.refs_1_, ...), custom_call_target="tpu_custom_call", output_to_operand_aliasing={{0}: (9, {}), {1}: (10, {})} | custom-call | tf_op jit(solution)/shard_map/place/pallas_call | solution.py:300
  (45 shorter events, 0.6 us)
Async XLA Ops:
  0.8 0.7 copy-start.5
  1.4 10.4 %copy-start.1 = (bf16[512,512]{1,0:T(8,128)(2,1)S(1)}, bf16[512,512]{1,0:T(8,128)(2,1)}, u32[]{:S(2)}) copy-start(bf16[512,512]{1,0:T(8,128)(2,1)} %cot.3) | copy-start | bytes 1572868
  11.3 3.2 %collective-permute-start.1 = (f32[512,640]{1,0:T(8,128)S(1)}, f32[512,640]{1,0:T(8,128)S(1)}, u32[]{:S(2)}, u32[]{:S(2)}) collective-permute-start(f32[512,640]{1,0:T(8,128)S(1)} %get-tuple-element.47), channel_id=1, source_target_pairs={{0,1},{1,0},{2,3},{3,2},{4,5},{5,4},{6,7},{7,6},{8,9},{9,8},{10,11... | collective-permute-start | bytes 3932168 | tf_op jit(solution)/shard_map/ppermute | solution.py:317
  12.8 6.4 %collective-permute-start = (f32[512,640]{1,0:T(8,128)S(1)}, f32[512,640]{1,0:T(8,128)S(1)}, u32[]{:S(2)}, u32[]{:S(2)}) collective-permute-start(f32[512,640]{1,0:T(8,128)S(1)} %get-tuple-element.43), channel_id=1, source_target_pairs={{0,1},{1,0},{2,3},{3,2},{4,5},{5,4},{6,7},{7,6},{8,9},{9,8},{10,11... | collective-permute-start | bytes 3932168 | tf_op jit(solution)/shard_map/ppermute | solution.py:317
  14.8 11.0 %collective-permute-start.2 = (f32[128,640]{1,0:T(8,128)S(1)}, f32[128,640]{1,0:T(8,128)S(1)}, u32[]{:S(2)}, u32[]{:S(2)}) collective-permute-start(f32[128,640]{1,0:T(8,128)S(1)} %get-tuple-element.48), channel_id=1, source_target_pairs={{0,4},{1,5},{2,6},{3,7},{4,0},{5,1},{6,2},{7,3},{8,12},{9,13},{10,... | collective-permute-start | bytes 983048 | tf_op jit(solution)/shard_map/ppermute | solution.py:317
  17.7 9.9 %collective-permute-start.5 = (f32[128,640]{1,0:T(8,128)S(1)}, f32[128,640]{1,0:T(8,128)S(1)}, u32[]{:S(2)}, u32[]{:S(2)}) collective-permute-start(f32[128,640]{1,0:T(8,128)S(1)} %get-tuple-element.54), channel_id=1, source_target_pairs={{0,2},{1,3},{2,0},{3,1},{4,6},{5,7},{6,4},{7,5},{8,10},{9,11},{10,... | collective-permute-start | bytes 983048 | tf_op jit(solution)/shard_map/ppermute | solution.py:317
  25.8 14.2 %collective-permute-start.15 = (f32[64,640]{1,0:T(8,128)S(1)}, f32[64,640]{1,0:T(8,128)S(1)}, u32[]{:S(2)}, u32[]{:S(2)}) collective-permute-start(f32[64,640]{1,0:T(8,128)S(1)} %get-tuple-element.60), channel_id=1, source_target_pairs={{0,2},{1,3},{2,0},{3,1},{4,6},{5,7},{6,4},{7,5},{8,10},{9,11},{10,... | collective-permute-start | bytes 491528 | tf_op jit(solution)/shard_map/ppermute | solution.py:317
  27.7 2.3 %copy-start = (bf16[512,2048]{1,0:T(8,128)(2,1)S(1)}, bf16[512,2048]{1,0:T(8,128)(2,1)}, u32[]{:S(2)}) copy-start(bf16[512,2048]{1,0:T(8,128)(2,1)} %in_proj.1) | copy-start | bytes 6291460
  27.7 2.3 %copy-start.4 = (s32[512]{0:T(512)S(1)}, s32[512]{0:T(512)}, u32[]{:S(2)}) copy-start(s32[512]{0:T(512)} %param.11) | copy-start | bytes 6148
  27.7 12.3 %collective-permute-start.16 = (f32[64,640]{1,0:T(8,128)S(1)}, f32[64,640]{1,0:T(8,128)S(1)}, u32[]{:S(2)}, u32[]{:S(2)}) collective-permute-start(f32[64,640]{1,0:T(8,128)S(1)} %get-tuple-element.63), channel_id=1, source_target_pairs={{0,4},{1,5},{2,6},{3,7},{4,0},{5,1},{6,2},{7,3},{8,12},{9,13},{10,... | collective-permute-start | bytes 491528 | tf_op jit(solution)/shard_map/ppermute | solution.py:317
  29.4 12.2 %collective-permute-start.3 = (f32[128,640]{1,0:T(8,128)S(1)}, f32[128,640]{1,0:T(8,128)}, u32[]{:S(2)}, u32[]{:S(2)}) collective-permute-start(f32[128,640]{1,0:T(8,128)S(1)} %get-tuple-element.49), channel_id=1, source_target_pairs={{0,4},{1,5},{2,6},{3,7},{4,0},{5,1},{6,2},{7,3},{8,12},{9,13},{10,... | collective-permute-start | bytes 983048 | tf_op jit(solution)/shard_map/ppermute | solution.py:317
  33.2 73.7 %all-to-all-start = ((f32[32,72,128]{2,1,0:T(8,128)}), f32[32,72,128]{2,1,0:T(8,128)S(1)}, u32[]{:S(2)}, u32[]{:S(2)}) async-start(f32[32,72,128]{2,1,0:T(8,128)} %items.1), calls=%async_computation | async-start | bytes 2359296 | tf_op jit(solution)/shard_map/all_to_all | solution.py:403
  38.2 21.4 %collective-permute-start.6 = (f32[128,640]{1,0:T(8,128)S(1)}, f32[128,640]{1,0:T(8,128)S(1)}, u32[]{:S(2)}, u32[]{:S(2)}) collective-permute-start(f32[128,640]{1,0:T(8,128)S(1)} %get-tuple-element.55), channel_id=1, source_target_pairs={{0,2},{1,3},{2,0},{3,1},{4,6},{5,7},{6,4},{7,5},{8,10},{9,11},{10,... | collective-permute-start | bytes 983048 | tf_op jit(solution)/shard_map/ppermute | solution.py:317
  40.1 21.4 %collective-permute-start.17 = (f32[64,640]{1,0:T(8,128)S(1)}, f32[64,640]{1,0:T(8,128)S(1)}, u32[]{:S(2)}, u32[]{:S(2)}) collective-permute-start(f32[64,640]{1,0:T(8,128)S(1)} %broadcast_select_fusion.2), channel_id=1, source_target_pairs={{0,8},{8,0},{16,24},{24,16},{1,9},{9,1},{17,25},{25,17},{2,10},{10... | collective-permute-start | bytes 491528 | tf_op jit(solution)/shard_map/ppermute | solution.py:317
  42.6 23.4 %collective-permute-start.4 = (f32[64,640]{1,0:T(8,128)S(1)}, f32[64,640]{1,0:T(8,128)S(1)}, u32[]{:S(2)}, u32[]{:S(2)}) collective-permute-start(f32[64,640]{1,0:T(8,128)S(1)} %get-tuple-element.51), channel_id=1, source_target_pairs={{0,2},{1,3},{2,0},{3,1},{4,6},{5,7},{6,4},{7,5},{8,10},{9,11},{10,... | collective-permute-start | bytes 491528 | tf_op jit(solution)/shard_map/ppermute | solution.py:317
  59.7 7.0 %collective-permute-start.7 = (f32[64,640]{1,0:T(8,128)S(1)}, f32[64,640]{1,0:T(8,128)S(1)}, u32[]{:S(2)}, u32[]{:S(2)}) collective-permute-start(f32[64,640]{1,0:T(8,128)S(1)} %get-tuple-element.57), channel_id=1, source_target_pairs={{0,4},{1,5},{2,6},{3,7},{4,0},{5,1},{6,2},{7,3},{8,12},{9,13},{10,... | collective-permute-start | bytes 491528 | tf_op jit(solution)/shard_map/ppermute | solution.py:317
  61.5 12.9 %collective-permute-start.18 = (f32[64,640]{1,0:T(8,128)S(1)}, f32[64,640]{1,0:T(8,128)S(1)}, u32[]{:S(2)}, u32[]{:S(2)}) collective-permute-start(f32[64,640]{1,0:T(8,128)S(1)} %select_add_fusion), channel_id=1, source_target_pairs={{0,16},{8,24},{16,0},{24,8},{1,17},{9,25},{17,1},{25,9},{2,18},{10... | collective-permute-start | bytes 491528 | tf_op jit(solution)/shard_map/ppermute | solution.py:317
  66.7 9.0 %collective-permute-start.8 = (f32[64,640]{1,0:T(8,128)S(1)}, f32[64,640]{1,0:T(8,128)S(1)}, u32[]{:S(2)}, u32[]{:S(2)}) collective-permute-start(f32[64,640]{1,0:T(8,128)S(1)} %broadcast_select_fusion.5), channel_id=1, source_target_pairs={{0,8},{8,0},{16,24},{24,16},{1,9},{9,1},{17,25},{25,17},{2,10},{10... | collective-permute-start | bytes 491528 | tf_op jit(solution)/shard_map/ppermute | solution.py:317
  74.4 7.3 %collective-permute-start.19 = (f32[64,640]{1,0:T(8,128)S(1)}, f32[64,640]{1,0:T(8,128)S(1)}, u32[]{:S(2)}, u32[]{:S(2)}) collective-permute-start(f32[64,640]{1,0:T(8,128)S(1)} %add_multiply_fusion), channel_id=1, source_target_pairs={{0,8},{8,0},{16,24},{24,16},{1,9},{9,1},{17,25},{25,17},{2,10},{10... | collective-permute-start | bytes 491528 | tf_op jit(solution)/shard_map/ppermute | solution.py:317
  75.7 9.1 %collective-permute-start.9 = (f32[64,640]{1,0:T(8,128)S(1)}, f32[64,640]{1,0:T(8,128)S(1)}, u32[]{:S(2)}, u32[]{:S(2)}) collective-permute-start(f32[64,640]{1,0:T(8,128)S(1)} %select_add_fusion.1), channel_id=1, source_target_pairs={{0,16},{8,24},{16,0},{24,8},{1,17},{9,25},{17,1},{25,9},{2,18},{10... | collective-permute-start | bytes 491528 | tf_op jit(solution)/shard_map/ppermute | solution.py:317
  81.7 5.4 %collective-permute-start.24 = (f32[64,640]{1,0:T(8,128)S(1)}, f32[64,640]{1,0:T(8,128)S(1)}, u32[]{:S(2)}, u32[]{:S(2)}) collective-permute-start(f32[64,640]{1,0:T(8,128)S(1)} %get-tuple-element.81), channel_id=1, source_target_pairs={{0,2},{1,3},{2,0},{3,1},{4,6},{5,7},{6,4},{7,5},{8,10},{9,11},{10,... | collective-permute-start | bytes 491528 | tf_op jit(solution)/shard_map/ppermute | solution.py:317
  84.8 5.4 %collective-permute-start.10 = (f32[64,640]{1,0:T(8,128)S(1)}, f32[64,640]{1,0:T(8,128)S(1)}, u32[]{:S(2)}, u32[]{:S(2)}) collective-permute-start(f32[64,640]{1,0:T(8,128)S(1)} %add_multiply_fusion.1), channel_id=1, source_target_pairs={{0,8},{8,0},{16,24},{24,16},{1,9},{9,1},{17,25},{25,17},{2,10},{10... | collective-permute-start | bytes 491528 | tf_op jit(solution)/shard_map/ppermute | solution.py:317
  84.8 7.2 %collective-permute-start.20 = (f32[64,640]{1,0:T(8,128)S(1)}, f32[64,640]{1,0:T(8,128)S(1)}, u32[]{:S(2)}, u32[]{:S(2)}) collective-permute-start(f32[64,640]{1,0:T(8,128)S(1)} %get-tuple-element.82), channel_id=1, source_target_pairs={{0,4},{1,5},{2,6},{3,7},{4,0},{5,1},{6,2},{7,3},{8,12},{9,13},{10,... | collective-permute-start | bytes 491528 | tf_op jit(solution)/shard_map/ppermute | solution.py:317
  87.1 15.7 %collective-permute-start.25 = (f32[128,640]{1,0:T(8,128)S(1)}, f32[128,640]{1,0:T(8,128)S(1)}, u32[]{:S(2)}, u32[]{:S(2)}) collective-permute-start(f32[128,640]{1,0:T(8,128)S(1)} %pad_maximum_fusion.3.refs_4_), channel_id=1, source_target_pairs={{0,4},{1,5},{2,6},{3,7},{4,0},{5,1},{6,2},{7,3},{8,12},{9,13},{10,... | collective-permute-start | bytes 983048 | tf_op jit(solution)/shard_map/ppermute | solution.py:317
  90.2 9.9 %collective-permute-start.11 = (f32[64,640]{1,0:T(8,128)S(1)}, f32[64,640]{1,0:T(8,128)S(1)}, u32[]{:S(2)}, u32[]{:S(2)}) collective-permute-start(f32[64,640]{1,0:T(8,128)S(1)} %get-tuple-element.88), channel_id=1, source_target_pairs={{0,4},{1,5},{2,6},{3,7},{4,0},{5,1},{6,2},{7,3},{8,12},{9,13},{10,... | collective-permute-start | bytes 491528 | tf_op jit(solution)/shard_map/ppermute | solution.py:317
  92.1 10.8 %collective-permute-start.21 = (f32[128,640]{1,0:T(8,128)S(1)}, f32[128,640]{1,0:T(8,128)}, u32[]{:S(2)}, u32[]{:S(2)}) collective-permute-start(f32[128,640]{1,0:T(8,128)S(1)} %pad_maximum_fusion.2.refs_0_), channel_id=1, source_target_pairs={{0,2},{1,3},{2,0},{3,1},{4,6},{5,7},{6,4},{7,5},{8,10},{9,11},{10,... | collective-permute-start | bytes 983048 | tf_op jit(solution)/shard_map/ppermute | solution.py:317
  93.6 11.1 %collective-permute-start.26 = (f32[128,640]{1,0:T(8,128)S(1)}, f32[128,640]{1,0:T(8,128)S(1)}, u32[]{:S(2)}, u32[]{:S(2)}) collective-permute-start(f32[128,640]{1,0:T(8,128)S(1)} %pad_maximum_fusion.3.refs_4_), channel_id=1, source_target_pairs={{0,1},{1,0},{2,3},{3,2},{4,5},{5,4},{6,7},{7,6},{8,9},{9,8},{10,11... | collective-permute-start | bytes 983048 | tf_op jit(solution)/shard_map/ppermute | solution.py:317
  93.6 9.1 %collective-permute-start.13 = (f32[64,640]{1,0:T(8,128)S(1)}, f32[64,640]{1,0:T(8,128)S(1)}, u32[]{:S(2)}, u32[]{:S(2)}) collective-permute-start(f32[64,640]{1,0:T(8,128)S(1)} %get-tuple-element.87), channel_id=1, source_target_pairs={{0,2},{1,3},{2,0},{3,1},{4,6},{5,7},{6,4},{7,5},{8,10},{9,11},{10,... | collective-permute-start | bytes 491528 | tf_op jit(solution)/shard_map/ppermute | solution.py:317
  100.1 9.6 %collective-permute-start.22 = (f32[128,640]{1,0:T(8,128)S(1)}, f32[128,640]{1,0:T(8,128)}, u32[]{:S(2)}, u32[]{:S(2)}) collective-permute-start(f32[128,640]{1,0:T(8,128)S(1)} %pad_maximum_fusion.2.refs_0_), channel_id=1, source_target_pairs={{0,1},{1,0},{2,3},{3,2},{4,5},{5,4},{6,7},{7,6},{8,9},{9,8},{10,11... | collective-permute-start | bytes 983048 | tf_op jit(solution)/shard_map/ppermute | solution.py:317
  102.8 6.9 %collective-permute-start.27 = (f32[128,640]{1,0:T(8,128)S(1)}, f32[128,640]{1,0:T(8,128)}, u32[]{:S(2)}, u32[]{:S(2)}) collective-permute-start(f32[128,640]{1,0:T(8,128)S(1)} %collective-permute-done.25.refs_5_), channel_id=1, source_target_pairs={{0,1},{1,0},{2,3},{3,2},{4,5},{5,4},{6,7},{7,6},{8,9},{9,8},{10,11... | collective-permute-start | bytes 983048 | tf_op jit(solution)/shard_map/ppermute | solution.py:317
  102.9 7.4 %collective-permute-start.23 = (f32[128,640]{1,0:T(8,128)}, f32[128,640]{1,0:T(8,128)}, u32[]{:S(2)}, u32[]{:S(2)}) collective-permute-start(f32[128,640]{1,0:T(8,128)} %collective-permute-done.21.refs_1_), channel_id=1, source_target_pairs={{0,1},{1,0},{2,3},{3,2},{4,5},{5,4},{6,7},{7,6},{8,9},{9,8},{10,11... | collective-permute-start | bytes 983048 | tf_op jit(solution)/shard_map/ppermute | solution.py:317
  103.3 9.9 %collective-permute-start.14 = (f32[128,640]{1,0:T(8,128)S(1)}, f32[128,640]{1,0:T(8,128)S(1)}, u32[]{:S(2)}, u32[]{:S(2)}) collective-permute-start(f32[128,640]{1,0:T(8,128)S(1)} %pad_maximum_fusion.1.refs_4_), channel_id=1, source_target_pairs={{0,4},{1,5},{2,6},{3,7},{4,0},{5,1},{6,2},{7,3},{8,12},{9,13},{10,... | collective-permute-start | bytes 983048 | tf_op jit(solution)/shard_map/ppermute | solution.py:317
  104.7 0.7 copy-start.2
  105.4 9.4 %collective-permute-start.12 = (f32[128,640]{1,0:T(8,128)S(1)}, f32[128,640]{1,0:T(8,128)S(1)}, u32[]{:S(2)}, u32[]{:S(2)}) collective-permute-start(f32[128,640]{1,0:T(8,128)S(1)} %pad_maximum_fusion.refs_0_), channel_id=1, source_target_pairs={{0,2},{1,3},{2,0},{3,1},{4,6},{5,7},{6,4},{7,5},{8,10},{9,11},{10,... | collective-permute-start | bytes 983048 | tf_op jit(solution)/shard_map/ppermute | solution.py:317
  106.9 3.3 %copy-start.3 = (f32[128,640]{1,0:T(8,128)S(1)}, f32[128,640]{1,0:T(8,128)}, u32[]{:S(2)}) copy-start(f32[128,640]{1,0:T(8,128)} %copy-done.2) | copy-start | bytes 983044
  109.7 5.7 %collective-permute-start.30 = (f32[128,640]{1,0:T(8,128)S(1)}, f32[128,640]{1,0:T(8,128)S(1)}, u32[]{:S(2)}, u32[]{:S(2)}) collective-permute-start(f32[128,640]{1,0:T(8,128)S(1)} %pad_maximum_fusion.1.refs_4_), channel_id=1, source_target_pairs={{0,1},{1,0},{2,3},{3,2},{4,5},{5,4},{6,7},{7,6},{8,9},{9,8},{10,11... | collective-permute-start | bytes 983048 | tf_op jit(solution)/shard_map/ppermute | solution.py:317
  109.7 5.6 %collective-permute-start.28 = (f32[128,640]{1,0:T(8,128)S(1)}, f32[128,640]{1,0:T(8,128)S(1)}, u32[]{:S(2)}, u32[]{:S(2)}) collective-permute-start(f32[128,640]{1,0:T(8,128)S(1)} %pad_maximum_fusion.refs_0_), channel_id=1, source_target_pairs={{0,1},{1,0},{2,3},{3,2},{4,5},{5,4},{6,7},{7,6},{8,9},{9,8},{10,11... | collective-permute-start | bytes 983048 | tf_op jit(solution)/shard_map/ppermute | solution.py:317
  114.8 1.6 %collective-permute-start.29 = (f32[128,640]{1,0:T(8,128)S(1)}, f32[128,640]{1,0:T(8,128)S(1)}, u32[]{:S(2)}, u32[]{:S(2)}) collective-permute-start(f32[128,640]{1,0:T(8,128)S(1)} %collective-permute-done.12.refs_1_), channel_id=1, source_target_pairs={{0,1},{1,0},{2,3},{3,2},{4,5},{5,4},{6,7},{7,6},{8,9},{9,8},{10,11... | collective-permute-start | bytes 983048 | tf_op jit(solution)/shard_map/ppermute | solution.py:317
  114.8 2.1 %collective-permute-start.31 = (f32[128,640]{1,0:T(8,128)S(1)}, f32[128,640]{1,0:T(8,128)S(1)}, u32[]{:S(2)}, u32[]{:S(2)}) collective-permute-start(f32[128,640]{1,0:T(8,128)S(1)} %collective-permute-done.14.refs_5_), channel_id=1, source_target_pairs={{0,1},{1,0},{2,3},{3,2},{4,5},{5,4},{6,7},{7,6},{8,9},{9,8},{10,11... | collective-permute-start | bytes 983048 | tf_op jit(solution)/shard_map/ppermute | solution.py:317

commit v4 on v2

--- a/solution.py
+++ b/solution.py
@@ -38,8 +38,8 @@
 
 def block_kernel(
     chunk, place, lengths, emb_hbm, cot_hbm, in_hbm, out_hbm,
-    keep, send, grad_pre, rel_a, rel_b, rel_g,
-    emb, cot, in_proj, out_proj, hid, dpre, mask, wts, dsc, att, gated_out, sems,
+    keep, send, grad_pre, rel_q, rel_r, rel_g,
+    emb, cot, in_proj, out_proj, hid, dpre, mask, wts, dsc, att, gated_out, rel_p, sems,
 ):
     rows, width = emb.shape
     head = width // H
@@ -77,11 +77,8 @@
     emb_t = emb[...].T
     count = width // chunk
     for c in range(count):
-        src = slice(c * chunk, (c + 1) * chunk)
-        to_a = pl.ds(pl.multiple_of((c ^ place[0]) * chunk, chunk), chunk)
-        to_b = pl.ds(pl.multiple_of((c ^ place[1]) * chunk, chunk), chunk)
-        rel_a[to_a, :] = emb_t[src]
-        rel_b[to_b, :] = emb_t[src]
+        for chain, rel in enumerate((rel_p, rel_q, rel_r)):
+            rel[moved(c, place, chain, chunk), :] = emb_t[c * chunk : (c + 1) * chunk]
     for h in range(H):
         v, q, k = (pl.ds((c * H + h) * head, head) for c in (1, 2, 3))
         for i in range(rows // TILE):
@@ -116,8 +113,7 @@
         grad_att.append(g.astype(jnp.bfloat16))
     gated_t = gated_out[...].T
     for c in range(count):
-        to_b = pl.ds(pl.multiple_of((c ^ place[1]) * chunk, chunk), chunk)
-        rel_g[to_b, :] = gated_t[c * chunk : (c + 1) * chunk]
+        rel_g[moved(c, place, 2, chunk), :] = gated_t[c * chunk : (c + 1) * chunk]
     for h in range(H):
         v, q, k = (pl.ds((c * H + h) * head, head) for c in (1, 2, 3))
         grad_v, grad_k = [None] * (rows // TILE), [None] * (rows // TILE)
@@ -137,16 +133,19 @@
             r = pl.ds(j * TILE, TILE)
             grad_pre[r, v] = (grad_v[j] * dpre[r, v]).astype(jnp.bfloat16)
             grad_pre[r, k] = (grad_k[j] * scale * dpre[r, k]).astype(jnp.bfloat16)
-    half, cut = width // 2, keep.shape[1]
-    for out, r in ((send, pl.ds(half, half)), (keep, pl.ds(0, half))):
-        out[:half, :] = dot_nn(rel_a[r, :], grad_pre[:, :cut])
-        out[half:, :] = dot_nn(rel_b[r, :], grad_pre[:, cut : 2 * cut])
-
-
-def block_call(chunk, place, lengths, emb, cot, in_proj, out_proj):
+    half, cut = keep.shape
+    keep[...] = dot_nn(rel_p[:half, :], grad_pre[:, :cut])
+    send[...] = dot_nn(rel_p[half:, :], grad_pre[:, :cut])
+
+
+def moved(c, place, chain, chunk):
+    return pl.ds(pl.multiple_of((c ^ place[chain]) * chunk, chunk), chunk)
+
+
+def block_call(chunk, cut, place, lengths, emb, cot, in_proj, out_proj):
     rows, width = emb.shape
     vmem = pl.BlockSpec(memory_space=VMEM)
-    part = jax.ShapeDtypeStruct((width, 5 * width // 4), jnp.float32)
+    part = jax.ShapeDtypeStruct((width // 2, cut), jnp.float32)
     square = jax.ShapeDtypeStruct((width, rows), jnp.bfloat16)
     return pl.pallas_call(
         functools.partial(block_kernel, chunk),
@@ -166,34 +165,37 @@
             pltpu.VMEM((H, rows, rows), jnp.float32),
             pltpu.VMEM((rows, width), jnp.float32),
             pltpu.VMEM((rows, width), jnp.bfloat16),
+            pltpu.VMEM((width, rows), jnp.bfloat16),
             pltpu.SemaphoreType.DMA((7,)),
         ],
-        compiler_params=pltpu.CompilerParams(vmem_limit_bytes=40 << 20),
-    )(place, lengths, emb, cot, in_proj, out_proj)
-
-
-def second_kernel(rel_a, rel_b, rel_g, cot, grad_pre, keep, send):
-    width = cot.shape[1]
-    half, cut = width // 2, keep.shape[1]
-    inner = 4 * width - 3 * cut
-    for out, r in ((send, pl.ds(half, half)), (keep, pl.ds(0, half))):
-        out[:half, :] = dot_nn(rel_a[r, :], grad_pre[:, 2 * cut : 3 * cut])
-        out[half:, :inner] = dot_nn(rel_b[r, :], grad_pre[:, 3 * cut :])
-        out[half:, inner:] = dot_nn(rel_g[r, :], cot[...])
-
-
-def second_call(rel_a, rel_b, rel_g, cot, grad_pre):
+        compiler_params=pltpu.CompilerParams(vmem_limit_bytes=28 << 20),
+    )(place, lengths, *(pltpu.with_memory_space_constraint(x, HBM) for x in (emb, cot, in_proj, out_proj)))
+
+
+def rest_kernel(first, rel_q, rel_r, rel_g, cot, grad_pre, keep_q, send_q, keep_r, send_r):
+    half, cut = keep_q.shape
+    at = first + cut
+    inner = grad_pre.shape[1] - at
+    for keep, r in ((keep_q, pl.ds(0, half)), (send_q, pl.ds(half, half))):
+        keep[...] = dot_nn(rel_q[r, :], grad_pre[:, first:at])
+    for keep, r in ((keep_r, pl.ds(0, half)), (send_r, pl.ds(half, half))):
+        if inner:
+            keep[:, :inner] = dot_nn(rel_r[r, :], grad_pre[:, at:])
+        keep[:, inner:] = dot_nn(rel_g[r, :], cot[...])
+
+
+def rest_call(cuts, rel_q, rel_r, rel_g, cot, grad_pre):
     width = cot.shape[1]
     vmem = pl.BlockSpec(memory_space=VMEM)
-    part = jax.ShapeDtypeStruct((width, 5 * width // 4), jnp.float32)
+    part_q, part_r = (jax.ShapeDtypeStruct((width // 2, n), jnp.float32) for n in cuts[1:])
     return pl.pallas_call(
-        second_kernel,
-        name="second",
-        out_shape=(part, part),
+        functools.partial(rest_kernel, cuts[0]),
+        name="rest",
+        out_shape=(part_q, part_q, part_r, part_r),
         in_specs=[vmem] * 5,
-        out_specs=(vmem,) * 2,
-        compiler_params=pltpu.CompilerParams(vmem_limit_bytes=16 << 20),
-    )(rel_a, rel_b, rel_g, cot, grad_pre)
+        out_specs=(vmem,) * 4,
+        compiler_params=pltpu.CompilerParams(vmem_limit_bytes=8 << 20),
+    )(rel_q, rel_r, rel_g, cot, grad_pre)
 
 
 def split_bf16(x):
@@ -240,7 +242,7 @@
         out_shape=jax.ShapeDtypeStruct((owners, (width // 128) * slots + 8, 128), jnp.float32),
         in_specs=[vmem] * 4,
         out_specs=vmem,
-        compiler_params=pltpu.CompilerParams(vmem_limit_bytes=40 << 20),
+        compiler_params=pltpu.CompilerParams(vmem_limit_bytes=8 << 20),
     )(ids, cot, grad_pre, in_proj)
 
 
@@ -266,27 +268,23 @@
         out_shape=jax.ShapeDtypeStruct((OWN_ROWS, width), jnp.float32),
         in_specs=[vmem],
         out_specs=vmem,
-        compiler_params=pltpu.CompilerParams(vmem_limit_bytes=40 << 20),
+        compiler_params=pltpu.CompilerParams(vmem_limit_bytes=8 << 20),
     )(got)
 
 
-def place_kernel(chunk, column, place, *refs):
-    pieces, outs, sems = refs[:8], refs[-3:-1], refs[-1]
-    in_grad, out_grad = outs
-    cut = pieces[0].shape[1]
+def place_kernel(chunk, spots, place, *refs):
+    pieces, (in_grad, out_grad), sems = refs[: len(spots)], refs[-3:-1], refs[-1]
     copies = []
-    for side in range(2):
-        first = column + side * cut
+    for piece, (chain, first, position) in zip(pieces, spots):
+        cut = piece.shape[1]
         inner = min(cut, in_grad.shape[1] - first)
-        position = 0
-        for piece in pieces[side * 4 : side * 4 + 4]:
-            for c in range(piece.shape[0] // chunk):
-                row = pl.ds(pl.multiple_of((position ^ place[side]) * chunk, chunk), chunk)
-                src = piece.at[pl.ds(c * chunk, chunk)]
+        for c in range(piece.shape[0] // chunk):
+            row = moved(position + c, place, chain, chunk)
+            src = piece.at[pl.ds(c * chunk, chunk)]
+            if inner:
                 copies.append((src.at[:, pl.ds(0, inner)], in_grad.at[row, pl.ds(first, inner)]))
-                if inner < cut:
-                    copies.append((src.at[:, pl.ds(inner, cut - inner)], out_grad.at[row, :]))
-                position += 1
+            if inner < cut:
+                copies.append((src.at[:, pl.ds(inner, cut - inner)], out_grad.at[row, :]))
     copies = [pltpu.make_async_copy(s, d, sems.at[i]) for i, (s, d) in enumerate(copies)]
     for c in copies:
         c.start()
@@ -294,96 +292,135 @@
         c.wait()
 
 
-def place_call(chunk, column, place, pieces, width, grads):
-    count = width // chunk
+def place_call(chunk, spots, place, pieces, width, grads):
     anywhere = pl.BlockSpec(memory_space=HBM)
+    vmem = pl.BlockSpec(memory_space=VMEM)
     return pl.pallas_call(
-        functools.partial(place_kernel, chunk, column),
+        functools.partial(place_kernel, chunk, spots),
         name="place",
         out_shape=(
             jax.ShapeDtypeStruct((width, 4 * width), jnp.float32),
             jax.ShapeDtypeStruct((width, width), jnp.float32),
         ),
-        in_specs=[pl.BlockSpec(memory_space=SMEM)] + [pl.BlockSpec(memory_space=VMEM)] * 8 + [anywhere] * len(grads),
+        in_specs=[pl.BlockSpec(memory_space=SMEM)] + [vmem] * len(pieces) + [anywhere] * len(grads),
         out_specs=(anywhere,) * 2,
-        scratch_shapes=[pltpu.SemaphoreType.DMA((3 * count,))],
-        input_output_aliases={9 + i: i for i in range(len(grads))},
-        compiler_params=pltpu.CompilerParams(vmem_limit_bytes=16 << 20),
+        scratch_shapes=[pltpu.SemaphoreType.DMA((4 * width // chunk,))],
+        input_output_aliases={1 + len(pieces) + i: i for i in range(len(grads))},
+        compiler_params=pltpu.CompilerParams(vmem_limit_bytes=2 << 20),
     )(place, *pieces, *grads)
 
 
-def swap(x, axis, distance):
+def swap(x, where):
+    axis, distance = where
     size = lax.axis_size(axis)
     return lax.ppermute(x, axis, [(i, i ^ distance) for i in range(size)])
 
 
-def orders(table_count):
-    bits = [1 << b for b in range(table_count.bit_length() - 1)]
-    first, rest = bits[:1], bits[1:]
-    cut = len(rest) // 2
-    return first + rest, first + rest[cut:] + rest[:cut]
-
-
-def position(order, index):
+def bits_of(axis):
+    return [(axis, 1 << b) for b in range(lax.axis_size(axis).bit_length() - 1)]
+
+
+def orders():
+    table = bits_of("table")
+    core, rest, z = table[:1], table[1:], bits_of("dp")
+    x, y = rest[: len(rest) // 2], rest[len(rest) // 2 :]
+    z, last = z[:-1], z[-1:]
+    return core + x + y + z + last, core + y + z + x + last, core + z + x + y + last
+
+
+def position(order):
     at = jnp.int32(0)
-    for bit in order:
-        at = 2 * at + (index // bit) % 2
+    for axis, distance in order:
+        at = 2 * at + (lax.axis_index(axis) // distance) % 2
     return at
+
+
+def after(x, *others):
+    return lax.optimization_barrier((x, *others))[0]
+
+
+def apart(*xs):
+    return lax.optimization_barrier(xs)
 
 
 def halve(x):
     n = x.shape[0] // 2
-    return x[:n], x[n:]
-
-
-def reduce_all(keep, send, order_a, order_b, scale):
-    dp_count = lax.axis_size("dp")
-    odd = lax.axis_index("dp") % 2 == 1
-    a, b = halve(keep + swap(send, "table", order_a[0]))
-    for bit_a, bit_b in zip(order_a[1:], order_b[1:]):
-        (a_keep, a_send), (b_keep, b_send) = halve(a), halve(b)
-        a = a_keep + swap(a_send, "table", bit_a)
-        b = b_keep + swap(b_send, "table", bit_b)
-    x = jnp.where(odd, b, a) + swap(jnp.where(odd, a, b), "dp", 1)
-    distance = 2
-    while distance < dp_count:
-        x = x + swap(x, "dp", distance)
-        distance *= 2
-    x = x * scale
-    other = swap(x, "dp", 1)
-    a, b = jnp.where(odd, other, x), jnp.where(odd, x, other)
-    for bit_a, bit_b in zip(order_a[:1:-1], order_b[:1:-1]):
-        a = jnp.concatenate([a, swap(a, "table", bit_a)], axis=0)
-        b = jnp.concatenate([b, swap(b, "table", bit_b)], axis=0)
-    pieces = []
-    for x, bit in ((a, order_a[1]), (b, order_b[1])):
-        far = swap(x, "table", bit)
-        pieces += [x, far, swap(x, "table", order_a[0]), swap(far, "table", order_a[0])]
-    return pieces
+    return apart(x[:n], x[n:])
+
+
+def exchange(keep, send, order, scale):
+    x = keep + (yield swap(send, order[0]))
+    for where in order[1:-1]:
+        keep, send = halve(x)
+        x = keep + (yield swap(send, where))
+    x = (x + (yield swap(x, order[-1]))) * scale
+    for where in order[-2:1:-1]:
+        (x,) = apart(x)
+        x = jnp.concatenate([x, (yield swap(x, where))], axis=0)
+    (x,) = apart(x)
+    return x, swap(x, order[1]), swap(x, order[0])
+
+
+class Run:
+    def __init__(self, steps):
+        self.steps, self.count, self.pieces, self.last = steps, 0, None, ()
+        self.waiting = next(steps)
+
+    def advance(self, *others):
+        here = after(self.waiting, *others)
+        self.count, self.last = self.count + 1, (here,)
+        try:
+            self.waiting = self.steps.send(here)
+        except StopIteration as stop:
+            self.pieces = stop.value
+
+
+CUTS = 8, 7, 5
+ITEMS_AT, SENT_AT, GOT_AT, TABLE_AT, STRICT = 1, 1, 3, 4, 1
 
 
 def per_device(item_emb, cotangent, in_proj, out_proj, history_lengths, item_ids):
     rows_here, width = item_emb.shape
-    table_count = lax.axis_size("table")
-    owners = lax.axis_size("dp") * table_count
+    owners = lax.axis_size("dp") * lax.axis_size("table")
     slots = max(8, rows_here // owners)
-    order_a, order_b = orders(table_count)
-    table_index = lax.axis_index("table")
-    place = jnp.stack([position(order_a, table_index), position(order_b, table_index)])
-    chunk = width // table_count
+    order = orders()
+    place = jnp.stack([position(o[:-1]) for o in order])
+    chunk = width >> (len(order[0]) - 1)
     scale = 1.0 / math.sqrt(rows_here * owners)
-
-    keep_e, send_e, grad_pre, *rel = block_call(
-        chunk, place, history_lengths, item_emb, cotangent, in_proj, out_proj
+    cuts = [c * 5 * width // 20 for c in CUTS]
+
+    *p, grad_pre, rel_q, rel_r, rel_g = block_call(
+        chunk, cuts[0], place, history_lengths, item_emb, cotangent, in_proj, out_proj
     )
-    keep_f, send_f = second_call(*rel, cotangent, grad_pre)
-    sent = item_call(owners, slots, item_ids.reshape(1, rows_here), cotangent, grad_pre, in_proj)
-    got = lax.all_to_all(sent, ("dp", "table"), split_axis=0, concat_axis=0, tiled=True)
-    pieces_e = reduce_all(keep_e, send_e, order_a, order_b, scale)
-    pieces_f = reduce_all(keep_f, send_f, order_a, order_b, scale)
-    grads = place_call(chunk, 0, place, pieces_e, width, ())
-    in_grad, out_grad = place_call(chunk, 2 * keep_e.shape[1], place, pieces_f, width, grads)
-    emb_grad = table_call(owners, slots, got, width)
+    q_keep, q_send, *r = rest_call(cuts, rel_q, rel_r, rel_g, cotangent, grad_pre)
+    runs = [Run(exchange(*x, o, scale)) for x, o in zip((p, (q_keep, q_send), r), order)]
+    hold, got, emb_grad = (), None, None
+    while runs[-1].pieces is None:
+        step = runs[0].count
+        if step == ITEMS_AT:
+            sent = item_call(owners, slots, item_ids.reshape(1, rows_here), cotangent, grad_pre, in_proj)
+            hold = (sent,)
+        if step == SENT_AT:
+            got = lax.all_to_all(after(sent, *(runs[0].last if SENT_AT > ITEMS_AT else ())), ("dp", "table"), split_axis=0, concat_axis=0, tiled=True)
+        if step == TABLE_AT:
+            emb_grad = table_call(owners, slots, after(got, *runs[0].last), width)
+            hold = (emb_grad,)
+        if step == GOT_AT:
+            hold = (got,)
+        for run in runs:
+            run.advance(*hold)
+            hold = run.last if step >= STRICT else hold
+        hold = hold if step >= STRICT else ()
+    if emb_grad is None:
+        emb_grad = table_call(owners, slots, got, width)
+    near, far, beside = zip(*(run.pieces for run in runs))
+    firsts = [sum(cuts[:chain]) for chain in range(len(cuts))]
+    quarter = width // chunk // 4
+    spots = lambda at: [(chain, first, at * quarter) for chain, first in enumerate(firsts)]
+    grads = place_call(chunk, spots(0) + spots(2), place, near + beside, width, ())
+    far = [after(x, *grads, emb_grad) for x in far]
+    across = [swap(x, o[0]) for x, o in zip(far, order)]
+    in_grad, out_grad = place_call(chunk, spots(1) + spots(3), place, far + across, width, grads)
     return (emb_grad, in_grad, out_grad)
 
 

time: 142 us -> 115 us (0.81)
  waiting for transfers between devices: 69.2 us -> 45.1 us
  local copies, waits for them, and re-layouts: 8.41 us -> 1.87 us
  starting transfers between devices: 37.1 us -> 38.7 us
    ppermute x32 -> x30, waiting for transfers between devices: 69.2 us -> 45.1 us  [swap(): return lax.ppermute(x, axis, [(i, i ^ distance) for i in range(size)])]
    unnamed x34 -> x12, local copies, waits for them, and re-layouts: 8.31 us -> 1.52 us
    all_to_all x1, starting transfers between devices: 4.89 us -> 7.15 us  [per_device(): lax.all_to_all(after(sent, *(runs[0].last if SENT_AT > ITEMS_AT else ()))...]
    add x8 -> x12, other arithmetic: 3.32 us -> 4.14 us  [the longest x3 3.86 us: exchange(): x = keep + (yield swap(send, order[0]))]
    ppermute x32 -> x30, starting transfers between devices: 32.2 us -> 31.5 us  [swap(): return lax.ppermute(x, axis, [(i, i ^ distance) for i in range(size)])]
  transfers between devices with their start and end apart: 33 -> 31, of which waited for: 17 -> 14; matrix products, arithmetic and copies ran while one was open for 3% -> 4% of each run, Pallas kernels for 6% -> 9%
where the time goes in v4:
time: 115 us
  waiting for transfers between devices  45.1 us (39%)
  starting transfers between devices  38.7 us (34%)
  Pallas kernels  23.7 us (21%)
  other arithmetic  4.41 us (4%)
  local copies, waits for them, and re-layouts  1.87 us (2%)
    ppermute x30, waiting for transfers between devices, swap(): return lax.ppermute(x, axis, [(i, i ^ distance) for i in range(size)])  45.1 us
    ppermute x30, starting transfers between devices, swap(): return lax.ppermute(x, axis, [(i, i ^ distance) for i in range(size)])  31.5 us
    pallas_call x1, Pallas kernels, block_call(): pl.pallas_call(functools.partial(block_kernel, chunk), name='block', out_...  10.6 us
    all_to_all x1, starting transfers between devices, per_device(): lax.all_to_all(after(sent, *(runs[0].last if SENT_AT > ITEMS_AT else ()))...  7.15 us
    pallas_call x2, Pallas kernels, place_call(): pl.pallas_call(functools.partial(place_kernel, chunk, spots), name='place...  5.15 us
    add x3, other arithmetic, exchange(): x = keep + (yield swap(send, order[0]))  3.86 us
    pallas_call x1, Pallas kernels, item_call(): pl.pallas_call(functools.partial(item_kernel, owners, slots), name='items...  3.3 us
    pallas_call x1, Pallas kernels, table_call(): pl.pallas_call(functools.partial(table_kernel, owners, slots), name='tabl...  2.77 us
  transfers between devices with their start and end apart: 31, of which 14 were waited for; matrix products, arithmetic and copies ran while one was open for 4% of the time, Pallas kernels for 9%

profile of v4, /device:TPU:0, one launch (start us, length us, event | category | flops | bytes accessed | tf_op | source)
XLA Modules:
  0.0 114.9 jit_solution(13932248863318578650)
XLA Ops:
  0.6 0.0 copy-start.1
  0.7 0.1 pad_add_fusion.place
  0.8 0.7 copy-done.5
  1.4 10.6 %block.1 = (f32[256,1024]{1,0:T(8,128)S(1)}, f32[256,1024]{1,0:T(8,128)}, bf16[512,2048]{1,0:T(8,128)(2,1)S(1)}, bf16[512,512]{1,0:T(8,128)(2,1)S(1)}, bf16[512,...) custom-call(s32[3]{0:T(128)S(1)} %pad_add_fusion.place, s32[1,8]{1,0:T(1,128)S(1)} %copy-done.5, ...), custom_call_target="tpu_custom_call" | custom-call | tf_op jit(solution)/shard_map/block/pallas_call | solution.py:150
  12.0 0.5 collective-permute-start
  12.6 2.0 %rest.1 = (f32[256,896]{1,0:T(8,128)S(1)}, f32[256,896]{1,0:T(8,128)}, f32[256,640]{1,0:T(8,128)S(1)}, f32[256,640]{1,0:T(8,128)}) custom-call(bf16[512,512]{1,0:T(8,128)(2,1)S(1)} %get-tuple-element.65.rel_q, bf16[512,512]{1,0:T(8,128)(2,1)S(1)} %get-tuple-element.66.rel_r, bf16[512,512]{1,0:T(8,128)(2,1)S(1)} %get-tuple-element.67.rel_g, ...), custom_call_target="tpu_custom_call" | custom-call | tf_op jit(solution)/shard_map/rest/pallas_call | solution.py:191
  14.5 0.8 copy-done.2
  15.4 0.0 collective-permute-start.5
  15.4 0.5 collective-permute-start.3
  15.9 3.3 %items.1 = f32[32,72,128]{2,1,0:T(8,128)} custom-call(s32[1,512]{1,0:T(1,128)S(1)} %bitcast.4, bf16[512,512]{1,0:T(8,128)(2,1)S(1)} %copy-done.1, bf16[512,2048]{1,0:T(8,128)(2,1)S(1)} %get-tuple-element.57.grad_pre, bf16[512,2048]{1,0:T(8,128)(2,1)S(1)} %copy-done), custom_call_target="tpu_custom_call" | custom-call | tf_op jit(solution)/shard_map/items/pallas_call | solution.py:239
  19.2 7.2 %all-to-all-start = ((f32[32,72,128]{2,1,0:T(8,128)}), f32[32,72,128]{2,1,0:T(8,128)S(1)}, u32[]{:S(2)}, u32[]{:S(2)}) async-start(f32[32,72,128]{2,1,0:T(8,128)} %items.1), calls=%async_computation | async-start | bytes 2359296 | tf_op jit(solution)/shard_map/all_to_all | solution.py:404
  26.4 0.0 collective-permute-done
  26.4 1.4 %add.110 = f32[256,1024]{1,0:T(8,128)S(1)} add(f32[256,1024]{1,0:T(8,128)S(1)} %get-tuple-element.58, f32[256,1024]{1,0:T(8,128)} %collective-permute-done) | non-fusion elementwise | flops 262144 | bytes 3145728 | tf_op jit(solution)/shard_map/add | solution.py:352
  27.8 0.1 fusion
  27.9 1.7 %collective-permute-start.1 = (f32[128,1024]{1,0:T(8,128)S(1)}, f32[128,1024]{1,0:T(8,128)S(1)}, u32[]{:S(2)}, u32[]{:S(2)}) collective-permute-start(f32[128,1024]{1,0:T(8,128)S(1)} %get-tuple-element.61), channel_id=1, source_target_pairs={{0,2},{1,3},{2,0},{3,1},{4,6},{5,7},{6,4},{7,5},{8,10},{9,11},{10,... | collective-permute-start | bytes 1572872 | tf_op jit(solution)/shard_map/ppermute | solution.py:316
  29.6 1.2 %add.112 = f32[256,640]{1,0:T(8,128)S(1)} add(f32[256,640]{1,0:T(8,128)S(1)} %copy-done.3, f32[256,640]{1,0:T(8,128)} %collective-permute-done.3) | non-fusion elementwise | flops 163840 | bytes 1966080 | tf_op jit(solution)/shard_map/add | solution.py:352
  30.7 1.3 %add.113 = f32[256,896]{1,0:T(8,128)S(1)} add(f32[256,896]{1,0:T(8,128)S(1)} %get-tuple-element.71, f32[256,896]{1,0:T(8,128)} %collective-permute-done.5) | non-fusion elementwise | flops 229376 | bytes 2752512 | tf_op jit(solution)/shard_map/add | solution.py:352
  32.0 0.1 fusion.1
  32.1 1.5 %collective-permute-start.6 = (f32[128,896]{1,0:T(8,128)S(1)}, f32[128,896]{1,0:T(8,128)S(1)}, u32[]{:S(2)}, u32[]{:S(2)}) collective-permute-start(f32[128,896]{1,0:T(8,128)S(1)} %get-tuple-element.73), channel_id=1, source_target_pairs={{0,4},{1,5},{2,6},{3,7},{4,0},{5,1},{6,2},{7,3},{8,12},{9,13},{10,... | collective-permute-start | bytes 1376264 | tf_op jit(solution)/shard_map/ppermute | solution.py:316
  33.7 1.5 %collective-permute-start.4 = (f32[128,640]{1,0:T(8,128)S(1)}, f32[128,640]{1,0:T(8,128)S(1)}, u32[]{:S(2)}, u32[]{:S(2)}) collective-permute-start(f32[128,640]{1,0:T(8,128)S(1)} %get-tuple-element.70), channel_id=1, source_target_pairs={{0,8},{8,0},{16,24},{24,16},{1,9},{9,1},{17,25},{25,17},{2,10},{10... | collective-permute-start | bytes 983048 | tf_op jit(solution)/shard_map/ppermute | solution.py:316
  35.2 16.3 %collective-permute-done.1 = f32[128,1024]{1,0:T(8,128)S(1)} collective-permute-done((f32[128,1024]{1,0:T(8,128)S(1)}, f32[128,1024]{1,0:T(8,128)S(1)}, u32[]{:S(2)}, u32[]{:S(2)}) %collective-permute-start.1) | collective-permute-done | bytes 524320 | tf_op jit(solution)/shard_map/ppermute | solution.py:316
  51.5 0.1 add.111
  51.7 2.3 %collective-permute-start.2 = (f32[64,1024]{1,0:T(8,128)S(1)}, f32[64,1024]{1,0:T(8,128)S(1)}, u32[]{:S(2)}, u32[]{:S(2)}) collective-permute-start(f32[64,1024]{1,0:T(8,128)S(1)} %get-tuple-element.64), channel_id=1, source_target_pairs={{0,4},{1,5},{2,6},{3,7},{4,0},{5,1},{6,2},{7,3},{8,12},{9,13},{10,... | collective-permute-start | bytes 786440 | tf_op jit(solution)/shard_map/ppermute | solution.py:316
  54.0 0.1 add.118
  54.1 0.0 collective-permute-done.4
  54.2 1.3 %collective-permute-start.10 = (f32[64,640]{1,0:T(8,128)S(1)}, f32[64,640]{1,0:T(8,128)S(1)}, u32[]{:S(2)}, u32[]{:S(2)}) collective-permute-start(f32[64,640]{1,0:T(8,128)S(1)} %get-tuple-element.84), channel_id=1, source_target_pairs={{0,2},{1,3},{2,0},{3,1},{4,6},{5,7},{6,4},{7,5},{8,10},{9,11},{10,... | collective-permute-start | bytes 491528 | tf_op jit(solution)/shard_map/ppermute | solution.py:316
  55.4 1.8 %collective-permute-start.11 = (f32[64,896]{1,0:T(8,128)S(1)}, f32[64,896]{1,0:T(8,128)S(1)}, u32[]{:S(2)}, u32[]{:S(2)}) collective-permute-start(f32[64,896]{1,0:T(8,128)S(1)} %get-tuple-element.86), channel_id=1, source_target_pairs={{0,8},{8,0},{16,24},{24,16},{1,9},{9,1},{17,25},{25,17},{2,10},{10... | collective-permute-start | bytes 688136 | tf_op jit(solution)/shard_map/ppermute | solution.py:316
  57.2 2.4 %collective-permute-done.2 = f32[64,1024]{1,0:T(8,128)S(1)} collective-permute-done((f32[64,1024]{1,0:T(8,128)S(1)}, f32[64,1024]{1,0:T(8,128)S(1)}, u32[]{:S(2)}, u32[]{:S(2)}) %collective-permute-start.2) | collective-permute-done | bytes 262176 | tf_op jit(solution)/shard_map/ppermute | solution.py:316
  59.7 1.9 %collective-permute-start.7 = (f32[32,1024]{1,0:T(8,128)S(1)}, f32[32,1024]{1,0:T(8,128)S(1)}, u32[]{:S(2)}, u32[]{:S(2)}) collective-permute-start(f32[32,1024]{1,0:T(8,128)S(1)} %get-tuple-element.77), channel_id=1, source_target_pairs={{0,8},{8,0},{16,24},{24,16},{1,9},{9,1},{17,25},{25,17},{2,10},{10... | collective-permute-start | bytes 393224 | tf_op jit(solution)/shard_map/ppermute | solution.py:316
  61.6 1.2 %collective-permute-done.11 = f32[64,896]{1,0:T(8,128)S(1)} collective-permute-done((f32[64,896]{1,0:T(8,128)S(1)}, f32[64,896]{1,0:T(8,128)S(1)}, u32[]{:S(2)}, u32[]{:S(2)}) %collective-permute-start.11) | collective-permute-done | bytes 229408 | tf_op jit(solution)/shard_map/ppermute | solution.py:316
  62.8 0.0 collective-permute-done.10
  62.8 0.1 collective-permute-start.13
  63.0 2.2 %collective-permute-done.7 = f32[32,1024]{1,0:T(8,128)S(1)} collective-permute-done((f32[32,1024]{1,0:T(8,128)S(1)}, f32[32,1024]{1,0:T(8,128)S(1)}, u32[]{:S(2)}, u32[]{:S(2)}) %collective-permute-start.7) | collective-permute-done | bytes 131104 | tf_op jit(solution)/shard_map/ppermute | solution.py:316
  65.2 3.6 %collective-permute-start.8 = (f32[32,1024]{1,0:T(8,128)S(1)}, f32[32,1024]{1,0:T(8,128)S(1)}, u32[]{:S(2)}, u32[]{:S(2)}) collective-permute-start(f32[32,1024]{1,0:T(8,128)S(1)} %add.115), channel_id=1, source_target_pairs={{0,16},{8,24},{16,0},{24,8},{1,17},{9,25},{17,1},{25,9},{2,18},{10... | collective-permute-start | bytes 393224 | tf_op jit(solution)/shard_map/ppermute | solution.py:316
  68.8 1.6 %collective-permute-start.12 = (f32[32,640]{1,0:T(8,128)S(1)}, f32[32,640]{1,0:T(8,128)S(1)}, u32[]{:S(2)}, u32[]{:S(2)}) collective-permute-start(f32[32,640]{1,0:T(8,128)S(1)} %get-tuple-element.90), channel_id=1, source_target_pairs={{0,4},{1,5},{2,6},{3,7},{4,0},{5,1},{6,2},{7,3},{8,12},{9,13},{10,... | collective-permute-start | bytes 245768 | tf_op jit(solution)/shard_map/ppermute | solution.py:316
  70.4 2.9 %collective-permute-done.12 = f32[32,640]{1,0:T(8,128)S(1)} collective-permute-done((f32[32,640]{1,0:T(8,128)S(1)}, f32[32,640]{1,0:T(8,128)S(1)}, u32[]{:S(2)}, u32[]{:S(2)}) %collective-permute-start.12) | collective-permute-done | bytes 81952 | tf_op jit(solution)/shard_map/ppermute | solution.py:316
  73.4 0.1 collective-permute-start.14
  73.4 2.9 %collective-permute-start.15 = (f32[32,896]{1,0:T(8,128)S(1)}, f32[32,896]{1,0:T(8,128)S(1)}, u32[]{:S(2)}, u32[]{:S(2)}) collective-permute-start(f32[32,896]{1,0:T(8,128)S(1)} %add.122), channel_id=1, source_target_pairs={{0,16},{8,24},{16,0},{24,8},{1,17},{9,25},{17,1},{25,9},{2,18},{10... | collective-permute-start | bytes 344072 | tf_op jit(solution)/shard_map/ppermute | solution.py:316
  76.3 2.8 %table.1 = f32[1024,512]{1,0:T(8,128)} custom-call(f32[32,72,128]{2,1,0:T(8,128)S(1)} %all-to-all-done.got), custom_call_target="tpu_custom_call" | custom-call | tf_op jit(solution)/shard_map/table/pallas_call | solution.py:265
  79.1 3.5 %collective-permute-done.15 = f32[32,896]{1,0:T(8,128)S(1)} collective-permute-done((f32[32,896]{1,0:T(8,128)S(1)}, f32[32,896]{1,0:T(8,128)S(1)}, u32[]{:S(2)}, u32[]{:S(2)}) %collective-permute-start.15) | collective-permute-done | bytes 114720 | tf_op jit(solution)/shard_map/ppermute | solution.py:316
  82.7 0.0 collective-permute-done.14
  82.7 0.1 collective-permute-start.9
  82.8 1.7 %collective-permute-start.17 = (f32[32,640]{1,0:T(8,128)S(1)}, f32[32,640]{1,0:T(8,128)S(1)}, u32[]{:S(2)}, u32[]{:S(2)}) collective-permute-start(f32[32,640]{1,0:T(8,128)S(1)} %add_multiply_fusion.2), channel_id=1, source_target_pairs={{0,4},{1,5},{2,6},{3,7},{4,0},{5,1},{6,2},{7,3},{8,12},{9,13},{10,... | collective-permute-start | bytes 245768 | tf_op jit(solution)/shard_map/ppermute | solution.py:316
  84.5 0.6 collective-permute-start.18
  85.1 2.6 %collective-permute-done.9 = f32[32,1024]{1,0:T(8,128)S(1)} collective-permute-done((f32[32,1024]{1,0:T(8,128)S(1)}, f32[32,1024]{1,0:T(8,128)S(1)}, u32[]{:S(2)}, u32[]{:S(2)}) %collective-permute-start.9) | collective-permute-done | bytes 131104 | tf_op jit(solution)/shard_map/ppermute | solution.py:316
  87.7 1.7 %collective-permute-start.16 = (f32[64,1024]{1,0:T(8,128)S(1)}, f32[64,1024]{1,0:T(8,128)S(1)}, u32[]{:S(2)}, u32[]{:S(2)}) collective-permute-start(f32[64,1024]{1,0:T(8,128)S(1)} %pad_maximum_fusion.3), channel_id=1, source_target_pairs={{0,4},{1,5},{2,6},{3,7},{4,0},{5,1},{6,2},{7,3},{8,12},{9,13},{10,... | collective-permute-start | bytes 786440 | tf_op jit(solution)/shard_map/ppermute | solution.py:316
  89.5 1.9 %collective-permute-start.20 = (f32[64,896]{1,0:T(8,128)S(1)}, f32[64,896]{1,0:T(8,128)S(1)}, u32[]{:S(2)}, u32[]{:S(2)}) collective-permute-start(f32[64,896]{1,0:T(8,128)S(1)} %pad_maximum_fusion.4), channel_id=1, source_target_pairs={{0,8},{8,0},{16,24},{24,16},{1,9},{9,1},{17,25},{25,17},{2,10},{10... | collective-permute-start | bytes 688136 | tf_op jit(solution)/shard_map/ppermute | solution.py:316
  91.4 0.7 collective-permute-start.21
  92.1 2.1 %collective-permute-done.16 = f32[64,1024]{1,0:T(8,128)S(1)} collective-permute-done((f32[64,1024]{1,0:T(8,128)S(1)}, f32[64,1024]{1,0:T(8,128)S(1)}, u32[]{:S(2)}, u32[]{:S(2)}) %collective-permute-start.16) | collective-permute-done | bytes 262176 | tf_op jit(solution)/shard_map/ppermute | solution.py:316
  94.2 0.1 collective-permute-start.22
  94.3 1.1 collective-permute-start.19
  95.4 0.1 collective-permute-done.20
  95.6 1.2 %collective-permute-done.21 = f32[64,640]{1,0:T(8,128)S(1)} collective-permute-done((f32[64,640]{1,0:T(8,128)S(1)}, f32[64,640]{1,0:T(8,128)S(1)}, u32[]{:S(2)}, u32[]{:S(2)}) %collective-permute-start.21) | collective-permute-done | bytes 163872 | tf_op jit(solution)/shard_map/ppermute | solution.py:316
  96.8 0.1 collective-permute-start.23
  96.9 0.5 collective-permute-start.24
  97.4 0.5 collective-permute-start.25
  97.9 1.3 %collective-permute-done.24.refs_5_ = f32[128,640]{1,0:T(8,128)S(1)} collective-permute-done((f32[128,640]{1,0:T(8,128)S(1)}, f32[128,640]{1,0:T(8,128)S(1)}, u32[]{:S(2)}, u32[]{:S(2)}) %collective-permute-start.24) | collective-permute-done | bytes 327712 | tf_op jit(solution)/shard_map/ppermute | solution.py:316
  99.1 0.7 collective-permute-start.26
  99.8 2.6 %place.2 = (f32[512,2048]{1,0:T(8,128)}, f32[512,512]{1,0:T(8,128)}) custom-call(s32[3]{0:T(128)S(1)} %pad_add_fusion.place, f32[128,1024]{1,0:T(8,128)S(1)} %pad_maximum_fusion.refs_0_, f32[128,896]{1,0:T(8,128)S(1)} %pad_maximum_fusion.1.refs_1_, f32[128,640]{1,0:T(8,128)S(1)} %pad_maximum_fusion.2.refs_2_, ...), custom_call_target="tpu_custom_call" | custom-call | tf_op jit(solution)/shard_map/place/pallas_call | solution.py:298
  102.4 6.2 %collective-permute-done.19.refs_0_ = f32[128,1024]{1,0:T(8,128)S(1)} collective-permute-done((f32[128,1024]{1,0:T(8,128)S(1)}, f32[128,1024]{1,0:T(8,128)S(1)}, u32[]{:S(2)}, u32[]{:S(2)}) %collective-permute-start.19) | collective-permute-done | bytes 524320 | tf_op jit(solution)/shard_map/ppermute | solution.py:316
  108.6 1.2 %collective-permute-done.25.refs_1_ = f32[128,896]{1,0:T(8,128)S(1)} collective-permute-done((f32[128,896]{1,0:T(8,128)S(1)}, f32[128,896]{1,0:T(8,128)S(1)}, u32[]{:S(2)}, u32[]{:S(2)}) %collective-permute-start.25) | collective-permute-done | bytes 458784 | tf_op jit(solution)/shard_map/ppermute | solution.py:316
  109.9 0.5 collective-permute-start.29
  110.4 1.8 %collective-permute-done.29.refs_5_ = f32[128,640]{1,0:T(8,128)S(1)} collective-permute-done((f32[128,640]{1,0:T(8,128)S(1)}, f32[128,640]{1,0:T(8,128)S(1)}, u32[]{:S(2)}, u32[]{:S(2)}) %collective-permute-start.29) | collective-permute-done | bytes 327712 | tf_op jit(solution)/shard_map/ppermute | solution.py:316
  112.2 2.6 %place.3 = (f32[512,2048]{1,0:T(8,128)}, f32[512,512]{1,0:T(8,128)}) custom-call(s32[3]{0:T(128)S(1)} %pad_add_fusion.place, f32[128,1024]{1,0:T(8,128)S(1)} %collective-permute-done.19.refs_0_, f32[128,896]{1,0:T(8,128)S(1)} %collective-permute-done.25.refs_1_, ...), custom_call_target="tpu_custom_call", output_to_operand_aliasing={{0}: (7, {}), {1}: (8, {})} | custom-call | tf_op jit(solution)/shard_map/place/pallas_call | solution.py:298
  (47 shorter events, 0.6 us)
Async XLA Ops:
  0.6 11.9 %copy-start.1 = (bf16[512,512]{1,0:T(8,128)(2,1)S(1)}, bf16[512,512]{1,0:T(8,128)(2,1)}, u32[]{:S(2)}) copy-start(bf16[512,512]{1,0:T(8,128)(2,1)} %cot.3) | copy-start | bytes 1572868
  0.8 0.7 copy-start.5
  12.0 14.3 %collective-permute-start = (f32[256,1024]{1,0:T(8,128)}, f32[256,1024]{1,0:T(8,128)}, u32[]{:S(2)}, u32[]{:S(2)}) collective-permute-start(f32[256,1024]{1,0:T(8,128)} %get-tuple-element.59), channel_id=1, source_target_pairs={{0,1},{1,0},{2,3},{3,2},{4,5},{5,4},{6,7},{7,6},{8,9},{9,8},{10,11... | collective-permute-start | bytes 3145736 | tf_op jit(solution)/shard_map/ppermute | solution.py:316
  12.6 3.3 %copy-start = (bf16[512,2048]{1,0:T(8,128)(2,1)S(1)}, bf16[512,2048]{1,0:T(8,128)(2,1)}, u32[]{:S(2)}) copy-start(bf16[512,2048]{1,0:T(8,128)(2,1)} %in_proj.1) | copy-start | bytes 6291460
  12.6 3.3 %copy-start.4 = (s32[512]{0:T(512)S(1)}, s32[512]{0:T(512)}, u32[]{:S(2)}) copy-start(s32[512]{0:T(512)} %param.11) | copy-start | bytes 6148
  14.5 0.8 copy-start.2
  15.4 15.4 %collective-permute-start.5 = (f32[256,896]{1,0:T(8,128)}, f32[256,896]{1,0:T(8,128)}, u32[]{:S(2)}, u32[]{:S(2)}) collective-permute-start(f32[256,896]{1,0:T(8,128)} %get-tuple-element.72), channel_id=1, source_target_pairs={{0,1},{1,0},{2,3},{3,2},{4,5},{5,4},{6,7},{7,6},{8,9},{9,8},{10,11... | collective-permute-start | bytes 2752520 | tf_op jit(solution)/shard_map/ppermute | solution.py:316
  15.4 14.2 %collective-permute-start.3 = (f32[256,640]{1,0:T(8,128)}, f32[256,640]{1,0:T(8,128)}, u32[]{:S(2)}, u32[]{:S(2)}) collective-permute-start(f32[256,640]{1,0:T(8,128)} %get-tuple-element.69), channel_id=1, source_target_pairs={{0,1},{1,0},{2,3},{3,2},{4,5},{5,4},{6,7},{7,6},{8,9},{9,8},{10,11... | collective-permute-start | bytes 1966088 | tf_op jit(solution)/shard_map/ppermute | solution.py:316
  19.2 46.0 %all-to-all-start = ((f32[32,72,128]{2,1,0:T(8,128)}), f32[32,72,128]{2,1,0:T(8,128)S(1)}, u32[]{:S(2)}, u32[]{:S(2)}) async-start(f32[32,72,128]{2,1,0:T(8,128)} %items.1), calls=%async_computation | async-start | bytes 2359296 | tf_op jit(solution)/shard_map/all_to_all | solution.py:404
  26.4 3.2 %copy-start.3 = (f32[256,640]{1,0:T(8,128)S(1)}, f32[256,640]{1,0:T(8,128)}, u32[]{:S(2)}) copy-start(f32[256,640]{1,0:T(8,128)} %copy-done.2) | copy-start | bytes 1966084
  27.9 23.6 %collective-permute-start.1 = (f32[128,1024]{1,0:T(8,128)S(1)}, f32[128,1024]{1,0:T(8,128)S(1)}, u32[]{:S(2)}, u32[]{:S(2)}) collective-permute-start(f32[128,1024]{1,0:T(8,128)S(1)} %get-tuple-element.61), channel_id=1, source_target_pairs={{0,2},{1,3},{2,0},{3,1},{4,6},{5,7},{6,4},{7,5},{8,10},{9,11},{10,... | collective-permute-start | bytes 1572872 | tf_op jit(solution)/shard_map/ppermute | solution.py:316
  32.1 21.9 %collective-permute-start.6 = (f32[128,896]{1,0:T(8,128)S(1)}, f32[128,896]{1,0:T(8,128)S(1)}, u32[]{:S(2)}, u32[]{:S(2)}) collective-permute-start(f32[128,896]{1,0:T(8,128)S(1)} %get-tuple-element.73), channel_id=1, source_target_pairs={{0,4},{1,5},{2,6},{3,7},{4,0},{5,1},{6,2},{7,3},{8,12},{9,13},{10,... | collective-permute-start | bytes 1376264 | tf_op jit(solution)/shard_map/ppermute | solution.py:316
  33.7 20.4 %collective-permute-start.4 = (f32[128,640]{1,0:T(8,128)S(1)}, f32[128,640]{1,0:T(8,128)S(1)}, u32[]{:S(2)}, u32[]{:S(2)}) collective-permute-start(f32[128,640]{1,0:T(8,128)S(1)} %get-tuple-element.70), channel_id=1, source_target_pairs={{0,8},{8,0},{16,24},{24,16},{1,9},{9,1},{17,25},{25,17},{2,10},{10... | collective-permute-start | bytes 983048 | tf_op jit(solution)/shard_map/ppermute | solution.py:316
  51.7 7.9 %collective-permute-start.2 = (f32[64,1024]{1,0:T(8,128)S(1)}, f32[64,1024]{1,0:T(8,128)S(1)}, u32[]{:S(2)}, u32[]{:S(2)}) collective-permute-start(f32[64,1024]{1,0:T(8,128)S(1)} %get-tuple-element.64), channel_id=1, source_target_pairs={{0,4},{1,5},{2,6},{3,7},{4,0},{5,1},{6,2},{7,3},{8,12},{9,13},{10,... | collective-permute-start | bytes 786440 | tf_op jit(solution)/shard_map/ppermute | solution.py:316
  54.2 8.7 %collective-permute-start.10 = (f32[64,640]{1,0:T(8,128)S(1)}, f32[64,640]{1,0:T(8,128)S(1)}, u32[]{:S(2)}, u32[]{:S(2)}) collective-permute-start(f32[64,640]{1,0:T(8,128)S(1)} %get-tuple-element.84), channel_id=1, source_target_pairs={{0,2},{1,3},{2,0},{3,1},{4,6},{5,7},{6,4},{7,5},{8,10},{9,11},{10,... | collective-permute-start | bytes 491528 | tf_op jit(solution)/shard_map/ppermute | solution.py:316
  55.4 7.3 %collective-permute-start.11 = (f32[64,896]{1,0:T(8,128)S(1)}, f32[64,896]{1,0:T(8,128)S(1)}, u32[]{:S(2)}, u32[]{:S(2)}) collective-permute-start(f32[64,896]{1,0:T(8,128)S(1)} %get-tuple-element.86), channel_id=1, source_target_pairs={{0,8},{8,0},{16,24},{24,16},{1,9},{9,1},{17,25},{25,17},{2,10},{10... | collective-permute-start | bytes 688136 | tf_op jit(solution)/shard_map/ppermute | solution.py:316
  59.7 5.5 %collective-permute-start.7 = (f32[32,1024]{1,0:T(8,128)S(1)}, f32[32,1024]{1,0:T(8,128)S(1)}, u32[]{:S(2)}, u32[]{:S(2)}) collective-permute-start(f32[32,1024]{1,0:T(8,128)S(1)} %get-tuple-element.77), channel_id=1, source_target_pairs={{0,8},{8,0},{16,24},{24,16},{1,9},{9,1},{17,25},{25,17},{2,10},{10... | collective-permute-start | bytes 393224 | tf_op jit(solution)/shard_map/ppermute | solution.py:316
  62.8 7.6 %collective-permute-start.13 = (f32[32,896]{1,0:T(8,128)S(1)}, f32[32,896]{1,0:T(8,128)S(1)}, u32[]{:S(2)}, u32[]{:S(2)}) collective-permute-start(f32[32,896]{1,0:T(8,128)S(1)} %get-tuple-element.92), channel_id=1, source_target_pairs={{0,2},{1,3},{2,0},{3,1},{4,6},{5,7},{6,4},{7,5},{8,10},{9,11},{10,... | collective-permute-start | bytes 344072 | tf_op jit(solution)/shard_map/ppermute | solution.py:316
  65.2 13.9 %collective-permute-start.8 = (f32[32,1024]{1,0:T(8,128)S(1)}, f32[32,1024]{1,0:T(8,128)S(1)}, u32[]{:S(2)}, u32[]{:S(2)}) collective-permute-start(f32[32,1024]{1,0:T(8,128)S(1)} %add.115), channel_id=1, source_target_pairs={{0,16},{8,24},{16,0},{24,8},{1,17},{9,25},{17,1},{25,9},{2,18},{10... | collective-permute-start | bytes 393224 | tf_op jit(solution)/shard_map/ppermute | solution.py:316
  68.8 4.5 %collective-permute-start.12 = (f32[32,640]{1,0:T(8,128)S(1)}, f32[32,640]{1,0:T(8,128)S(1)}, u32[]{:S(2)}, u32[]{:S(2)}) collective-permute-start(f32[32,640]{1,0:T(8,128)S(1)} %get-tuple-element.90), channel_id=1, source_target_pairs={{0,4},{1,5},{2,6},{3,7},{4,0},{5,1},{6,2},{7,3},{8,12},{9,13},{10,... | collective-permute-start | bytes 245768 | tf_op jit(solution)/shard_map/ppermute | solution.py:316
  73.4 9.3 %collective-permute-start.14 = (f32[32,640]{1,0:T(8,128)S(1)}, f32[32,640]{1,0:T(8,128)S(1)}, u32[]{:S(2)}, u32[]{:S(2)}) collective-permute-start(f32[32,640]{1,0:T(8,128)S(1)} %add.121), channel_id=1, source_target_pairs={{0,16},{8,24},{16,0},{24,8},{1,17},{9,25},{17,1},{25,9},{2,18},{10... | collective-permute-start | bytes 245768 | tf_op jit(solution)/shard_map/ppermute | solution.py:316
  73.4 9.2 %collective-permute-start.15 = (f32[32,896]{1,0:T(8,128)S(1)}, f32[32,896]{1,0:T(8,128)S(1)}, u32[]{:S(2)}, u32[]{:S(2)}) collective-permute-start(f32[32,896]{1,0:T(8,128)S(1)} %add.122), channel_id=1, source_target_pairs={{0,16},{8,24},{16,0},{24,8},{1,17},{9,25},{17,1},{25,9},{2,18},{10... | collective-permute-start | bytes 344072 | tf_op jit(solution)/shard_map/ppermute | solution.py:316
  82.7 5.0 %collective-permute-start.9 = (f32[32,1024]{1,0:T(8,128)S(1)}, f32[32,1024]{1,0:T(8,128)S(1)}, u32[]{:S(2)}, u32[]{:S(2)}) collective-permute-start(f32[32,1024]{1,0:T(8,128)S(1)} %add_multiply_fusion), channel_id=1, source_target_pairs={{0,8},{8,0},{16,24},{24,16},{1,9},{9,1},{17,25},{25,17},{2,10},{10... | collective-permute-start | bytes 393224 | tf_op jit(solution)/shard_map/ppermute | solution.py:316
  82.8 6.7 %collective-permute-start.17 = (f32[32,640]{1,0:T(8,128)S(1)}, f32[32,640]{1,0:T(8,128)S(1)}, u32[]{:S(2)}, u32[]{:S(2)}) collective-permute-start(f32[32,640]{1,0:T(8,128)S(1)} %add_multiply_fusion.2), channel_id=1, source_target_pairs={{0,4},{1,5},{2,6},{3,7},{4,0},{5,1},{6,2},{7,3},{8,12},{9,13},{10,... | collective-permute-start | bytes 245768 | tf_op jit(solution)/shard_map/ppermute | solution.py:316
  84.5 5.0 %collective-permute-start.18 = (f32[32,896]{1,0:T(8,128)S(1)}, f32[32,896]{1,0:T(8,128)S(1)}, u32[]{:S(2)}, u32[]{:S(2)}) collective-permute-start(f32[32,896]{1,0:T(8,128)S(1)} %add_multiply_fusion.1), channel_id=1, source_target_pairs={{0,2},{1,3},{2,0},{3,1},{4,6},{5,7},{6,4},{7,5},{8,10},{9,11},{10,... | collective-permute-start | bytes 344072 | tf_op jit(solution)/shard_map/ppermute | solution.py:316
  87.7 6.4 %collective-permute-start.16 = (f32[64,1024]{1,0:T(8,128)S(1)}, f32[64,1024]{1,0:T(8,128)S(1)}, u32[]{:S(2)}, u32[]{:S(2)}) collective-permute-start(f32[64,1024]{1,0:T(8,128)S(1)} %pad_maximum_fusion.3), channel_id=1, source_target_pairs={{0,4},{1,5},{2,6},{3,7},{4,0},{5,1},{6,2},{7,3},{8,12},{9,13},{10,... | collective-permute-start | bytes 786440 | tf_op jit(solution)/shard_map/ppermute | solution.py:316
  89.5 6.1 %collective-permute-start.20 = (f32[64,896]{1,0:T(8,128)S(1)}, f32[64,896]{1,0:T(8,128)S(1)}, u32[]{:S(2)}, u32[]{:S(2)}) collective-permute-start(f32[64,896]{1,0:T(8,128)S(1)} %pad_maximum_fusion.4), channel_id=1, source_target_pairs={{0,8},{8,0},{16,24},{24,16},{1,9},{9,1},{17,25},{25,17},{2,10},{10... | collective-permute-start | bytes 688136 | tf_op jit(solution)/shard_map/ppermute | solution.py:316
  91.4 5.4 %collective-permute-start.21 = (f32[64,640]{1,0:T(8,128)S(1)}, f32[64,640]{1,0:T(8,128)S(1)}, u32[]{:S(2)}, u32[]{:S(2)}) collective-permute-start(f32[64,640]{1,0:T(8,128)S(1)} %pad_maximum_fusion.5), channel_id=1, source_target_pairs={{0,2},{1,3},{2,0},{3,1},{4,6},{5,7},{6,4},{7,5},{8,10},{9,11},{10,... | collective-permute-start | bytes 491528 | tf_op jit(solution)/shard_map/ppermute | solution.py:316
  94.2 5.6 %collective-permute-start.22 = (f32[128,1024]{1,0:T(8,128)S(1)}, f32[128,1024]{1,0:T(8,128)S(1)}, u32[]{:S(2)}, u32[]{:S(2)}) collective-permute-start(f32[128,1024]{1,0:T(8,128)S(1)} %pad_maximum_fusion.refs_0_), channel_id=1, source_target_pairs={{0,1},{1,0},{2,3},{3,2},{4,5},{5,4},{6,7},{7,6},{8,9},{9,8},{10,11... | collective-permute-start | bytes 1572872 | tf_op jit(solution)/shard_map/ppermute | solution.py:316
  94.3 14.3 %collective-permute-start.19 = (f32[128,1024]{1,0:T(8,128)S(1)}, f32[128,1024]{1,0:T(8,128)S(1)}, u32[]{:S(2)}, u32[]{:S(2)}) collective-permute-start(f32[128,1024]{1,0:T(8,128)S(1)} %pad_maximum_fusion.refs_0_), channel_id=1, source_target_pairs={{0,2},{1,3},{2,0},{3,1},{4,6},{5,7},{6,4},{7,5},{8,10},{9,11},{10,... | collective-permute-start | bytes 1572872 | tf_op jit(solution)/shard_map/ppermute | solution.py:316
  96.8 3.0 %collective-permute-start.23 = (f32[128,896]{1,0:T(8,128)S(1)}, f32[128,896]{1,0:T(8,128)S(1)}, u32[]{:S(2)}, u32[]{:S(2)}) collective-permute-start(f32[128,896]{1,0:T(8,128)S(1)} %pad_maximum_fusion.1.refs_1_), channel_id=1, source_target_pairs={{0,1},{1,0},{2,3},{3,2},{4,5},{5,4},{6,7},{7,6},{8,9},{9,8},{10,11... | collective-permute-start | bytes 1376264 | tf_op jit(solution)/shard_map/ppermute | solution.py:316
  96.9 2.3 %collective-permute-start.24 = (f32[128,640]{1,0:T(8,128)S(1)}, f32[128,640]{1,0:T(8,128)S(1)}, u32[]{:S(2)}, u32[]{:S(2)}) collective-permute-start(f32[128,640]{1,0:T(8,128)S(1)} %pad_maximum_fusion.2.refs_2_), channel_id=1, source_target_pairs={{0,1},{1,0},{2,3},{3,2},{4,5},{5,4},{6,7},{7,6},{8,9},{9,8},{10,11... | collective-permute-start | bytes 983048 | tf_op jit(solution)/shard_map/ppermute | solution.py:316
  97.4 12.5 %collective-permute-start.25 = (f32[128,896]{1,0:T(8,128)S(1)}, f32[128,896]{1,0:T(8,128)S(1)}, u32[]{:S(2)}, u32[]{:S(2)}) collective-permute-start(f32[128,896]{1,0:T(8,128)S(1)} %pad_maximum_fusion.1.refs_1_), channel_id=1, source_target_pairs={{0,4},{1,5},{2,6},{3,7},{4,0},{5,1},{6,2},{7,3},{8,12},{9,13},{10,... | collective-permute-start | bytes 1376264 | tf_op jit(solution)/shard_map/ppermute | solution.py:316
  99.1 10.7 %collective-permute-start.26 = (f32[128,640]{1,0:T(8,128)S(1)}, f32[128,640]{1,0:T(8,128)S(1)}, u32[]{:S(2)}, u32[]{:S(2)}) collective-permute-start(f32[128,640]{1,0:T(8,128)S(1)} %pad_maximum_fusion.2.refs_2_), channel_id=1, source_target_pairs={{0,8},{8,0},{16,24},{24,16},{1,9},{9,1},{17,25},{25,17},{2,10},{10... | collective-permute-start | bytes 983048 | tf_op jit(solution)/shard_map/ppermute | solution.py:316
  108.6 3.5 %collective-permute-start.27 = (f32[128,1024]{1,0:T(8,128)S(1)}, f32[128,1024]{1,0:T(8,128)S(1)}, u32[]{:S(2)}, u32[]{:S(2)}) collective-permute-start(f32[128,1024]{1,0:T(8,128)S(1)} %collective-permute-done.19.refs_0_), channel_id=1, source_target_pairs={{0,1},{1,0},{2,3},{3,2},{4,5},{5,4},{6,7},{7,6},{8,9},{9,8},{10,11... | collective-permute-start | bytes 1572872 | tf_op jit(solution)/shard_map/ppermute | solution.py:316
  109.9 2.3 %collective-permute-start.28 = (f32[128,896]{1,0:T(8,128)S(1)}, f32[128,896]{1,0:T(8,128)S(1)}, u32[]{:S(2)}, u32[]{:S(2)}) collective-permute-start(f32[128,896]{1,0:T(8,128)S(1)} %collective-permute-done.25.refs_1_), channel_id=1, source_target_pairs={{0,1},{1,0},{2,3},{3,2},{4,5},{5,4},{6,7},{7,6},{8,9},{9,8},{10,11... | collective-permute-start | bytes 1376264 | tf_op jit(solution)/shard_map/ppermute | solution.py:316
  109.9 2.3 %collective-permute-start.29 = (f32[128,640]{1,0:T(8,128)S(1)}, f32[128,640]{1,0:T(8,128)S(1)}, u32[]{:S(2)}, u32[]{:S(2)}) collective-permute-start(f32[128,640]{1,0:T(8,128)S(1)} %collective-permute-done.26.refs_2_), channel_id=1, source_target_pairs={{0,1},{1,0},{2,3},{3,2},{4,5},{5,4},{6,7},{7,6},{8,9},{9,8},{10,11... | collective-permute-start | bytes 983048 | tf_op jit(solution)/shard_map/ppermute | solution.py:316

commit v5 on v4

--- a/solution.py
+++ b/solution.py
@@ -375,7 +375,7 @@
             self.pieces = stop.value
 
 
-CUTS = 8, 7, 5
+CUTS = 7, 8, 5
 ITEMS_AT, SENT_AT, GOT_AT, TABLE_AT, STRICT = 1, 1, 3, 4, 1
 
 

time: 115 us -> 115 us (level)
    unnamed x12 -> x14, local copies, waits for them, and re-layouts: 1.52 us -> 2.36 us
  transfers between devices with their start and end apart: 31 -> 31, of which waited for: 14 -> 14; matrix products, arithmetic and copies ran while one was open for 4% -> 3% of each run, Pallas kernels for 9% -> 9%
where the time goes in v5:
time: 115 us; the launch traced here: 114 us
  waiting for transfers between devices  44.4 us (39%)
  starting transfers between devices  39.1 us (34%)
  Pallas kernels  23.5 us (20%)
  other arithmetic  3.45 us (3%)
  local copies, waits for them, and re-layouts  2.69 us (2%)
    ppermute x30, waiting for transfers between devices, swap(): return lax.ppermute(x, axis, [(i, i ^ distance) for i in range(size)])  44.4 us
    ppermute x30, starting transfers between devices, swap(): return lax.ppermute(x, axis, [(i, i ^ distance) for i in range(size)])  31.6 us
    pallas_call x1, Pallas kernels, block_call(): pl.pallas_call(functools.partial(block_kernel, chunk), name='block', out_...  10.6 us
    all_to_all x1, starting transfers between devices, per_device(): lax.all_to_all(after(sent, *(runs[0].last if SENT_AT > ITEMS_AT else ()))...  7.47 us
    pallas_call x2, Pallas kernels, place_call(): pl.pallas_call(functools.partial(place_kernel, chunk, spots), name='place...  5.16 us
    pallas_call x1, Pallas kernels, item_call(): pl.pallas_call(functools.partial(item_kernel, owners, slots), name='items...  3.3 us
    add x3, other arithmetic, exchange(): x = keep + (yield swap(send, order[0]))  2.91 us
    pallas_call x1, Pallas kernels, table_call(): pl.pallas_call(functools.partial(table_kernel, owners, slots), name='tabl...  2.77 us
  transfers between devices with their start and end apart: 31, of which 14 were waited for; matrix products, arithmetic and copies ran while one was open for 3% of the time, Pallas kernels for 9%

profile of v5, /device:TPU:0, one launch (start us, length us, event | category | flops | bytes accessed | tf_op | source)
XLA Modules:
  0.0 114.2 jit_solution(15939453541914839207)
XLA Ops:
  0.6 0.0 copy-start.1
  0.7 0.1 pad_add_fusion.place
  0.8 0.7 copy-done.5
  1.4 10.6 %block.1 = (f32[256,896]{1,0:T(8,128)S(1)}, f32[256,896]{1,0:T(8,128)}, bf16[512,2048]{1,0:T(8,128)(2,1)S(1)}, bf16[512,512]{1,0:T(8,128)(2,1)S(1)}, bf16[512,51...) custom-call(s32[3]{0:T(128)S(1)} %pad_add_fusion.place, s32[1,8]{1,0:T(1,128)S(1)} %copy-done.5, ...), custom_call_target="tpu_custom_call" | custom-call | tf_op jit(solution)/shard_map/block/pallas_call | solution.py:150
  12.0 0.5 collective-permute-start
  12.6 1.7 %rest.1 = (f32[256,1024]{1,0:T(8,128)S(1)}, f32[256,1024]{1,0:T(8,128)}, f32[256,640]{1,0:T(8,128)S(1)}, f32[256,640]{1,0:T(8,128)S(1)}) custom-call(bf16[512,512]{1,0:T(8,128)(2,1)S(1)} %get-tuple-element.65.rel_q, bf16[512,512]{1,0:T(8,128)(2,1)S(1)} %get-tuple-element.66.rel_r, bf16[512,512]{1,0:T(8,128)(2,1)S(1)} %get-tuple-element.67.rel_g, ...), custom_call_target="tpu_custom_call" | custom-call | tf_op jit(solution)/shard_map/rest/pallas_call | solution.py:191
  14.3 0.8 copy-done.2
  15.1 0.8 copy-done.6
  16.0 0.1 collective-permute-start.5
  16.0 3.3 %items.1 = f32[32,72,128]{2,1,0:T(8,128)} custom-call(s32[1,512]{1,0:T(1,128)S(1)} %bitcast.4, bf16[512,512]{1,0:T(8,128)(2,1)S(1)} %copy-done.1, bf16[512,2048]{1,0:T(8,128)(2,1)S(1)} %get-tuple-element.57.grad_pre, bf16[512,2048]{1,0:T(8,128)(2,1)S(1)} %copy-done), custom_call_target="tpu_custom_call" | custom-call | tf_op jit(solution)/shard_map/items/pallas_call | solution.py:239
  19.3 7.5 %all-to-all-start = ((f32[32,72,128]{2,1,0:T(8,128)}), f32[32,72,128]{2,1,0:T(8,128)S(1)}, u32[]{:S(2)}, u32[]{:S(2)}) async-start(f32[32,72,128]{2,1,0:T(8,128)} %items.1), calls=%async_computation | async-start | bytes 2359296 | tf_op jit(solution)/shard_map/all_to_all | solution.py:404
  26.8 0.1 collective-permute-start.3
  27.0 0.0 collective-permute-done
  27.0 1.3 %add.110 = f32[256,896]{1,0:T(8,128)S(1)} add(f32[256,896]{1,0:T(8,128)S(1)} %get-tuple-element.58, f32[256,896]{1,0:T(8,128)} %collective-permute-done) | non-fusion elementwise | flops 229376 | bytes 2752512 | tf_op jit(solution)/shard_map/add | solution.py:352
  28.3 0.1 fusion.1
  28.4 1.7 %collective-permute-start.1 = (f32[128,896]{1,0:T(8,128)S(1)}, f32[128,896]{1,0:T(8,128)S(1)}, u32[]{:S(2)}, u32[]{:S(2)}) collective-permute-start(f32[128,896]{1,0:T(8,128)S(1)} %get-tuple-element.61), channel_id=1, source_target_pairs={{0,2},{1,3},{2,0},{3,1},{4,6},{5,7},{6,4},{7,5},{8,10},{9,11},{10,... | collective-permute-start | bytes 1376264 | tf_op jit(solution)/shard_map/ppermute | solution.py:316
  30.1 1.5 %add.113 = f32[256,1024]{1,0:T(8,128)S(1)} add(f32[256,1024]{1,0:T(8,128)S(1)} %get-tuple-element.71, f32[256,1024]{1,0:T(8,128)} %collective-permute-done.5) | non-fusion elementwise | flops 262144 | bytes 3145728 | tf_op jit(solution)/shard_map/add | solution.py:352
  31.6 0.1 fusion
  31.7 1.5 %collective-permute-start.6 = (f32[128,1024]{1,0:T(8,128)S(1)}, f32[128,1024]{1,0:T(8,128)S(1)}, u32[]{:S(2)}, u32[]{:S(2)}) collective-permute-start(f32[128,1024]{1,0:T(8,128)S(1)} %get-tuple-element.73), channel_id=1, source_target_pairs={{0,4},{1,5},{2,6},{3,7},{4,0},{5,1},{6,2},{7,3},{8,12},{9,13},{10,... | collective-permute-start | bytes 1572872 | tf_op jit(solution)/shard_map/ppermute | solution.py:316
  33.3 0.1 add.112
  33.4 1.5 %collective-permute-start.4 = (f32[128,640]{1,0:T(8,128)S(1)}, f32[128,640]{1,0:T(8,128)S(1)}, u32[]{:S(2)}, u32[]{:S(2)}) collective-permute-start(f32[128,640]{1,0:T(8,128)S(1)} %get-tuple-element.70), channel_id=1, source_target_pairs={{0,8},{8,0},{16,24},{24,16},{1,9},{9,1},{17,25},{25,17},{2,10},{10... | collective-permute-start | bytes 983048 | tf_op jit(solution)/shard_map/ppermute | solution.py:316
  34.9 15.5 %collective-permute-done.1 = f32[128,896]{1,0:T(8,128)S(1)} collective-permute-done((f32[128,896]{1,0:T(8,128)S(1)}, f32[128,896]{1,0:T(8,128)S(1)}, u32[]{:S(2)}, u32[]{:S(2)}) %collective-permute-start.1) | collective-permute-done | bytes 458784 | tf_op jit(solution)/shard_map/ppermute | solution.py:316
  50.5 1.1 collective-permute-start.2
  51.6 1.6 %collective-permute-done.6 = f32[128,1024]{1,0:T(8,128)S(1)} collective-permute-done((f32[128,1024]{1,0:T(8,128)S(1)}, f32[128,1024]{1,0:T(8,128)S(1)}, u32[]{:S(2)}, u32[]{:S(2)}) %collective-permute-start.6) | collective-permute-done | bytes 524320 | tf_op jit(solution)/shard_map/ppermute | solution.py:316
  53.2 0.1 add.118
  53.3 0.9 collective-permute-done.4
  54.1 1.7 %collective-permute-start.11 = (f32[64,1024]{1,0:T(8,128)S(1)}, f32[64,1024]{1,0:T(8,128)S(1)}, u32[]{:S(2)}, u32[]{:S(2)}) collective-permute-start(f32[64,1024]{1,0:T(8,128)S(1)} %get-tuple-element.86), channel_id=1, source_target_pairs={{0,8},{8,0},{16,24},{24,16},{1,9},{9,1},{17,25},{25,17},{2,10},{10... | collective-permute-start | bytes 786440 | tf_op jit(solution)/shard_map/ppermute | solution.py:316
  56.0 1.7 %collective-permute-start.10 = (f32[64,640]{1,0:T(8,128)S(1)}, f32[64,640]{1,0:T(8,128)S(1)}, u32[]{:S(2)}, u32[]{:S(2)}) collective-permute-start(f32[64,640]{1,0:T(8,128)S(1)} %get-tuple-element.84), channel_id=1, source_target_pairs={{0,2},{1,3},{2,0},{3,1},{4,6},{5,7},{6,4},{7,5},{8,10},{9,11},{10,... | collective-permute-start | bytes 491528 | tf_op jit(solution)/shard_map/ppermute | solution.py:316
  57.7 1.1 collective-permute-done.2
  58.9 1.7 %collective-permute-start.7 = (f32[32,896]{1,0:T(8,128)S(1)}, f32[32,896]{1,0:T(8,128)S(1)}, u32[]{:S(2)}, u32[]{:S(2)}) collective-permute-start(f32[32,896]{1,0:T(8,128)S(1)} %get-tuple-element.77), channel_id=1, source_target_pairs={{0,8},{8,0},{16,24},{24,16},{1,9},{9,1},{17,25},{25,17},{2,10},{10... | collective-permute-start | bytes 344072 | tf_op jit(solution)/shard_map/ppermute | solution.py:316
  60.6 2.4 %collective-permute-done.11 = f32[64,1024]{1,0:T(8,128)S(1)} collective-permute-done((f32[64,1024]{1,0:T(8,128)S(1)}, f32[64,1024]{1,0:T(8,128)S(1)}, u32[]{:S(2)}, u32[]{:S(2)}) %collective-permute-start.11) | collective-permute-done | bytes 262176 | tf_op jit(solution)/shard_map/ppermute | solution.py:316
  63.1 0.0 collective-permute-done.10
  63.1 1.9 %collective-permute-start.13 = (f32[32,1024]{1,0:T(8,128)S(1)}, f32[32,1024]{1,0:T(8,128)S(1)}, u32[]{:S(2)}, u32[]{:S(2)}) collective-permute-start(f32[32,1024]{1,0:T(8,128)S(1)} %get-tuple-element.92), channel_id=1, source_target_pairs={{0,2},{1,3},{2,0},{3,1},{4,6},{5,7},{6,4},{7,5},{8,10},{9,11},{10,... | collective-permute-start | bytes 393224 | tf_op jit(solution)/shard_map/ppermute | solution.py:316
  65.1 0.0 collective-permute-done.7
  65.1 0.0 all-to-all-done.got
  65.1 3.6 %collective-permute-start.8 = (f32[32,896]{1,0:T(8,128)S(1)}, f32[32,896]{1,0:T(8,128)S(1)}, u32[]{:S(2)}, u32[]{:S(2)}) collective-permute-start(f32[32,896]{1,0:T(8,128)S(1)} %add.115), channel_id=1, source_target_pairs={{0,16},{8,24},{16,0},{24,8},{1,17},{9,25},{17,1},{25,9},{2,18},{10... | collective-permute-start | bytes 344072 | tf_op jit(solution)/shard_map/ppermute | solution.py:316
  68.7 1.6 %collective-permute-start.12 = (f32[32,640]{1,0:T(8,128)S(1)}, f32[32,640]{1,0:T(8,128)S(1)}, u32[]{:S(2)}, u32[]{:S(2)}) collective-permute-start(f32[32,640]{1,0:T(8,128)S(1)} %get-tuple-element.90), channel_id=1, source_target_pairs={{0,4},{1,5},{2,6},{3,7},{4,0},{5,1},{6,2},{7,3},{8,12},{9,13},{10,... | collective-permute-start | bytes 245768 | tf_op jit(solution)/shard_map/ppermute | solution.py:316
  70.3 0.0 collective-permute-done.13
  70.3 2.9 %collective-permute-done.12 = f32[32,640]{1,0:T(8,128)S(1)} collective-permute-done((f32[32,640]{1,0:T(8,128)S(1)}, f32[32,640]{1,0:T(8,128)S(1)}, u32[]{:S(2)}, u32[]{:S(2)}) %collective-permute-start.12) | collective-permute-done | bytes 81952 | tf_op jit(solution)/shard_map/ppermute | solution.py:316
  73.3 0.1 collective-permute-start.14
  73.3 2.9 %collective-permute-start.15 = (f32[32,1024]{1,0:T(8,128)S(1)}, f32[32,1024]{1,0:T(8,128)S(1)}, u32[]{:S(2)}, u32[]{:S(2)}) collective-permute-start(f32[32,1024]{1,0:T(8,128)S(1)} %add.122), channel_id=1, source_target_pairs={{0,16},{8,24},{16,0},{24,8},{1,17},{9,25},{17,1},{25,9},{2,18},{10... | collective-permute-start | bytes 393224 | tf_op jit(solution)/shard_map/ppermute | solution.py:316
  76.3 2.8 %table.1 = f32[1024,512]{1,0:T(8,128)} custom-call(f32[32,72,128]{2,1,0:T(8,128)S(1)} %all-to-all-done.got), custom_call_target="tpu_custom_call" | custom-call | tf_op jit(solution)/shard_map/table/pallas_call | solution.py:265
  79.0 0.6 collective-permute-start.9
  79.7 3.2 %collective-permute-done.15 = f32[32,1024]{1,0:T(8,128)S(1)} collective-permute-done((f32[32,1024]{1,0:T(8,128)S(1)}, f32[32,1024]{1,0:T(8,128)S(1)}, u32[]{:S(2)}, u32[]{:S(2)}) %collective-permute-start.15) | collective-permute-done | bytes 131104 | tf_op jit(solution)/shard_map/ppermute | solution.py:316
  82.9 1.6 %collective-permute-start.18 = (f32[32,1024]{1,0:T(8,128)S(1)}, f32[32,1024]{1,0:T(8,128)S(1)}, u32[]{:S(2)}, u32[]{:S(2)}) collective-permute-start(f32[32,1024]{1,0:T(8,128)S(1)} %add_multiply_fusion), channel_id=1, source_target_pairs={{0,2},{1,3},{2,0},{3,1},{4,6},{5,7},{6,4},{7,5},{8,10},{9,11},{10,... | collective-permute-start | bytes 393224 | tf_op jit(solution)/shard_map/ppermute | solution.py:316
  84.5 1.8 %collective-permute-start.17 = (f32[32,640]{1,0:T(8,128)S(1)}, f32[32,640]{1,0:T(8,128)S(1)}, u32[]{:S(2)}, u32[]{:S(2)}) collective-permute-start(f32[32,640]{1,0:T(8,128)S(1)} %add_multiply_fusion.2), channel_id=1, source_target_pairs={{0,4},{1,5},{2,6},{3,7},{4,0},{5,1},{6,2},{7,3},{8,12},{9,13},{10,... | collective-permute-start | bytes 245768 | tf_op jit(solution)/shard_map/ppermute | solution.py:316
  86.4 0.3 collective-permute-start.16
  86.7 1.2 %collective-permute-done.18 = f32[32,1024]{1,0:T(8,128)S(1)} collective-permute-done((f32[32,1024]{1,0:T(8,128)S(1)}, f32[32,1024]{1,0:T(8,128)S(1)}, u32[]{:S(2)}, u32[]{:S(2)}) %collective-permute-start.18) | collective-permute-done | bytes 131104 | tf_op jit(solution)/shard_map/ppermute | solution.py:316
  87.9 0.1 collective-permute-start.20
  88.0 1.9 %collective-permute-done.17 = f32[32,640]{1,0:T(8,128)S(1)} collective-permute-done((f32[32,640]{1,0:T(8,128)S(1)}, f32[32,640]{1,0:T(8,128)S(1)}, u32[]{:S(2)}, u32[]{:S(2)}) %collective-permute-start.17) | collective-permute-done | bytes 81952 | tf_op jit(solution)/shard_map/ppermute | solution.py:316
  89.9 0.5 collective-permute-start.21
  90.4 2.7 %collective-permute-done.16 = f32[64,896]{1,0:T(8,128)S(1)} collective-permute-done((f32[64,896]{1,0:T(8,128)S(1)}, f32[64,896]{1,0:T(8,128)S(1)}, u32[]{:S(2)}, u32[]{:S(2)}) %collective-permute-start.16) | collective-permute-done | bytes 229408 | tf_op jit(solution)/shard_map/ppermute | solution.py:316
  93.2 0.1 collective-permute-start.22
  93.3 1.1 collective-permute-done.20
  94.4 1.6 %collective-permute-start.25 = (f32[128,1024]{1,0:T(8,128)S(1)}, f32[128,1024]{1,0:T(8,128)S(1)}, u32[]{:S(2)}, u32[]{:S(2)}) collective-permute-start(f32[128,1024]{1,0:T(8,128)S(1)} %pad_maximum_fusion.refs_1_), channel_id=1, source_target_pairs={{0,4},{1,5},{2,6},{3,7},{4,0},{5,1},{6,2},{7,3},{8,12},{9,13},{10,... | collective-permute-start | bytes 1572872 | tf_op jit(solution)/shard_map/ppermute | solution.py:316
  96.0 0.6 collective-permute-start.24
  96.6 1.9 %collective-permute-start.19 = (f32[128,896]{1,0:T(8,128)S(1)}, f32[128,896]{1,0:T(8,128)S(1)}, u32[]{:S(2)}, u32[]{:S(2)}) collective-permute-start(f32[128,896]{1,0:T(8,128)S(1)} %pad_maximum_fusion.1.refs_0_), channel_id=1, source_target_pairs={{0,2},{1,3},{2,0},{3,1},{4,6},{5,7},{6,4},{7,5},{8,10},{9,11},{10,... | collective-permute-start | bytes 1376264 | tf_op jit(solution)/shard_map/ppermute | solution.py:316
  98.4 0.0 collective-permute-start.26
  98.5 2.6 %place.2 = (f32[512,2048]{1,0:T(8,128)}, f32[512,512]{1,0:T(8,128)}) custom-call(s32[3]{0:T(128)S(1)} %pad_add_fusion.place, f32[128,896]{1,0:T(8,128)S(1)} %pad_maximum_fusion.1.refs_0_, f32[128,1024]{1,0:T(8,128)S(1)} %pad_maximum_fusion.refs_1_, f32[128,640]{1,0:T(8,128)S(1)} %pad_maximum_fusion.2.refs_2_, ...), custom_call_target="tpu_custom_call" | custom-call | tf_op jit(solution)/shard_map/place/pallas_call | solution.py:298
  101.0 6.7 %collective-permute-done.25.refs_1_ = f32[128,1024]{1,0:T(8,128)S(1)} collective-permute-done((f32[128,1024]{1,0:T(8,128)S(1)}, f32[128,1024]{1,0:T(8,128)S(1)}, u32[]{:S(2)}, u32[]{:S(2)}) %collective-permute-start.25) | collective-permute-done | bytes 524320 | tf_op jit(solution)/shard_map/ppermute | solution.py:316
  107.7 1.5 %collective-permute-done.19.refs_0_ = f32[128,896]{1,0:T(8,128)S(1)} collective-permute-done((f32[128,896]{1,0:T(8,128)S(1)}, f32[128,896]{1,0:T(8,128)S(1)}, u32[]{:S(2)}, u32[]{:S(2)}) %collective-permute-start.19) | collective-permute-done | bytes 458784 | tf_op jit(solution)/shard_map/ppermute | solution.py:316
  109.2 0.5 collective-permute-start.29
  109.7 1.8 %collective-permute-done.29.refs_5_ = f32[128,640]{1,0:T(8,128)S(1)} collective-permute-done((f32[128,640]{1,0:T(8,128)S(1)}, f32[128,640]{1,0:T(8,128)S(1)}, u32[]{:S(2)}, u32[]{:S(2)}) %collective-permute-start.29) | collective-permute-done | bytes 327712 | tf_op jit(solution)/shard_map/ppermute | solution.py:316
  111.5 2.6 %place.3 = (f32[512,2048]{1,0:T(8,128)}, f32[512,512]{1,0:T(8,128)}) custom-call(s32[3]{0:T(128)S(1)} %pad_add_fusion.place, f32[128,896]{1,0:T(8,128)S(1)} %collective-permute-done.19.refs_0_, f32[128,1024]{1,0:T(8,128)S(1)} %collective-permute-done.25.refs_1_, ...), custom_call_target="tpu_custom_call", output_to_operand_aliasing={{0}: (7, {}), {1}: (8, {})} | custom-call | tf_op jit(solution)/shard_map/place/pallas_call | solution.py:298
  (49 shorter events, 0.6 us)
Async XLA Ops:
  0.6 11.9 %copy-start.1 = (bf16[512,512]{1,0:T(8,128)(2,1)S(1)}, bf16[512,512]{1,0:T(8,128)(2,1)}, u32[]{:S(2)}) copy-start(bf16[512,512]{1,0:T(8,128)(2,1)} %cot.3) | copy-start | bytes 1572868
  0.8 0.7 copy-start.5
  12.0 14.9 %collective-permute-start = (f32[256,896]{1,0:T(8,128)}, f32[256,896]{1,0:T(8,128)}, u32[]{:S(2)}, u32[]{:S(2)}) collective-permute-start(f32[256,896]{1,0:T(8,128)} %get-tuple-element.59), channel_id=1, source_target_pairs={{0,1},{1,0},{2,3},{3,2},{4,5},{5,4},{6,7},{7,6},{8,9},{9,8},{10,11... | collective-permute-start | bytes 2752520 | tf_op jit(solution)/shard_map/ppermute | solution.py:316
  12.6 3.5 %copy-start = (bf16[512,2048]{1,0:T(8,128)(2,1)S(1)}, bf16[512,2048]{1,0:T(8,128)(2,1)}, u32[]{:S(2)}) copy-start(bf16[512,2048]{1,0:T(8,128)(2,1)} %in_proj.1) | copy-start | bytes 6291460
  12.6 3.5 %copy-start.4 = (s32[512]{0:T(512)S(1)}, s32[512]{0:T(512)}, u32[]{:S(2)}) copy-start(s32[512]{0:T(512)} %param.11) | copy-start | bytes 6148
  14.3 0.8 copy-start.2
  15.1 0.8 copy-start.6
  16.0 14.1 %collective-permute-start.5 = (f32[256,1024]{1,0:T(8,128)}, f32[256,1024]{1,0:T(8,128)}, u32[]{:S(2)}, u32[]{:S(2)}) collective-permute-start(f32[256,1024]{1,0:T(8,128)} %get-tuple-element.72), channel_id=1, source_target_pairs={{0,1},{1,0},{2,3},{3,2},{4,5},{5,4},{6,7},{7,6},{8,9},{9,8},{10,11... | collective-permute-start | bytes 3145736 | tf_op jit(solution)/shard_map/ppermute | solution.py:316
  19.3 45.7 %all-to-all-start = ((f32[32,72,128]{2,1,0:T(8,128)}), f32[32,72,128]{2,1,0:T(8,128)S(1)}, u32[]{:S(2)}, u32[]{:S(2)}) async-start(f32[32,72,128]{2,1,0:T(8,128)} %items.1), calls=%async_computation | async-start | bytes 2359296 | tf_op jit(solution)/shard_map/all_to_all | solution.py:404
  26.8 6.4 %collective-permute-start.3 = (f32[256,640]{1,0:T(8,128)}, f32[256,640]{1,0:T(8,128)S(1)}, u32[]{:S(2)}, u32[]{:S(2)}) collective-permute-start(f32[256,640]{1,0:T(8,128)} %copy-done.6), channel_id=1, source_target_pairs={{0,1},{1,0},{2,3},{3,2},{4,5},{5,4},{6,7},{7,6},{8,9},{9,8},{10,11... | collective-permute-start | bytes 1966088 | tf_op jit(solution)/shard_map/ppermute | solution.py:316
  28.4 22.0 %collective-permute-start.1 = (f32[128,896]{1,0:T(8,128)S(1)}, f32[128,896]{1,0:T(8,128)S(1)}, u32[]{:S(2)}, u32[]{:S(2)}) collective-permute-start(f32[128,896]{1,0:T(8,128)S(1)} %get-tuple-element.61), channel_id=1, source_target_pairs={{0,2},{1,3},{2,0},{3,1},{4,6},{5,7},{6,4},{7,5},{8,10},{9,11},{10,... | collective-permute-start | bytes 1376264 | tf_op jit(solution)/shard_map/ppermute | solution.py:316
  30.1 3.1 %copy-start.3 = (f32[256,640]{1,0:T(8,128)S(1)}, f32[256,640]{1,0:T(8,128)}, u32[]{:S(2)}) copy-start(f32[256,640]{1,0:T(8,128)} %copy-done.2) | copy-start | bytes 1966084
  31.7 21.4 %collective-permute-start.6 = (f32[128,1024]{1,0:T(8,128)S(1)}, f32[128,1024]{1,0:T(8,128)S(1)}, u32[]{:S(2)}, u32[]{:S(2)}) collective-permute-start(f32[128,1024]{1,0:T(8,128)S(1)} %get-tuple-element.73), channel_id=1, source_target_pairs={{0,4},{1,5},{2,6},{3,7},{4,0},{5,1},{6,2},{7,3},{8,12},{9,13},{10,... | collective-permute-start | bytes 1572872 | tf_op jit(solution)/shard_map/ppermute | solution.py:316
  33.4 20.7 %collective-permute-start.4 = (f32[128,640]{1,0:T(8,128)S(1)}, f32[128,640]{1,0:T(8,128)S(1)}, u32[]{:S(2)}, u32[]{:S(2)}) collective-permute-start(f32[128,640]{1,0:T(8,128)S(1)} %get-tuple-element.70), channel_id=1, source_target_pairs={{0,8},{8,0},{16,24},{24,16},{1,9},{9,1},{17,25},{25,17},{2,10},{10... | collective-permute-start | bytes 983048 | tf_op jit(solution)/shard_map/ppermute | solution.py:316
  50.5 8.3 %collective-permute-start.2 = (f32[64,896]{1,0:T(8,128)S(1)}, f32[64,896]{1,0:T(8,128)S(1)}, u32[]{:S(2)}, u32[]{:S(2)}) collective-permute-start(f32[64,896]{1,0:T(8,128)S(1)} %get-tuple-element.64), channel_id=1, source_target_pairs={{0,4},{1,5},{2,6},{3,7},{4,0},{5,1},{6,2},{7,3},{8,12},{9,13},{10,... | collective-permute-start | bytes 688136 | tf_op jit(solution)/shard_map/ppermute | solution.py:316
  54.1 8.9 %collective-permute-start.11 = (f32[64,1024]{1,0:T(8,128)S(1)}, f32[64,1024]{1,0:T(8,128)S(1)}, u32[]{:S(2)}, u32[]{:S(2)}) collective-permute-start(f32[64,1024]{1,0:T(8,128)S(1)} %get-tuple-element.86), channel_id=1, source_target_pairs={{0,8},{8,0},{16,24},{24,16},{1,9},{9,1},{17,25},{25,17},{2,10},{10... | collective-permute-start | bytes 786440 | tf_op jit(solution)/shard_map/ppermute | solution.py:316
  56.0 7.1 %collective-permute-start.10 = (f32[64,640]{1,0:T(8,128)S(1)}, f32[64,640]{1,0:T(8,128)S(1)}, u32[]{:S(2)}, u32[]{:S(2)}) collective-permute-start(f32[64,640]{1,0:T(8,128)S(1)} %get-tuple-element.84), channel_id=1, source_target_pairs={{0,2},{1,3},{2,0},{3,1},{4,6},{5,7},{6,4},{7,5},{8,10},{9,11},{10,... | collective-permute-start | bytes 491528 | tf_op jit(solution)/shard_map/ppermute | solution.py:316
  58.9 6.2 %collective-permute-start.7 = (f32[32,896]{1,0:T(8,128)S(1)}, f32[32,896]{1,0:T(8,128)S(1)}, u32[]{:S(2)}, u32[]{:S(2)}) collective-permute-start(f32[32,896]{1,0:T(8,128)S(1)} %get-tuple-element.77), channel_id=1, source_target_pairs={{0,8},{8,0},{16,24},{24,16},{1,9},{9,1},{17,25},{25,17},{2,10},{10... | collective-permute-start | bytes 344072 | tf_op jit(solution)/shard_map/ppermute | solution.py:316
  63.1 7.2 %collective-permute-start.13 = (f32[32,1024]{1,0:T(8,128)S(1)}, f32[32,1024]{1,0:T(8,128)S(1)}, u32[]{:S(2)}, u32[]{:S(2)}) collective-permute-start(f32[32,1024]{1,0:T(8,128)S(1)} %get-tuple-element.92), channel_id=1, source_target_pairs={{0,2},{1,3},{2,0},{3,1},{4,6},{5,7},{6,4},{7,5},{8,10},{9,11},{10,... | collective-permute-start | bytes 393224 | tf_op jit(solution)/shard_map/ppermute | solution.py:316
  65.1 13.9 %collective-permute-start.8 = (f32[32,896]{1,0:T(8,128)S(1)}, f32[32,896]{1,0:T(8,128)S(1)}, u32[]{:S(2)}, u32[]{:S(2)}) collective-permute-start(f32[32,896]{1,0:T(8,128)S(1)} %add.115), channel_id=1, source_target_pairs={{0,16},{8,24},{16,0},{24,8},{1,17},{9,25},{17,1},{25,9},{2,18},{10... | collective-permute-start | bytes 344072 | tf_op jit(solution)/shard_map/ppermute | solution.py:316
  68.7 4.5 %collective-permute-start.12 = (f32[32,640]{1,0:T(8,128)S(1)}, f32[32,640]{1,0:T(8,128)S(1)}, u32[]{:S(2)}, u32[]{:S(2)}) collective-permute-start(f32[32,640]{1,0:T(8,128)S(1)} %get-tuple-element.90), channel_id=1, source_target_pairs={{0,4},{1,5},{2,6},{3,7},{4,0},{5,1},{6,2},{7,3},{8,12},{9,13},{10,... | collective-permute-start | bytes 245768 | tf_op jit(solution)/shard_map/ppermute | solution.py:316
  73.3 9.6 %collective-permute-start.14 = (f32[32,640]{1,0:T(8,128)S(1)}, f32[32,640]{1,0:T(8,128)S(1)}, u32[]{:S(2)}, u32[]{:S(2)}) collective-permute-start(f32[32,640]{1,0:T(8,128)S(1)} %add.121), channel_id=1, source_target_pairs={{0,16},{8,24},{16,0},{24,8},{1,17},{9,25},{17,1},{25,9},{2,18},{10... | collective-permute-start | bytes 245768 | tf_op jit(solution)/shard_map/ppermute | solution.py:316
  73.3 9.5 %collective-permute-start.15 = (f32[32,1024]{1,0:T(8,128)S(1)}, f32[32,1024]{1,0:T(8,128)S(1)}, u32[]{:S(2)}, u32[]{:S(2)}) collective-permute-start(f32[32,1024]{1,0:T(8,128)S(1)} %add.122), channel_id=1, source_target_pairs={{0,16},{8,24},{16,0},{24,8},{1,17},{9,25},{17,1},{25,9},{2,18},{10... | collective-permute-start | bytes 393224 | tf_op jit(solution)/shard_map/ppermute | solution.py:316
  79.0 7.3 %collective-permute-start.9 = (f32[32,896]{1,0:T(8,128)S(1)}, f32[32,896]{1,0:T(8,128)S(1)}, u32[]{:S(2)}, u32[]{:S(2)}) collective-permute-start(f32[32,896]{1,0:T(8,128)S(1)} %add_multiply_fusion.1), channel_id=1, source_target_pairs={{0,8},{8,0},{16,24},{24,16},{1,9},{9,1},{17,25},{25,17},{2,10},{10... | collective-permute-start | bytes 344072 | tf_op jit(solution)/shard_map/ppermute | solution.py:316
  82.9 5.0 %collective-permute-start.18 = (f32[32,1024]{1,0:T(8,128)S(1)}, f32[32,1024]{1,0:T(8,128)S(1)}, u32[]{:S(2)}, u32[]{:S(2)}) collective-permute-start(f32[32,1024]{1,0:T(8,128)S(1)} %add_multiply_fusion), channel_id=1, source_target_pairs={{0,2},{1,3},{2,0},{3,1},{4,6},{5,7},{6,4},{7,5},{8,10},{9,11},{10,... | collective-permute-start | bytes 393224 | tf_op jit(solution)/shard_map/ppermute | solution.py:316
  84.5 5.3 %collective-permute-start.17 = (f32[32,640]{1,0:T(8,128)S(1)}, f32[32,640]{1,0:T(8,128)S(1)}, u32[]{:S(2)}, u32[]{:S(2)}) collective-permute-start(f32[32,640]{1,0:T(8,128)S(1)} %add_multiply_fusion.2), channel_id=1, source_target_pairs={{0,4},{1,5},{2,6},{3,7},{4,0},{5,1},{6,2},{7,3},{8,12},{9,13},{10,... | collective-permute-start | bytes 245768 | tf_op jit(solution)/shard_map/ppermute | solution.py:316
  86.4 6.8 %collective-permute-start.16 = (f32[64,896]{1,0:T(8,128)S(1)}, f32[64,896]{1,0:T(8,128)S(1)}, u32[]{:S(2)}, u32[]{:S(2)}) collective-permute-start(f32[64,896]{1,0:T(8,128)S(1)} %pad_maximum_fusion.4), channel_id=1, source_target_pairs={{0,4},{1,5},{2,6},{3,7},{4,0},{5,1},{6,2},{7,3},{8,12},{9,13},{10,... | collective-permute-start | bytes 688136 | tf_op jit(solution)/shard_map/ppermute | solution.py:316
  87.9 6.4 %collective-permute-start.20 = (f32[64,1024]{1,0:T(8,128)S(1)}, f32[64,1024]{1,0:T(8,128)S(1)}, u32[]{:S(2)}, u32[]{:S(2)}) collective-permute-start(f32[64,1024]{1,0:T(8,128)S(1)} %pad_maximum_fusion.3), channel_id=1, source_target_pairs={{0,8},{8,0},{16,24},{24,16},{1,9},{9,1},{17,25},{25,17},{2,10},{10... | collective-permute-start | bytes 786440 | tf_op jit(solution)/shard_map/ppermute | solution.py:316
  89.9 6.1 %collective-permute-start.21 = (f32[64,640]{1,0:T(8,128)S(1)}, f32[64,640]{1,0:T(8,128)S(1)}, u32[]{:S(2)}, u32[]{:S(2)}) collective-permute-start(f32[64,640]{1,0:T(8,128)S(1)} %pad_maximum_fusion.5), channel_id=1, source_target_pairs={{0,2},{1,3},{2,0},{3,1},{4,6},{5,7},{6,4},{7,5},{8,10},{9,11},{10,... | collective-permute-start | bytes 491528 | tf_op jit(solution)/shard_map/ppermute | solution.py:316
  93.2 5.3 %collective-permute-start.22 = (f32[128,896]{1,0:T(8,128)S(1)}, f32[128,896]{1,0:T(8,128)S(1)}, u32[]{:S(2)}, u32[]{:S(2)}) collective-permute-start(f32[128,896]{1,0:T(8,128)S(1)} %pad_maximum_fusion.1.refs_0_), channel_id=1, source_target_pairs={{0,1},{1,0},{2,3},{3,2},{4,5},{5,4},{6,7},{7,6},{8,9},{9,8},{10,11... | collective-permute-start | bytes 1376264 | tf_op jit(solution)/shard_map/ppermute | solution.py:316
  94.4 13.3 %collective-permute-start.25 = (f32[128,1024]{1,0:T(8,128)S(1)}, f32[128,1024]{1,0:T(8,128)S(1)}, u32[]{:S(2)}, u32[]{:S(2)}) collective-permute-start(f32[128,1024]{1,0:T(8,128)S(1)} %pad_maximum_fusion.refs_1_), channel_id=1, source_target_pairs={{0,4},{1,5},{2,6},{3,7},{4,0},{5,1},{6,2},{7,3},{8,12},{9,13},{10,... | collective-permute-start | bytes 1572872 | tf_op jit(solution)/shard_map/ppermute | solution.py:316
  96.0 2.5 %collective-permute-start.23 = (f32[128,1024]{1,0:T(8,128)S(1)}, f32[128,1024]{1,0:T(8,128)S(1)}, u32[]{:S(2)}, u32[]{:S(2)}) collective-permute-start(f32[128,1024]{1,0:T(8,128)S(1)} %pad_maximum_fusion.refs_1_), channel_id=1, source_target_pairs={{0,1},{1,0},{2,3},{3,2},{4,5},{5,4},{6,7},{7,6},{8,9},{9,8},{10,11... | collective-permute-start | bytes 1572872 | tf_op jit(solution)/shard_map/ppermute | solution.py:316
  96.0 2.4 %collective-permute-start.24 = (f32[128,640]{1,0:T(8,128)S(1)}, f32[128,640]{1,0:T(8,128)S(1)}, u32[]{:S(2)}, u32[]{:S(2)}) collective-permute-start(f32[128,640]{1,0:T(8,128)S(1)} %pad_maximum_fusion.2.refs_2_), channel_id=1, source_target_pairs={{0,1},{1,0},{2,3},{3,2},{4,5},{5,4},{6,7},{7,6},{8,9},{9,8},{10,11... | collective-permute-start | bytes 983048 | tf_op jit(solution)/shard_map/ppermute | solution.py:316
  96.6 12.6 %collective-permute-start.19 = (f32[128,896]{1,0:T(8,128)S(1)}, f32[128,896]{1,0:T(8,128)S(1)}, u32[]{:S(2)}, u32[]{:S(2)}) collective-permute-start(f32[128,896]{1,0:T(8,128)S(1)} %pad_maximum_fusion.1.refs_0_), channel_id=1, source_target_pairs={{0,2},{1,3},{2,0},{3,1},{4,6},{5,7},{6,4},{7,5},{8,10},{9,11},{10,... | collective-permute-start | bytes 1376264 | tf_op jit(solution)/shard_map/ppermute | solution.py:316
  98.4 10.8 %collective-permute-start.26 = (f32[128,640]{1,0:T(8,128)S(1)}, f32[128,640]{1,0:T(8,128)S(1)}, u32[]{:S(2)}, u32[]{:S(2)}) collective-permute-start(f32[128,640]{1,0:T(8,128)S(1)} %pad_maximum_fusion.2.refs_2_), channel_id=1, source_target_pairs={{0,8},{8,0},{16,24},{24,16},{1,9},{9,1},{17,25},{25,17},{2,10},{10... | collective-permute-start | bytes 983048 | tf_op jit(solution)/shard_map/ppermute | solution.py:316
  107.7 3.8 %collective-permute-start.28 = (f32[128,1024]{1,0:T(8,128)S(1)}, f32[128,1024]{1,0:T(8,128)S(1)}, u32[]{:S(2)}, u32[]{:S(2)}) collective-permute-start(f32[128,1024]{1,0:T(8,128)S(1)} %collective-permute-done.25.refs_1_), channel_id=1, source_target_pairs={{0,1},{1,0},{2,3},{3,2},{4,5},{5,4},{6,7},{7,6},{8,9},{9,8},{10,11... | collective-permute-start | bytes 1572872 | tf_op jit(solution)/shard_map/ppermute | solution.py:316
  109.2 2.3 %collective-permute-start.27 = (f32[128,896]{1,0:T(8,128)S(1)}, f32[128,896]{1,0:T(8,128)S(1)}, u32[]{:S(2)}, u32[]{:S(2)}) collective-permute-start(f32[128,896]{1,0:T(8,128)S(1)} %collective-permute-done.19.refs_0_), channel_id=1, source_target_pairs={{0,1},{1,0},{2,3},{3,2},{4,5},{5,4},{6,7},{7,6},{8,9},{9,8},{10,11... | collective-permute-start | bytes 1376264 | tf_op jit(solution)/shard_map/ppermute | solution.py:316
  109.2 2.3 %collective-permute-start.29 = (f32[128,640]{1,0:T(8,128)S(1)}, f32[128,640]{1,0:T(8,128)S(1)}, u32[]{:S(2)}, u32[]{:S(2)}) collective-permute-start(f32[128,640]{1,0:T(8,128)S(1)} %collective-permute-done.26.refs_2_), channel_id=1, source_target_pairs={{0,1},{1,0},{2,3},{3,2},{4,5},{5,4},{6,7},{7,6},{8,9},{9,8},{10,11... | collective-permute-start | bytes 983048 | tf_op jit(solution)/shard_map/ppermute | solution.py:316
